TPU v7x, 32 devices: a whole 2x2x4 slice. The times are simulated.
32 devices in a mesh: group: 2 (over y), rows: 4 (over z), sec: 2 (over x), sub: 2 (over core).
Axes of the slice: x: 2, y: 2, z: 4, core: 2. Of those that a mesh axis runs over, the one named last changes fastest.
Arguments:
- row_seeds: int32 [16384], P(('group', 'rows')), parts along dimension 0, may hold values from 0 to 65520
- labels: int32 [16384], P(('group', 'rows')), parts along dimension 0, may hold values from 0 to 1
- weights: float32 [131072], P(('group', 'sec', 'sub')), parts along dimension 0, may hold values from -5 to 5
- sketch: bfloat16 [65536, 64], P(('sec', 'sub')), may hold values from -5 to 5
Outputs:
- step: float32 [131072], P(('group', 'sec', 'sub')), parts along dimension 0
- sketched: float32 [131072, 64], P(('group', 'sec', 'sub')), parts along dimension 0
There are 2 independent parts, one for each index of `group`. A program takes and returns all parts, laid end to end along the dimension named above; an argument that names none is the same for every part. Nothing has to cross between parts.
All inputs are finite; a program needn't handle non-finite values.
Results may differ from a plain program's by a relative error of at most 0.0029.
Values may be sent and summed in bfloat16 or wider, within the bound.
No kernel may reach another device: no remote copies, remote signals or barrier semaphores. Data moves between devices by JAX's collectives and lax.ppermute only.
A program may use at most 128 MiB of HBM per device.

v0:
```python
import jax
import jax.numpy as jnp
from jax import lax
from jax.sharding import PartitionSpec as P

ROOT = 256


def table_block(seeds, first, count):
    cols = first + lax.iota(jnp.int32, count)
    part_a = cols * 30011 % 65521
    part_b = seeds * 16411 % 65521
    mixer = (part_b[:, None] + part_a[None, :]) % 65521
    folded = mixer % 46337
    mixer = folded * folded % 65521
    mixer = (mixer * 31 + part_a[None, :] + 7) % 65521
    level = mixer % 16
    return ((level.astype(jnp.float32) - 7.5) * (1.0 / (4.0 * ROOT))).astype(jnp.bfloat16)


def block_size():
    return 512


def margin_rows(seeds, first, stacked):
    count = seeds.shape[0]
    blk = block_size()
    nblk = count // blk
    nfeat = stacked.shape[0]

    def one_block(block_seeds):
        return jnp.dot(
            table_block(block_seeds, first, nfeat), stacked, preferred_element_type=jnp.float32
        )

    return lax.map(one_block, seeds.reshape(nblk, blk)).reshape(count, stacked.shape[1])


def accumulate(seeds, mixed, first, nfeat):
    count = seeds.shape[0]
    blk = block_size()
    nblk = count // blk

    def add_block(index, acc):
        block_seeds = lax.dynamic_slice_in_dim(seeds, index * blk, blk, 0)
        block_mixed = lax.dynamic_slice_in_dim(mixed, index * blk, blk, 0)
        tab = table_block(block_seeds, first, nfeat)
        return acc + lax.dot_general(
            tab, block_mixed, (((0,), (0,)), ((), ())), preferred_element_type=jnp.float32
        )

    return lax.fori_loop(0, nblk, add_block, jnp.zeros((nfeat, mixed.shape[1]), jnp.float32))


def weigh(margins, labels):
    prob = jax.nn.sigmoid(margins[:, 0])
    resid = prob - labels.astype(jnp.float32)
    curv = prob * (1.0 - prob)
    return jnp.concatenate([resid[:, None], curv[:, None] * margins[:, 1:]], axis=1).astype(
        jnp.bfloat16
    )


def products(sketch_part, sketched, grad):
    highest = lax.Precision.HIGHEST
    core = lax.dot_general(
        sketch_part.astype(jnp.float32), sketched, (((0,), (0,)), ((), ())), precision=highest
    )
    square = lax.dot_general(sketched, sketched, (((0,), (0,)), ((), ())), precision=highest)
    proj = lax.dot_general(sketched, grad, (((0,), (0,)), ((), ())), precision=highest)
    return (core, square, proj)


def finish(core, square, proj, sketched, grad, lam):
    inner = lam * core + square
    inner = 0.5 * (inner + inner.T)
    factor = jnp.linalg.cholesky(inner)
    middle = lax.linalg.triangular_solve(factor, proj[:, None], left_side=True, lower=True)
    coef = lax.linalg.triangular_solve(
        factor, middle, left_side=True, lower=True, transpose_a=True
    )[:, 0]
    return (grad - jnp.dot(sketched, coef, precision=lax.Precision.HIGHEST)) / lam


def local(row_seeds, labels, weights, sketch):
    lam = 0.05
    nfeat = weights.shape[0]
    first = lax.axis_index(("sec", "sub")) * nfeat
    stacked = jnp.concatenate([weights.astype(jnp.bfloat16)[:, None], sketch], axis=1)
    local_margins = margin_rows(row_seeds, first, stacked)
    margins = lax.psum(local_margins, ("sec", "sub"))
    mixed = weigh(margins, labels)
    partial_total = accumulate(row_seeds, mixed, first, nfeat)
    piece = lax.psum_scatter(partial_total, "rows", scatter_dimension=0, tiled=True)
    count = piece.shape[0]
    position = lax.axis_index("rows") * count
    own_weights = lax.dynamic_slice_in_dim(weights, position, count, 0)
    own_sketch = lax.dynamic_slice_in_dim(sketch, position, count, 0)
    grad = piece[:, 0] + lam * own_weights
    sketched = piece[:, 1:] + lam * own_sketch.astype(jnp.float32)
    core, square, proj = products(own_sketch, sketched, grad)
    core, square, proj = lax.psum((core, square, proj), ("rows", "sec", "sub"))
    step = finish(core, square, proj, sketched, grad, lam)
    step, sketched = (
        lax.all_gather(step, "rows", axis=0, tiled=True),
        lax.all_gather(sketched, "rows", axis=0, tiled=True),
    )
    return (step, sketched)


def solution(mesh):
    placed = (
        P(("group", "rows")),
        P(("group", "rows")),
        P(("group", "sec", "sub")),
        P(("sec", "sub"), None),
    )
    return jax.shard_map(
        local,
        mesh=mesh,
        in_specs=placed,
        out_specs=(P(("group", "sec", "sub")), P(("group", "sec", "sub"), None)),
        check_vma=False,
    )
```

profile of v0, /device:TPU:0, one launch (start us, length us, event | category | flops | bytes accessed | tf_op | source)
XLA Modules:
  0.0 1060.1 jit_solution(18047026899343946793)
XLA Ops:
  8.1 3.8 broadcast_in_dim.39
  11.9 4.7 copy.29
  17.4 5.9 pad_maximum_fusion
  23.3 415.5 %while.30 = (s32[]{:T(128)}, f32[4,512,65]{1,0,2:T(4,128)S(1)}, s32[4,512]{1,0:T(4,128)S(1)}, s32[]{:T(128)}, bf16[16384,65]{1,0:T(8,128)(2,1)}, /*index=5*/s32[]{:T(128)}, s32[]{:T(128)}) while((s32[]{:T(128)}, f32[4,512,65]{1,0,2:T(4,128)S(1)}, s32[4,512]{1,0:T(4,128)S(1)}, s32[]{:T(128)}, bf16[16384,65]{1,0:T(8,128)(2,1)}, ...), condition=%wide.region_1.2_spmd, body=%wide.region_0.1_spmd.sunk | while | flops 1459752448 | bytes 45011060 | solution.py:36
  23.4 91.7 %fusion.121 = bf16[512,16384]{1,0:T(8,128)(2,1)} fusion(s32[16384]{0:T(1024)S(1)} %add_select_fusion.18, s32[512]{0:T(512)S(1)} %add_select_fusion.19), kind=kLoop, calls=%fused_computation.18.clone.clone.clone.clone.1.clone.1 | loop fusion | flops 369098752 | bytes 16844800 | tf_op jit(solution)/shard_map/while/body/eval_jaxpr/dot_general | solution.py:32
  115.0 8.8 fusion.122
  127.3 91.7 %fusion.121 = bf16[512,16384]{1,0:T(8,128)(2,1)} fusion(s32[16384]{0:T(1024)S(1)} %add_select_fusion.18, s32[512]{0:T(512)S(1)} %add_select_fusion.19), kind=kLoop, calls=%fused_computation.18.clone.clone.clone.clone.1.clone.1 | loop fusion | flops 369098752 | bytes 16844800 | tf_op jit(solution)/shard_map/while/body/eval_jaxpr/dot_general | solution.py:32
  218.9 8.8 fusion.122
  231.1 91.7 %fusion.121 = bf16[512,16384]{1,0:T(8,128)(2,1)} fusion(s32[16384]{0:T(1024)S(1)} %add_select_fusion.18, s32[512]{0:T(512)S(1)} %add_select_fusion.19), kind=kLoop, calls=%fused_computation.18.clone.clone.clone.clone.1.clone.1 | loop fusion | flops 369098752 | bytes 16844800 | tf_op jit(solution)/shard_map/while/body/eval_jaxpr/dot_general | solution.py:32
  322.8 8.8 fusion.122
  335.0 91.7 %fusion.121 = bf16[512,16384]{1,0:T(8,128)(2,1)} fusion(s32[16384]{0:T(1024)S(1)} %add_select_fusion.18, s32[512]{0:T(512)S(1)} %add_select_fusion.19), kind=kLoop, calls=%fused_computation.18.clone.clone.clone.clone.1.clone.1 | loop fusion | flops 369098752 | bytes 16844800 | tf_op jit(solution)/shard_map/while/body/eval_jaxpr/dot_general | solution.py:32
  426.7 8.8 fusion.122
  440.0 36.3 %all-reduce.3.cloned.1.call-done = f32[2048,65]{0,1:T(8,128)} async-done(((f32[2048,65]{0,1:T(8,128)}), f32[2048,65]{0,1:T(8,128)}) %all-reduce.3.cloned.1.call-update) | async-done | bytes 532496 | tf_op jit(solution)/shard_map/psum | solution.py:91
  478.4 381.5 %while.31 = (s32[]{:T(128)}, f32[16384,65]{0,1:T(8,128)}, s32[2048]{0:T(1024)}, s32[]{:T(128)}, bf16[2048,65]{0,1:T(8,128)(2,1)S(1)}, /*index=5*/s32[]{:T(128)}, s32[]{:T(128)}, s32[]{:T(128)}, s32[]{:T(128)}) while((s32[]{:T(128)}, f32[16384,65]{0,1:T(8,128)}, s32[2048]{0:T(1024)}, s32[]{:T(128)}, bf16[2048,65]{0,1:T(8,128)(2,1)S(1)}, ...), condition=%wide.region_4.5_spmd.clone, body=%wide.region_3.4_spmd.clone.sunk | while | flops 1461882368 | bytes 8730785 | solution.py:52
  479.6 93.6 %convolution_add_fusion.2 = f32[16384,65]{0,1:T(8,128)} fusion(s32[16384]{0:T(1024)S(1)} %add_select_fusion.20, s32[512]{0:T(512)S(1)} %add_select_fusion.21, f32[16384,65]{0,1:T(8,128)} %get-tuple-element.400, pred[]{:T(512)S(6)} %compare.19, bf16[2048,65]{0,1:T(8,128)(2,1)S(1)} %get-tuple-element.412, s32[]{:T(128)S(6)} %select_n.397), kind=kOutput, calls=%fused_computation.70.clone.3 | convolution fusion | flops 1461747712 | bytes 8660997 | tf_op jit(solution)/shard_map/while/body/eval_jaxpr/dot_general | solution.py:48
  574.0 94.8 %convolution_add_fusion.2 = f32[16384,65]{0,1:T(8,128)} fusion(s32[16384]{0:T(1024)S(1)} %add_select_fusion.20, s32[512]{0:T(512)S(1)} %add_select_fusion.21, f32[16384,65]{0,1:T(8,128)} %get-tuple-element.400, pred[]{:T(512)S(6)} %compare.19, bf16[2048,65]{0,1:T(8,128)(2,1)S(1)} %get-tuple-element.412, s32[]{:T(128)S(6)} %select_n.397), kind=kOutput, calls=%fused_computation.70.clone.3 | convolution fusion | flops 1461747712 | bytes 8660997 | tf_op jit(solution)/shard_map/while/body/eval_jaxpr/dot_general | solution.py:48
  669.6 94.8 %convolution_add_fusion.2 = f32[16384,65]{0,1:T(8,128)} fusion(s32[16384]{0:T(1024)S(1)} %add_select_fusion.20, s32[512]{0:T(512)S(1)} %add_select_fusion.21, f32[16384,65]{0,1:T(8,128)} %get-tuple-element.400, pred[]{:T(512)S(6)} %compare.19, bf16[2048,65]{0,1:T(8,128)(2,1)S(1)} %get-tuple-element.412, s32[]{:T(128)S(6)} %select_n.397), kind=kOutput, calls=%fused_computation.70.clone.3 | convolution fusion | flops 1461747712 | bytes 8660997 | tf_op jit(solution)/shard_map/while/body/eval_jaxpr/dot_general | solution.py:48
  765.2 94.8 %convolution_add_fusion.2 = f32[16384,65]{0,1:T(8,128)} fusion(s32[16384]{0:T(1024)S(1)} %add_select_fusion.20, s32[512]{0:T(512)S(1)} %add_select_fusion.21, f32[16384,65]{0,1:T(8,128)} %get-tuple-element.400, pred[]{:T(512)S(6)} %compare.19, bf16[2048,65]{0,1:T(8,128)(2,1)S(1)} %get-tuple-element.412, s32[]{:T(128)S(6)} %select_n.397), kind=kOutput, calls=%fused_computation.70.clone.3 | convolution fusion | flops 1461747712 | bytes 8660997 | tf_op jit(solution)/shard_map/while/body/eval_jaxpr/dot_general | solution.py:48
  860.0 85.3 %reduce-scatter.2.cloned.1.call-done = f32[4096,65]{0,1:T(8,128)} async-done(((f32[16384,65]{0,1:T(8,128)}), f32[4096,65]{0,1:T(8,128)}) %reduce-scatter.2.cloned.1.call-update) | async-done | bytes 1064976 | tf_op jit(solution)/shard_map/reduce_scatter | solution.py:94
  956.0 64.8 %all-reduce = (f32[64,64]{0,1:T(8,128)S(1)}, f32[64,64]{0,1:T(8,128)S(1)}, f32[64]{0:T(128)S(1)}) all-reduce(f32[64,64]{0,1:T(8,128)S(1)} %fusion.91, f32[64,64]{0,1:T(8,128)S(1)} %fusion.78, f32[64]{0:T(128)S(1)} %convolution_bitcast_fusion), channel_id=1, replica_groups=mesh['group'=2,'rows'=4,'sec'=2,'sub'=2] {'rows','sec','sub'}, use_global_device_ids=true, to_apply=%region_7.8 | all-reduce | flops 8256 | bytes 66048 | tf_op jit(solution)/shard_map/psum | solution.py:102
  1021.0 5.8 cholesky.16
  1028.2 4.9 custom-call.8
  1035.3 13.1 %all_gather.6 = f32[16384]{0:T(1024)S(1)} all-gather(f32[4096]{0:T(1024)S(1)} %subtract_multiply_fusion), channel_id=1, replica_groups=mesh['group'=2,'rows'=4,'sec'=2,'sub'=2] {'rows'}, dimensions={0}, use_global_device_ids=true | all-gather | bytes 81920 | tf_op jit(solution)/shard_map/all_gather | solution.py:105
  1049.1 4.5 copy.62
  (77 shorter events, 36.7 us)
Async XLA Ops:
  7.2 469.1 %all-reduce.3.cloned.1.call-start = ((), (), s32[]{:S(2)}) async-start(), calls=%async_computation.1 | async-start | bytes 1179648 | tf_op jit(solution)/shard_map/psum | solution.py:91
  23.3 453.9 %copy-start.2 = (s32[2048]{0:T(1024)S(1)}, s32[2048]{0:T(1024)}, u32[]{:S(2)}) copy-start(s32[2048]{0:T(1024)} %param.9) | copy-start | bytes 24580
  23.3 91.7 %copy-start = (bf16[16384,65]{1,0:T(8,128)(2,1)S(1)}, bf16[16384,65]{1,0:T(8,128)(2,1)}, u32[]{:S(2)}) copy-start(bf16[16384,65]{1,0:T(8,128)(2,1)} %get-tuple-element.387) | copy-start | bytes 6389764 | tf_op jit(solution)/shard_map/while
  127.2 91.8 %copy-start = (bf16[16384,65]{1,0:T(8,128)(2,1)S(1)}, bf16[16384,65]{1,0:T(8,128)(2,1)}, u32[]{:S(2)}) copy-start(bf16[16384,65]{1,0:T(8,128)(2,1)} %get-tuple-element.387) | copy-start | bytes 6389764 | tf_op jit(solution)/shard_map/while
  231.0 91.8 %copy-start = (bf16[16384,65]{1,0:T(8,128)(2,1)S(1)}, bf16[16384,65]{1,0:T(8,128)(2,1)}, u32[]{:S(2)}) copy-start(bf16[16384,65]{1,0:T(8,128)(2,1)} %get-tuple-element.387) | copy-start | bytes 6389764 | tf_op jit(solution)/shard_map/while
  334.9 91.8 %copy-start = (bf16[16384,65]{1,0:T(8,128)(2,1)S(1)}, bf16[16384,65]{1,0:T(8,128)(2,1)}, u32[]{:S(2)}) copy-start(bf16[16384,65]{1,0:T(8,128)(2,1)} %get-tuple-element.387) | copy-start | bytes 6389764 | tf_op jit(solution)/shard_map/while
  440.0 505.4 %reduce-scatter.2.cloned.1.call-start = ((), (), s32[]{:S(2)}) async-start(), calls=%async_computation.2 | async-start | bytes 5898240 | tf_op jit(solution)/shard_map/reduce_scatter | solution.py:94
  478.4 466.9 %copy-start.1 = (bf16[16384,64]{0,1:T(8,128)(2,1)S(1)}, bf16[16384,64]{0,1:T(8,128)(2,1)}, u32[]{:S(2)}) copy-start(bf16[16384,64]{0,1:T(8,128)(2,1)} %param.11) | copy-start | bytes 6291460
  860.0 188.5 %all-gather.2.cloned.1.call-start = ((), (), s32[]{:S(2)}) async-start(), calls=%async_computation.3 | async-start | bytes 5242880 | tf_op jit(solution)/shard_map/all_gather | solution.py:106
Sparse Core Ops, SparseCore 0:
  440.1 36.1 all-reduce.2
  860.1 85.2 reduce-scatter.1
  947.9 82.4 all-gather.1
where the time goes:
time: 1060 us
  matrix products  422 us (40%)
  other arithmetic  394 us (37%)
  waiting for transfers between devices  122 us (12%)
  blocking collectives  77.9 us (7%)
  local copies, waits for them, and re-layouts  29.7 us (3%)
  between operations  13.9 us (1%)
    dot_general x4, matrix products, add_block(): lax.dot_general(tab, block_mixed, (((0,), (0,)), ((), ())), preferred_ele...  378 us
    dot_general x4, other arithmetic, one_block(): jnp.dot(table_block(block_seeds, first, nfeat), stacked, preferred_elemen...  367 us
    reduce_scatter x1, waiting for transfers between devices, local(): lax.psum_scatter(partial_total, 'rows', scatter_dimension=0, tiled=True)  85.3 us
    psum x1, blocking collectives, local(): core, square, proj = lax.psum((core, square, proj), ('rows', 'sec', 'sub'))  64.8 us
    psum x1, waiting for transfers between devices, local(): margins = lax.psum(local_margins, ('sec', 'sub'))  36.3 us
    dot_general x4, matrix products, one_block(): jnp.dot(table_block(block_seeds, first, nfeat), stacked, preferred_elemen...  35.3 us
  transfers between devices with their start and end apart: 3, of which 2 were waited for; matrix products, arithmetic and copies ran while one was open for 2% of the time, Pallas kernels for 0%

commit v1 on v0

v1 whole, which is shorter than its diff:
```python
import functools

import jax
import jax.numpy as jnp
from jax import lax
from jax.experimental import pallas as pl
from jax.experimental.pallas import tpu as pltpu
from jax.sharding import PartitionSpec as P

PRIME = 65521
FOLD = 46337
STEP_A = 30011
STEP_B = 16411
SHIFT = STEP_B * pow(STEP_A, -1, PRIME) % PRIME
LAM = 0.05
SCALE = 1.0 / 1024.0
LANES = 128


def window_table(length):
    rows = -(-length // (8 * LANES)) * 8
    n = lax.broadcasted_iota(jnp.int32, (rows, LANES), 0) * LANES + lax.broadcasted_iota(
        jnp.int32, (rows, LANES), 1
    )
    mixer = n % PRIME * STEP_A % PRIME
    folded = mixer % FOLD
    entry = (folded * folded % PRIME * 31 + 7) % PRIME
    return entry.astype(jnp.float32) - (PRIME - 0.5)


def window_starts(seeds, first):
    high = seeds * (SHIFT // 256) % PRIME
    return (high * 256 + seeds * (SHIFT % 256) + first) % PRIME


def table_body(start_ref, tab_ref, a_ref, feat_ref, data_ref, marg_ref, scr, *, unroll, pitch):
    nrow, nfeat = data_ref.shape
    nsub = nfeat // LANES
    high = min(8, nsub)
    lane = lax.broadcasted_iota(jnp.int32, (high, LANES), 1)
    base = pl.program_id(0) * nrow
    part = a_ref[...]

    def samples(group, carry):
        for u in range(unroll):
            row = group * unroll + u
            start = start_ref[base + row]
            top = start >> 7
            off = start & (LANES - 1)
            early = lane < off
            one = tab_ref[pl.ds(top, nsub), :]
            two = tab_ref[pl.ds(top + 1, nsub), :]
            for v in range(0, nsub, high):
                win = jnp.where(early, two[v : v + high], one[v : v + high])
                win = pltpu.roll(win, LANES - off, 1)
                level = (win + part[v : v + high]).astype(jnp.int32) & 15
                scr[pl.ds(row + v * pitch, high, stride=pitch), :] = level.astype(jnp.float32)
        return carry

    lax.fori_loop(0, nrow // unroll, samples, 0)
    for r in range(nsub):
        data_ref[:, r * LANES : (r + 1) * LANES] = scr[pl.ds(r * pitch, nrow), :].astype(jnp.bfloat16)
    marg_ref[...] = lax.dot_general(
        feat_ref[...], data_ref[...], (((1,), (1,)), ((), ())), preferred_element_type=jnp.float32
    )


def make_table(starts, tab, part, feats):
    count = starts.shape[0]
    nsub = part.shape[0]
    nfeat = nsub * LANES
    ncol = feats.shape[0]
    nrow = min(256, count)
    pitch = nrow + 8
    return pl.pallas_call(
        functools.partial(table_body, unroll=64, pitch=pitch),
        grid_spec=pltpu.PrefetchScalarGridSpec(
            num_scalar_prefetch=1,
            grid=(count // nrow,),
            in_specs=[
                pl.BlockSpec(tab.shape, lambda i, s: (0, 0)),
                pl.BlockSpec(part.shape, lambda i, s: (0, 0)),
                pl.BlockSpec((ncol, nfeat), lambda i, s: (0, 0)),
            ],
            out_specs=[
                pl.BlockSpec((nrow, nfeat), lambda i, s: (i, 0)),
                pl.BlockSpec((ncol, nrow), lambda i, s: (0, i)),
            ],
            scratch_shapes=[pltpu.VMEM((nsub * pitch, LANES), jnp.float32)],
        ),
        out_shape=[
            jax.ShapeDtypeStruct((count, nfeat), jnp.bfloat16),
            jax.ShapeDtypeStruct((ncol, count), jnp.float32),
        ],
        compiler_params=pltpu.CompilerParams(vmem_limit_bytes=48 << 20),
        cost_estimate=pl.CostEstimate(
            flops=count * nfeat * 1500, bytes_accessed=count * nfeat * 2, transcendentals=0
        ),
        name="make_table",
    )(starts, tab, part, feats)


def back_body(mix_ref, data_ref, old_ref, out_ref):
    @pl.when(pl.program_id(1) == 0)
    def _():
        out_ref[...] = old_ref[...]

    out_ref[...] += jnp.dot(mix_ref[...], data_ref[...], preferred_element_type=jnp.float32)


def back(mixed, data, total):
    ncol, count = mixed.shape
    nfeat = data.shape[1]
    kb = min(1024, count)
    fb = min(4096, nfeat)
    return pl.pallas_call(
        back_body,
        grid=(nfeat // fb, count // kb),
        in_specs=[
            pl.BlockSpec((ncol, kb), lambda f, k: (0, k)),
            pl.BlockSpec((kb, fb), lambda f, k: (k, f)),
            pl.BlockSpec((ncol, fb), lambda f, k: (0, f)),
        ],
        out_specs=pl.BlockSpec((ncol, fb), lambda f, k: (0, f)),
        out_shape=jax.ShapeDtypeStruct((ncol, nfeat), jnp.float32),
        compiler_params=pltpu.CompilerParams(vmem_limit_bytes=48 << 20),
        cost_estimate=pl.CostEstimate(
            flops=2 * count * nfeat * ncol, bytes_accessed=count * nfeat * 2, transcendentals=0
        ),
        name="back",
    )(mixed, data, total)


def shift(x, axis, size, by):
    return lax.ppermute(x, axis, [(i, (i + by) % size) for i in range(size)])


def scatter_sum(x, axis, size):
    if size <= 4:
        total = x[:, 0]
        for d in range(1, size):
            total = total + shift(x[:, d], axis, size, d)
        return total

    def hop(i, acc):
        return shift(acc, axis, size, 1) + lax.dynamic_index_in_dim(x, size - 2 - i, 1, False)

    return lax.fori_loop(0, size - 1, hop, x[:, size - 1])


def collect(x, axis, size, at):
    if size <= 4:
        return jnp.stack([x] + [shift(x, axis, size, -d) for d in range(1, size)], axis=at)

    def hop(cur, _):
        cur = shift(cur, axis, size, -1)
        return cur, cur

    _, rest = lax.scan(hop, x, None, length=size - 1)
    return jnp.moveaxis(jnp.concatenate([x[None], rest], axis=0), 0, at)


def all_sum(x, axis, size):
    if size & (size - 1) == 0 and size <= 4:
        step = 1
        while step < size:
            x = x + lax.ppermute(x, axis, [(i, i ^ step) for i in range(size)])
            step *= 2
        return x
    return lax.psum(x, axis)


def roll_to(x, dim, size, index):
    return lax.dynamic_slice_in_dim(jnp.concatenate([x, x], axis=dim), index, size, dim)


def weigh(margins, labels):
    prob = jax.nn.sigmoid(margins[64:])
    resid = prob - labels.astype(jnp.float32)
    return jnp.concatenate([prob * (1.0 - prob) * margins[:64], resid], axis=0).astype(jnp.bfloat16)


def local(sizes, row_seeds, labels, weights, sketch):
    nrows, nsec, nsub = sizes
    count = row_seeds.shape[0]
    rank = sketch.shape[1]
    nfeat = weights.shape[0] // nrows
    z, s, u = lax.axis_index("rows"), lax.axis_index("sec"), lax.axis_index("sub")
    own = z * nfeat
    first = (s * nsub + u) * weights.shape[0] + own

    nchunk = 4
    piece = count // (nchunk * nsec * nsub)
    seeds = row_seeds.reshape(nchunk, nsec, nsub, piece)
    seeds = roll_to(roll_to(seeds, 1, nsec, s), 2, nsub, u)
    starts = window_starts(collect(seeds, "rows", nrows, 3).transpose(0, 2, 1, 3, 4), first)
    starts = starts.reshape(nchunk, -1)
    labels = labels.reshape(nchunk, nsec, nsub, piece)
    labels = lax.dynamic_slice(labels, (0, s, u, 0), (nchunk, 1, 1, piece)).reshape(nchunk, 1, piece)

    tab = window_table(PRIME + nfeat + LANES)
    cols = first + lax.iota(jnp.int32, nfeat)
    part = (cols * STEP_A % PRIME).astype(jnp.float32).reshape(nfeat // LANES, LANES)
    sketch_t = lax.dynamic_slice_in_dim(sketch.T, own, nfeat, 1)
    own_weights = lax.dynamic_slice_in_dim(weights, own, nfeat, 0)[None]
    feats = jnp.concatenate([sketch_t, own_weights.astype(jnp.bfloat16)], axis=0)
    ncol = rank + 1
    feat_sum = jnp.sum(feats.astype(jnp.float32), axis=1, keepdims=True) * 7.5

    datas, mixes = [], []
    for c in range(nchunk):
        data, marg = make_table(starts[c], tab, part, feats)
        marg = (marg - feat_sum) * SCALE
        marg = scatter_sum(marg.reshape(ncol, nsub, -1), "sub", nsub)
        marg = scatter_sum(marg.reshape(ncol, nsec, -1), "sec", nsec)
        marg = scatter_sum(marg.reshape(ncol, nrows, -1), "rows", nrows)
        mixed = weigh(marg, labels[c])
        mixed = collect(mixed, "rows", nrows, 1).reshape(ncol, -1)
        mixed = collect(mixed, "sec", nsec, 1).reshape(ncol, -1)
        mixed = collect(mixed, "sub", nsub, 1).reshape(ncol, -1)
        datas.append(data)
        mixes.append(mixed)

    total = jnp.zeros((ncol, nfeat), jnp.float32)
    mix_sum = 0.0
    for data, mixed in zip(datas, mixes):
        total = back(mixed, data, total)
        mix_sum = mix_sum + jnp.sum(mixed.astype(jnp.float32), axis=1, keepdims=True)
    total = (total - 7.5 * mix_sum) * SCALE

    sketch_f = sketch_t.astype(jnp.float32)
    grad = total[rank:] + LAM * own_weights
    sketched = total[:rank] + LAM * sketch_f
    left = jnp.concatenate([LAM * sketch_f + sketched, grad], axis=0)
    prods = lax.dot_general(
        left, sketched, (((1,), (1,)), ((), ())), precision=lax.Precision.HIGHEST
    )
    prods = all_sum(all_sum(all_sum(prods, "sub", nsub), "sec", nsec), "rows", nrows)
    inner = prods[:rank]
    inner = 0.5 * (inner + inner.T)
    factor = jnp.linalg.cholesky(inner)
    middle = lax.linalg.triangular_solve(factor, prods[rank:].T, left_side=True, lower=True)
    coef = lax.linalg.triangular_solve(
        factor, middle, left_side=True, lower=True, transpose_a=True
    )
    step = (grad - jnp.dot(coef.T, sketched, precision=lax.Precision.HIGHEST)) / LAM

    def spread(x):
        parts = collect(x, "rows", nrows, 0)
        parts = roll_to(parts, 0, nrows, (nrows - z) % nrows)
        return jnp.moveaxis(parts, 0, 1).reshape(x.shape[0], -1).astype(jnp.float32)

    wide = spread(sketched.astype(jnp.bfloat16))
    return (spread(step)[0], wide.T)


def solution(mesh):
    placed = (
        P(("group", "rows")),
        P(("group", "rows")),
        P(("group", "sec", "sub")),
        P(("sec", "sub"), None),
    )
    sizes = tuple(mesh.shape[name] for name in ("rows", "sec", "sub"))
    return jax.shard_map(
        functools.partial(local, sizes),
        mesh=mesh,
        in_specs=placed,
        out_specs=(P(("group", "sec", "sub")), P(("group", "sec", "sub"), None)),
        check_vma=False,
    )
```

time: 1060 us -> 280 us (0.26)
  matrix products: 422 us -> 2.19 us
  other arithmetic: 394 us -> 23.2 us
  Pallas kernels: 0 us -> 108 us
  blocking collectives: 77.9 us -> 0 us
  starting transfers between devices: 0.12 us -> 64.3 us
  waiting for transfers between devices: 122 us -> 60.8 us
  between operations: 13.9 us -> 1.84 us
    dot_general x12 -> x2, matrix products: 422 us -> 1.88 us  [the longest x1 1.16 us: local(): lax.dot_general(left, sketched, (((1,), (1,)), ((), ())), precision=lax.P...]
    dot_general x4 -> x0, other arithmetic: 367 us -> none  [one_block(): jnp.dot(table_block(block_seeds, first, nfeat), stacked, preferred_elemen...]
    pallas_call x0 -> x8, Pallas kernels: none -> 108 us  [the longest x4 78 us: make_table(): pl.pallas_call(functools.partial(table_body, unroll=64, pitch=pitch), gri...]
    reduce_scatter x1 -> x0, waiting for transfers between devices: 85.3 us -> none  [local(): lax.psum_scatter(partial_total, 'rows', scatter_dimension=0, tiled=True)]
    psum x1 -> x0, blocking collectives: 64.8 us -> none  [local(): core, square, proj = lax.psum((core, square, proj), ('rows', 'sec', 'sub'))]
    ppermute x0 -> x53, starting transfers between devices: none -> 64.3 us  [the longest x49 62.8 us: shift(): return lax.ppermute(x, axis, [(i, (i + by) % size) for i in range(size)])]
    ppermute x0 -> x53, waiting for transfers between devices: none -> 60.8 us  [the longest x49 48.4 us: shift(): return lax.ppermute(x, axis, [(i, (i + by) % size) for i in range(size)])]
    psum x1 -> x0, waiting for transfers between devices: 36.3 us -> none  [local(): margins = lax.psum(local_margins, ('sec', 'sub'))]
  transfers between devices with their start and end apart: 3 -> 53, of which waited for: 2 -> 19; matrix products, arithmetic and copies ran while one was open for 2% -> 7% of each run, Pallas kernels for 0% -> 0%
where the time goes in v1:
time: 280 us
  Pallas kernels  108 us (39%)
  starting transfers between devices  64.3 us (23%)
  waiting for transfers between devices  60.8 us (22%)
  other arithmetic  23.2 us (8%)
  local copies, waits for them, and re-layouts  19.7 us (7%)
    pallas_call x4, Pallas kernels, make_table(): pl.pallas_call(functools.partial(table_body, unroll=64, pitch=pitch), gri...  78 us
    ppermute x49, starting transfers between devices, shift(): return lax.ppermute(x, axis, [(i, (i + by) % size) for i in range(size)])  62.8 us
    ppermute x49, waiting for transfers between devices, shift(): return lax.ppermute(x, axis, [(i, (i + by) % size) for i in range(size)])  48.4 us
    pallas_call x4, Pallas kernels, back(): pl.pallas_call(back_body, grid=(nfeat // fb, count // kb), in_specs=[pl.B...  29.8 us
    ppermute x4, waiting for transfers between devices, all_sum(): x = x + lax.ppermute(x, axis, [(i, i ^ step) for i in range(size)])  12.4 us
    another operation x3, other arithmetic, local(): factor = jnp.linalg.cholesky(inner)  6.52 us
    unnamed x58, local copies, waits for them, and re-layouts  5.89 us
  transfers between devices with their start and end apart: 53, of which 19 were waited for; matrix products, arithmetic and copies ran while one was open for 7% of the time, Pallas kernels for 0%

profile of v1, /device:TPU:0, one launch (start us, length us, event | category | flops | bytes accessed | tf_op | source)
XLA Modules:
  0.0 279.8 jit_solution(640189620106224948)
XLA Ops:
  1.4 5.1 %collective-permute-start = (s32[4,2,2,128]{3,2,1,0:T(2,128)S(1)}, s32[4,2,2,128]{3,2,1,0:T(2,128)S(1)}, u32[]{:S(2)}, u32[]{:S(2)}) collective-permute-start(s32[4,2,2,128]{3,2,1,0:T(2,128)S(1)} %fusion.57), channel_id=1, source_target_pairs={{0,12},{4,0},{8,4},{12,8},{1,13},{5,1},{9,5},{13,9},{2,14},{6,2},{... | collective-permute-start | bytes 24584 | tf_op jit(solution)/shard_map/ppermute | solution.py:135
  12.1 19.5 %make_table.4 = (bf16[2048,4096]{1,0:T(8,128)(2,1)}, f32[65,2048]{1,0:T(8,128)S(1)}) custom-call(s32[2048]{0:T(1024)S(1)} %bitcast.323, f32[552,128]{1,0:T(8,128)S(1)} %fusion.19.tab_ref, f32[32,128]{1,0:T(8,128)S(1)} %fusion.53.a_ref, bf16[65,4096]{1,0:T(8,128)(2,1)S(1)} %pad_maximum_fusion.feat_ref), custom_call_target="tpu_custom_call" | custom-call | flops 12582912000 | bytes 16777216 | tf_op jit(solution)/shard_map/make_table/pallas_call | solution.py:75
  31.7 19.5 %make_table.5 = (bf16[2048,4096]{1,0:T(8,128)(2,1)}, f32[65,2048]{1,0:T(8,128)S(1)}) custom-call(s32[2048]{0:T(1024)S(1)} %bitcast.321, f32[552,128]{1,0:T(8,128)S(1)} %fusion.19.tab_ref, f32[32,128]{1,0:T(8,128)S(1)} %fusion.53.a_ref, bf16[65,4096]{1,0:T(8,128)(2,1)S(1)} %pad_maximum_fusion.feat_ref), custom_call_target="tpu_custom_call" | custom-call | flops 12582912000 | bytes 16777216 | tf_op jit(solution)/shard_map/make_table/pallas_call | solution.py:75
  51.1 19.5 %make_table.6 = (bf16[2048,4096]{1,0:T(8,128)(2,1)}, f32[65,2048]{1,0:T(8,128)S(1)}) custom-call(s32[2048]{0:T(1024)S(1)} %bitcast.324, f32[552,128]{1,0:T(8,128)S(1)} %fusion.19.tab_ref, f32[32,128]{1,0:T(8,128)S(1)} %fusion.53.a_ref, bf16[65,4096]{1,0:T(8,128)(2,1)S(1)} %pad_maximum_fusion.feat_ref), custom_call_target="tpu_custom_call" | custom-call | flops 12582912000 | bytes 16777216 | tf_op jit(solution)/shard_map/make_table/pallas_call | solution.py:75
  70.7 19.5 %make_table.7 = (bf16[2048,4096]{1,0:T(8,128)(2,1)}, f32[65,2048]{1,0:T(8,128)S(1)}) custom-call(s32[2048]{0:T(1024)S(1)} %bitcast.322, f32[552,128]{1,0:T(8,128)S(1)} %fusion.19.tab_ref, f32[32,128]{1,0:T(8,128)S(1)} %fusion.53.a_ref, bf16[65,4096]{1,0:T(8,128)(2,1)S(1)} %pad_maximum_fusion.feat_ref), custom_call_target="tpu_custom_call" | custom-call | flops 12582912000 | bytes 16777216 | tf_op jit(solution)/shard_map/make_table/pallas_call | solution.py:75
  117.9 3.0 %collective-permute-start.7 = (f32[65,128]{1,0:T(8,128)S(1)}, f32[65,128]{1,0:T(8,128)S(1)}, u32[]{:S(2)}, u32[]{:S(2)}) collective-permute-start(f32[65,128]{1,0:T(8,128)S(1)} %bitcast.375), channel_id=1, source_target_pairs={{0,12},{4,0},{8,4},{12,8},{1,13},{5,1},{9,5},{13,9},{2,14},{6,2},{... | collective-permute-start | bytes 99848 | tf_op jit(solution)/shard_map/ppermute | solution.py:135
  121.8 3.1 %collective-permute-start.17 = (f32[65,128]{1,0:T(8,128)S(1)}, f32[65,128]{1,0:T(8,128)S(1)}, u32[]{:S(2)}, u32[]{:S(2)}) collective-permute-start(f32[65,128]{1,0:T(8,128)S(1)} %bitcast.372), channel_id=1, source_target_pairs={{0,12},{4,0},{8,4},{12,8},{1,13},{5,1},{9,5},{13,9},{2,14},{6,2},{... | collective-permute-start | bytes 99848 | tf_op jit(solution)/shard_map/ppermute | solution.py:135
  127.0 2.9 %collective-permute-start.37 = (f32[65,128]{1,0:T(8,128)S(1)}, f32[65,128]{1,0:T(8,128)S(1)}, u32[]{:S(2)}, u32[]{:S(2)}) collective-permute-start(f32[65,128]{1,0:T(8,128)S(1)} %bitcast.364), channel_id=1, source_target_pairs={{0,12},{4,0},{8,4},{12,8},{1,13},{5,1},{9,5},{13,9},{2,14},{6,2},{... | collective-permute-start | bytes 99848 | tf_op jit(solution)/shard_map/ppermute | solution.py:135
  132.3 4.2 %collective-permute-start.28 = (bf16[65,128]{1,0:T(8,128)(2,1)S(1)}, bf16[65,128]{1,0:T(8,128)(2,1)S(1)}, u32[]{:S(2)}, u32[]{:S(2)}) collective-permute-start(bf16[65,128]{1,0:T(8,128)(2,1)S(1)} %pad_maximum_fusion.15), channel_id=1, source_target_pairs={{0,12},{4,0},{8,4},{12,8},{1,13},{5,1},{9,5},{13,9},{2,14},{6,2},{... | collective-permute-start | bytes 49928 | tf_op jit(solution)/shard_map/ppermute | solution.py:135
  137.2 3.2 %collective-permute-start.38 = (bf16[65,128]{1,0:T(8,128)(2,1)S(1)}, bf16[65,128]{1,0:T(8,128)(2,1)S(1)}, u32[]{:S(2)}, u32[]{:S(2)}) collective-permute-start(bf16[65,128]{1,0:T(8,128)(2,1)S(1)} %pad_maximum_fusion.16), channel_id=1, source_target_pairs={{0,12},{4,0},{8,4},{12,8},{1,13},{5,1},{9,5},{13,9},{2,14},{6,2},{... | collective-permute-start | bytes 49928 | tf_op jit(solution)/shard_map/ppermute | solution.py:135
  141.7 3.8 %collective-permute-start.18 = (bf16[65,128]{1,0:T(8,128)(2,1)S(1)}, bf16[65,128]{1,0:T(8,128)(2,1)S(1)}, u32[]{:S(2)}, u32[]{:S(2)}) collective-permute-start(bf16[65,128]{1,0:T(8,128)(2,1)S(1)} %pad_maximum_fusion.14), channel_id=1, source_target_pairs={{0,12},{4,0},{8,4},{12,8},{1,13},{5,1},{9,5},{13,9},{2,14},{6,2},{... | collective-permute-start | bytes 49928 | tf_op jit(solution)/shard_map/ppermute | solution.py:135
  146.2 3.2 %collective-permute-start.8 = (bf16[65,128]{1,0:T(8,128)(2,1)S(1)}, bf16[65,128]{1,0:T(8,128)(2,1)S(1)}, u32[]{:S(2)}, u32[]{:S(2)}) collective-permute-start(bf16[65,128]{1,0:T(8,128)(2,1)S(1)} %pad_maximum_fusion.13), channel_id=1, source_target_pairs={{0,12},{4,0},{8,4},{12,8},{1,13},{5,1},{9,5},{13,9},{2,14},{6,2},{... | collective-permute-start | bytes 49928 | tf_op jit(solution)/shard_map/ppermute | solution.py:135
  168.2 7.6 %back.4.old_ref = f32[65,4096]{1,0:T(8,128)S(1)} custom-call(bf16[65,2048]{1,0:T(8,128)(2,1)S(1)} %bitcast.317, bf16[2048,4096]{1,0:T(8,128)(2,1)} %get-tuple-element.17.data_ref, f32[65,4096]{1,0:T(8,128)S(1)} %broadcast_in_dim.3.old_ref), custom_call_target="tpu_custom_call" | custom-call | flops 1090519040 | bytes 16777216 | tf_op jit(solution)/shard_map/back/pallas_call | solution.py:116
  175.8 7.4 %back.5.old_ref = f32[65,4096]{1,0:T(8,128)S(1)} custom-call(bf16[65,2048]{1,0:T(8,128)(2,1)S(1)} %bitcast.318, bf16[2048,4096]{1,0:T(8,128)(2,1)} %get-tuple-element.15.data_ref, f32[65,4096]{1,0:T(8,128)S(1)} %back.4.old_ref), custom_call_target="tpu_custom_call" | custom-call | flops 1090519040 | bytes 16777216 | tf_op jit(solution)/shard_map/back/pallas_call | solution.py:116
  183.2 7.4 %back.6.old_ref = f32[65,4096]{1,0:T(8,128)S(1)} custom-call(bf16[65,2048]{1,0:T(8,128)(2,1)S(1)} %bitcast.319, bf16[2048,4096]{1,0:T(8,128)(2,1)} %get-tuple-element.13.data_ref, f32[65,4096]{1,0:T(8,128)S(1)} %back.5.old_ref), custom_call_target="tpu_custom_call" | custom-call | flops 1090519040 | bytes 16777216 | tf_op jit(solution)/shard_map/back/pallas_call | solution.py:116
  190.6 7.4 %back.7 = f32[65,4096]{1,0:T(8,128)S(1)} custom-call(bf16[65,2048]{1,0:T(8,128)(2,1)S(1)} %bitcast.320, bf16[2048,4096]{1,0:T(8,128)(2,1)} %get-tuple-element.11.data_ref, f32[65,4096]{1,0:T(8,128)S(1)} %back.6.old_ref), custom_call_target="tpu_custom_call" | custom-call | flops 1090519040 | bytes 16777216 | tf_op jit(solution)/shard_map/back/pallas_call | solution.py:116
  203.1 2.6 collective-permute-done.44
  205.8 3.9 %collective-permute-done.45 = f32[65,64]{0,1:T(8,128)S(1)} collective-permute-done((f32[65,64]{0,1:T(8,128)S(1)}, f32[65,64]{0,1:T(8,128)S(1)}, u32[]{:S(2)}, u32[]{:S(2)}) %collective-permute-start.45) | collective-permute-done | bytes 16672 | tf_op jit(solution)/shard_map/ppermute | solution.py:167
  209.7 4.8 %collective-permute-done.46 = f32[65,64]{0,1:T(8,128)S(1)} collective-permute-done((f32[65,64]{0,1:T(8,128)S(1)}, f32[65,64]{0,1:T(8,128)S(1)}, u32[]{:S(2)}, u32[]{:S(2)}) %collective-permute-start.46) | collective-permute-done | bytes 16672 | tf_op jit(solution)/shard_map/ppermute | solution.py:167
  214.9 5.8 %cholesky.16 = f32[64,64]{1,0:T(8,128)S(1)} custom-call(f32[64,64]{1,0:T(8,128)S(1)} %fusion.51), custom_call_target="Cholesky" | custom-call | tf_op jit(solution)/shard_map/jit(cholesky)/cholesky | solution.py:241
  222.0 4.9 %custom-call.8 = f32[1,64,64]{1,2,0:T(8,128)S(1)} custom-call(f32[1,64,64]{2,1,0:T(8,128)S(1)} %fusion.42), custom_call_target="InvertDiagBlocksLowerTriangular" | custom-call | tf_op jit(solution)/shard_map/triangular_solve | solution.py:243
  234.3 2.8 %collective-permute-start.49 = (f32[1,4096]{1,0:T(1,128)S(1)}, f32[1,4096]{1,0:T(1,128)S(1)}, u32[]{:S(2)}, u32[]{:S(2)}) collective-permute-start(f32[1,4096]{1,0:T(1,128)S(1)} %get-tuple-element.73), channel_id=1, source_target_pairs={{0,4},{4,8},{8,12},{12,0},{1,5},{5,9},{9,13},{13,1},{2,6},{6,10},{... | collective-permute-start | bytes 49160 | tf_op jit(solution)/shard_map/ppermute | solution.py:135
  237.1 38.8 %collective-permute-done.48 = f32[1,4096]{1,0:T(1,128)S(1)} collective-permute-done((f32[1,4096]{1,0:T(1,128)S(1)}, f32[1,4096]{1,0:T(1,128)S(1)}, u32[]{:S(2)}, u32[]{:S(2)}) %collective-permute-start.48) | collective-permute-done | bytes 16416 | tf_op jit(solution)/shard_map/ppermute | solution.py:135
  277.5 2.3 copy.157
  (286 shorter events, 75.7 us)
Async XLA Ops:
  1.4 9.8 %collective-permute-start = (s32[4,2,2,128]{3,2,1,0:T(2,128)S(1)}, s32[4,2,2,128]{3,2,1,0:T(2,128)S(1)}, u32[]{:S(2)}, u32[]{:S(2)}) collective-permute-start(s32[4,2,2,128]{3,2,1,0:T(2,128)S(1)} %fusion.57), channel_id=1, source_target_pairs={{0,12},{4,0},{8,4},{12,8},{1,13},{5,1},{9,5},{13,9},{2,14},{6,2},{... | collective-permute-start | bytes 24584 | tf_op jit(solution)/shard_map/ppermute | solution.py:135
  94.5 7.9 %collective-permute-start.3 = (f32[65,1024]{1,0:T(8,128)}, f32[65,1024]{1,0:T(8,128)}, u32[]{:S(2)}, u32[]{:S(2)}) collective-permute-start(f32[65,1024]{1,0:T(8,128)} %bitcast.299), channel_id=1, source_target_pairs={{0,1},{1,0},{2,3},{3,2},{4,5},{5,4},{6,7},{7,6},{8,9},{9,8},{10,11... | collective-permute-start | bytes 798728 | tf_op jit(solution)/shard_map/ppermute | solution.py:135
  96.7 7.9 %collective-permute-start.13 = (f32[65,1024]{1,0:T(8,128)}, f32[65,1024]{1,0:T(8,128)}, u32[]{:S(2)}, u32[]{:S(2)}) collective-permute-start(f32[65,1024]{1,0:T(8,128)} %bitcast.298), channel_id=1, source_target_pairs={{0,1},{1,0},{2,3},{3,2},{4,5},{5,4},{6,7},{7,6},{8,9},{9,8},{10,11... | collective-permute-start | bytes 798728 | tf_op jit(solution)/shard_map/ppermute | solution.py:135
  98.3 9.3 %collective-permute-start.33 = (f32[65,1024]{1,0:T(8,128)}, f32[65,1024]{1,0:T(8,128)S(1)}, u32[]{:S(2)}, u32[]{:S(2)}) collective-permute-start(f32[65,1024]{1,0:T(8,128)} %bitcast.296), channel_id=1, source_target_pairs={{0,1},{1,0},{2,3},{3,2},{4,5},{5,4},{6,7},{7,6},{8,9},{9,8},{10,11... | collective-permute-start | bytes 798728 | tf_op jit(solution)/shard_map/ppermute | solution.py:135
  106.0 7.9 %collective-permute-start.14 = (f32[65,512]{1,0:T(8,128)S(1)}, f32[65,512]{1,0:T(8,128)S(1)}, u32[]{:S(2)}, u32[]{:S(2)}) collective-permute-start(f32[65,512]{1,0:T(8,128)S(1)} %bitcast.347), channel_id=1, source_target_pairs={{0,2},{2,0},{1,3},{3,1},{4,6},{6,4},{5,7},{7,5},{8,10},{10,8},{9,1... | collective-permute-start | bytes 399368 | tf_op jit(solution)/shard_map/ppermute | solution.py:135
  108.1 8.3 %collective-permute-start.34 = (f32[65,512]{1,0:T(8,128)S(1)}, f32[65,512]{1,0:T(8,128)S(1)}, u32[]{:S(2)}, u32[]{:S(2)}) collective-permute-start(f32[65,512]{1,0:T(8,128)S(1)} %bitcast.348), channel_id=1, source_target_pairs={{0,2},{2,0},{1,3},{3,1},{4,6},{6,4},{5,7},{7,5},{8,10},{10,8},{9,1... | collective-permute-start | bytes 399368 | tf_op jit(solution)/shard_map/ppermute | solution.py:135
  108.9 9.0 %collective-permute-start.25 = (f32[65,128]{1,0:T(8,128)S(1)}, f32[65,128]{1,0:T(8,128)S(1)}, u32[]{:S(2)}, u32[]{:S(2)}) collective-permute-start(f32[65,128]{1,0:T(8,128)S(1)} %bitcast.371), channel_id=1, source_target_pairs={{0,4},{4,8},{8,12},{12,0},{1,5},{5,9},{9,13},{13,1},{2,6},{6,10},{... | collective-permute-start | bytes 99848 | tf_op jit(solution)/shard_map/ppermute | solution.py:135
  110.8 10.1 %collective-permute-start.26 = (f32[65,128]{1,0:T(8,128)S(1)}, f32[65,128]{1,0:T(8,128)S(1)}, u32[]{:S(2)}, u32[]{:S(2)}) collective-permute-start(f32[65,128]{1,0:T(8,128)S(1)} %bitcast.370), channel_id=1, source_target_pairs={{0,8},{4,12},{8,0},{12,4},{1,9},{5,13},{9,1},{13,5},{2,10},{6,14},... | collective-permute-start | bytes 99848 | tf_op jit(solution)/shard_map/ppermute | solution.py:135
  111.7 9.2 %collective-permute-start.27 = (f32[65,128]{1,0:T(8,128)S(1)}, f32[65,128]{1,0:T(8,128)S(1)}, u32[]{:S(2)}, u32[]{:S(2)}) collective-permute-start(f32[65,128]{1,0:T(8,128)S(1)} %bitcast.368), channel_id=1, source_target_pairs={{0,12},{4,0},{8,4},{12,8},{1,13},{5,1},{9,5},{13,9},{2,14},{6,2},{... | collective-permute-start | bytes 99848 | tf_op jit(solution)/shard_map/ppermute | solution.py:135
  113.9 7.8 %collective-permute-start.5 = (f32[65,128]{1,0:T(8,128)S(1)}, f32[65,128]{1,0:T(8,128)S(1)}, u32[]{:S(2)}, u32[]{:S(2)}) collective-permute-start(f32[65,128]{1,0:T(8,128)S(1)} %bitcast.369), channel_id=1, source_target_pairs={{0,4},{4,8},{8,12},{12,0},{1,5},{5,9},{9,13},{13,1},{2,6},{6,10},{... | collective-permute-start | bytes 99848 | tf_op jit(solution)/shard_map/ppermute | solution.py:135
  116.4 8.5 %collective-permute-start.6 = (f32[65,128]{1,0:T(8,128)S(1)}, f32[65,128]{1,0:T(8,128)S(1)}, u32[]{:S(2)}, u32[]{:S(2)}) collective-permute-start(f32[65,128]{1,0:T(8,128)S(1)} %bitcast.366), channel_id=1, source_target_pairs={{0,8},{4,12},{8,0},{12,4},{1,9},{5,13},{9,1},{13,5},{2,10},{6,14},... | collective-permute-start | bytes 99848 | tf_op jit(solution)/shard_map/ppermute | solution.py:135
  120.9 9.0 %collective-permute-start.16 = (f32[65,128]{1,0:T(8,128)S(1)}, f32[65,128]{1,0:T(8,128)S(1)}, u32[]{:S(2)}, u32[]{:S(2)}) collective-permute-start(f32[65,128]{1,0:T(8,128)S(1)} %bitcast.373), channel_id=1, source_target_pairs={{0,8},{4,12},{8,0},{12,4},{1,9},{5,13},{9,1},{13,5},{2,10},{6,14},... | collective-permute-start | bytes 99848 | tf_op jit(solution)/shard_map/ppermute | solution.py:135
  121.8 8.1 %collective-permute-start.17 = (f32[65,128]{1,0:T(8,128)S(1)}, f32[65,128]{1,0:T(8,128)S(1)}, u32[]{:S(2)}, u32[]{:S(2)}) collective-permute-start(f32[65,128]{1,0:T(8,128)S(1)} %bitcast.372), channel_id=1, source_target_pairs={{0,12},{4,0},{8,4},{12,8},{1,13},{5,1},{9,5},{13,9},{2,14},{6,2},{... | collective-permute-start | bytes 99848 | tf_op jit(solution)/shard_map/ppermute | solution.py:135
  132.3 9.3 %collective-permute-start.28 = (bf16[65,128]{1,0:T(8,128)(2,1)S(1)}, bf16[65,128]{1,0:T(8,128)(2,1)S(1)}, u32[]{:S(2)}, u32[]{:S(2)}) collective-permute-start(bf16[65,128]{1,0:T(8,128)(2,1)S(1)} %pad_maximum_fusion.15), channel_id=1, source_target_pairs={{0,12},{4,0},{8,4},{12,8},{1,13},{5,1},{9,5},{13,9},{2,14},{6,2},{... | collective-permute-start | bytes 49928 | tf_op jit(solution)/shard_map/ppermute | solution.py:135
  136.5 9.0 %collective-permute-start.30 = (bf16[65,128]{1,0:T(8,128)(2,1)S(1)}, bf16[65,128]{1,0:T(8,128)(2,1)S(1)}, u32[]{:S(2)}, u32[]{:S(2)}) collective-permute-start(bf16[65,128]{1,0:T(8,128)(2,1)S(1)} %pad_maximum_fusion.15), channel_id=1, source_target_pairs={{0,4},{4,8},{8,12},{12,0},{1,5},{5,9},{9,13},{13,1},{2,6},{6,10},{... | collective-permute-start | bytes 49928 | tf_op jit(solution)/shard_map/ppermute | solution.py:135
  137.2 8.3 %collective-permute-start.38 = (bf16[65,128]{1,0:T(8,128)(2,1)S(1)}, bf16[65,128]{1,0:T(8,128)(2,1)S(1)}, u32[]{:S(2)}, u32[]{:S(2)}) collective-permute-start(bf16[65,128]{1,0:T(8,128)(2,1)S(1)} %pad_maximum_fusion.16), channel_id=1, source_target_pairs={{0,12},{4,0},{8,4},{12,8},{1,13},{5,1},{9,5},{13,9},{2,14},{6,2},{... | collective-permute-start | bytes 49928 | tf_op jit(solution)/shard_map/ppermute | solution.py:135
  141.6 7.8 %collective-permute-start.40 = (bf16[65,128]{1,0:T(8,128)(2,1)S(1)}, bf16[65,128]{1,0:T(8,128)(2,1)S(1)}, u32[]{:S(2)}, u32[]{:S(2)}) collective-permute-start(bf16[65,128]{1,0:T(8,128)(2,1)S(1)} %pad_maximum_fusion.16), channel_id=1, source_target_pairs={{0,4},{4,8},{8,12},{12,0},{1,5},{5,9},{9,13},{13,1},{2,6},{6,10},{... | collective-permute-start | bytes 49928 | tf_op jit(solution)/shard_map/ppermute | solution.py:135
  141.7 8.9 %collective-permute-start.18 = (bf16[65,128]{1,0:T(8,128)(2,1)S(1)}, bf16[65,128]{1,0:T(8,128)(2,1)S(1)}, u32[]{:S(2)}, u32[]{:S(2)}) collective-permute-start(bf16[65,128]{1,0:T(8,128)(2,1)S(1)} %pad_maximum_fusion.14), channel_id=1, source_target_pairs={{0,12},{4,0},{8,4},{12,8},{1,13},{5,1},{9,5},{13,9},{2,14},{6,2},{... | collective-permute-start | bytes 49928 | tf_op jit(solution)/shard_map/ppermute | solution.py:135
  151.6 8.5 %collective-permute-start.41 = (bf16[65,512]{1,0:T(8,128)(2,1)S(1)}, bf16[65,512]{1,0:T(8,128)(2,1)S(1)}, u32[]{:S(2)}, u32[]{:S(2)}) collective-permute-start(bf16[65,512]{1,0:T(8,128)(2,1)S(1)} %bitcast.355), channel_id=1, source_target_pairs={{0,2},{2,0},{1,3},{3,1},{4,6},{6,4},{5,7},{7,5},{8,10},{10,8},{9,1... | collective-permute-start | bytes 199688 | tf_op jit(solution)/shard_map/ppermute | solution.py:135
  229.3 47.4 %collective-permute-start.50 = (bf16[64,4096]{1,0:T(8,128)(2,1)S(1)}, bf16[64,4096]{1,0:T(8,128)(2,1)S(1)}, u32[]{:S(2)}, u32[]{:S(2)}) collective-permute-start(bf16[64,4096]{1,0:T(8,128)(2,1)S(1)} %get-tuple-element.19), channel_id=1, source_target_pairs={{0,12},{4,0},{8,4},{12,8},{1,13},{5,1},{9,5},{13,9},{2,14},{6,2},{... | collective-permute-start | bytes 1572872 | tf_op jit(solution)/shard_map/ppermute | solution.py:135
  230.7 46.0 %collective-permute-start.51 = (bf16[64,4096]{1,0:T(8,128)(2,1)S(1)}, bf16[64,4096]{1,0:T(8,128)(2,1)S(1)}, u32[]{:S(2)}, u32[]{:S(2)}) collective-permute-start(bf16[64,4096]{1,0:T(8,128)(2,1)S(1)} %get-tuple-element.19), channel_id=1, source_target_pairs={{0,8},{4,12},{8,0},{12,4},{1,9},{5,13},{9,1},{13,5},{2,10},{6,14},... | collective-permute-start | bytes 1572872 | tf_op jit(solution)/shard_map/ppermute | solution.py:135
  232.7 44.1 %collective-permute-start.52 = (bf16[64,4096]{1,0:T(8,128)(2,1)S(1)}, bf16[64,4096]{1,0:T(8,128)(2,1)S(1)}, u32[]{:S(2)}, u32[]{:S(2)}) collective-permute-start(bf16[64,4096]{1,0:T(8,128)(2,1)S(1)} %get-tuple-element.19), channel_id=1, source_target_pairs={{0,4},{4,8},{8,12},{12,0},{1,5},{5,9},{9,13},{13,1},{2,6},{6,10},{... | collective-permute-start | bytes 1572872 | tf_op jit(solution)/shard_map/ppermute | solution.py:135
  232.8 43.2 %collective-permute-start.48 = (f32[1,4096]{1,0:T(1,128)S(1)}, f32[1,4096]{1,0:T(1,128)S(1)}, u32[]{:S(2)}, u32[]{:S(2)}) collective-permute-start(f32[1,4096]{1,0:T(1,128)S(1)} %get-tuple-element.73), channel_id=1, source_target_pairs={{0,8},{4,12},{8,0},{12,4},{1,9},{5,13},{9,1},{13,5},{2,10},{6,14},... | collective-permute-start | bytes 49160 | tf_op jit(solution)/shard_map/ppermute | solution.py:135
  234.3 41.7 %collective-permute-start.49 = (f32[1,4096]{1,0:T(1,128)S(1)}, f32[1,4096]{1,0:T(1,128)S(1)}, u32[]{:S(2)}, u32[]{:S(2)}) collective-permute-start(f32[1,4096]{1,0:T(1,128)S(1)} %get-tuple-element.73), channel_id=1, source_target_pairs={{0,4},{4,8},{8,12},{12,0},{1,5},{5,9},{9,13},{13,1},{2,6},{6,10},{... | collective-permute-start | bytes 49160 | tf_op jit(solution)/shard_map/ppermute | solution.py:135
  (30 other events, 145.3 us)

commit v2 on v1

--- a/solution.py
+++ b/solution.py
@@ -54,13 +54,13 @@
                 win = jnp.where(early, two[v : v + high], one[v : v + high])
                 win = pltpu.roll(win, LANES - off, 1)
                 level = (win + part[v : v + high]).astype(jnp.int32) & 15
-                scr[pl.ds(row + v * pitch, high, stride=pitch), :] = level.astype(jnp.float32)
+                scr[pl.ds(row + v * pitch, high, stride=pitch), :] = level.astype(jnp.float32) - 7.5
         return carry
 
     lax.fori_loop(0, nrow // unroll, samples, 0)
     for r in range(nsub):
         data_ref[:, r * LANES : (r + 1) * LANES] = scr[pl.ds(r * pitch, nrow), :].astype(jnp.bfloat16)
-    marg_ref[...] = lax.dot_general(
+    marg_ref[...] = SCALE * lax.dot_general(
         feat_ref[...], data_ref[...], (((1,), (1,)), ((), ())), preferred_element_type=jnp.float32
     )
 
@@ -175,9 +175,30 @@
 
 
 def weigh(margins, labels):
-    prob = jax.nn.sigmoid(margins[64:])
+    prob = jax.nn.sigmoid(margins[-1:])
     resid = prob - labels.astype(jnp.float32)
-    return jnp.concatenate([prob * (1.0 - prob) * margins[:64], resid], axis=0).astype(jnp.bfloat16)
+    return jnp.concatenate([prob * (1.0 - prob) * margins[:-1], resid], axis=0).astype(jnp.bfloat16)
+
+
+def after(x, *deps):
+    return lax.optimization_barrier((x, *deps))[0]
+
+
+def split(x, size, at):
+    width = x.shape[1] // size
+    return x[:, at * width : (at + 1) * width]
+
+
+def scatter_rows(x, size):
+    if size <= 4:
+        return split(x, size, 0), [shift(split(x, size, d), "rows", size, d) for d in range(1, size)]
+    return scatter_sum(x.reshape(x.shape[0], size, -1), "rows", size), []
+
+
+def collect_rows(x, size):
+    if size <= 4:
+        return [x] + [shift(x, "rows", size, -d) for d in range(1, size)]
+    return [collect(x, "rows", size, 1).reshape(x.shape[0], -1)]
 
 
 def local(sizes, row_seeds, labels, weights, sketch):
@@ -189,12 +210,11 @@
     own = z * nfeat
     first = (s * nsub + u) * weights.shape[0] + own
 
-    nchunk = 4
+    nchunk = 2
     piece = count // (nchunk * nsec * nsub)
     seeds = row_seeds.reshape(nchunk, nsec, nsub, piece)
     seeds = roll_to(roll_to(seeds, 1, nsec, s), 2, nsub, u)
-    starts = window_starts(collect(seeds, "rows", nrows, 3).transpose(0, 2, 1, 3, 4), first)
-    starts = starts.reshape(nchunk, -1)
+    starts = window_starts(collect(seeds, "rows", nrows, 3), first)
     labels = labels.reshape(nchunk, nsec, nsub, piece)
     labels = lax.dynamic_slice(labels, (0, s, u, 0), (nchunk, 1, 1, piece)).reshape(nchunk, 1, piece)
 
@@ -205,37 +225,89 @@
     own_weights = lax.dynamic_slice_in_dim(weights, own, nfeat, 0)[None]
     feats = jnp.concatenate([sketch_t, own_weights.astype(jnp.bfloat16)], axis=0)
     ncol = rank + 1
-    feat_sum = jnp.sum(feats.astype(jnp.float32), axis=1, keepdims=True) * 7.5
-
-    datas, mixes = [], []
+
+    order = [(c, du, ds) for c in range(nchunk) for du in reversed(range(nsub)) for ds in reversed(range(nsec))]
+    data, marg, from_sub, from_sec, mixed, stage = {}, {}, {}, {}, {}, {}
+    older, due = [], []
+
+    def advance(c, at, *deps):
+        if at == 0:
+            held, come = scatter_rows(sum(from_sec[c][1:], from_sec[c][0]), nrows)
+            stage[c] = (held, come)
+            return come or [held]
+        if at == 1:
+            held, come = stage[c]
+            held = after(weigh(sum(come, held), labels[c]), *deps)
+            stage[c] = collect_rows(held, nrows)
+            return stage[c]
+        if at == 2:
+            mixed[c, 0, 0] = after(jnp.concatenate(stage[c], axis=1), *deps)
+            for ds in range(1, nsec):
+                mixed[c, 0, ds] = shift(mixed[c, 0, 0], "sec", nsec, -ds)
+            return [mixed[c, 0, ds] for ds in range(1, nsec)]
+        if at == 3:
+            half = jnp.concatenate([mixed[c, 0, ds] for ds in range(nsec)], axis=1)
+            half = after(half, *deps)
+            for du in range(1, nsub):
+                come = shift(half, "sub", nsub, -du)
+                for ds in range(nsec):
+                    mixed[c, du, ds] = split(come, nsec, ds)
+            return [mixed[c, nsub - 1, 0]]
+        return []
+
+    running = []
+
+    def boundary(*deps):
+        out = []
+        for chunk in list(running):
+            out += advance(chunk[0], chunk[1], *deps)
+            chunk[1] += 1
+            if chunk[1] > 3:
+                running.remove(chunk)
+        return out
+
+    last = []
+    for c, du, ds in order:
+        begin = after(starts[c, ds, du].reshape(-1), *last, *older)
+        data[c, du, ds], marg[c, du, ds] = make_table(begin, tab, part, feats)
+        last = [marg[c, du, ds]]
+        older, due = due, boundary()
+        if du:
+            from_sub[c, du, ds] = shift(marg[c, du, ds], "sub", nsub, du)
+            due.append(from_sub[c, du, ds])
+        else:
+            summed = sum([from_sub[c, e, ds] for e in range(1, nsub)], marg[c, du, ds])
+            if ds:
+                from_sec.setdefault(c, []).append(shift(summed, "sec", nsec, ds))
+                due.append(from_sec[c][-1])
+            else:
+                from_sec[c].insert(0, summed)
+                running.append([c, 0])
+                if (c, du, ds) == order[-1]:
+                    due += boundary()
+
+    total = jnp.zeros((ncol, nfeat), jnp.float32)
     for c in range(nchunk):
-        data, marg = make_table(starts[c], tab, part, feats)
-        marg = (marg - feat_sum) * SCALE
-        marg = scatter_sum(marg.reshape(ncol, nsub, -1), "sub", nsub)
-        marg = scatter_sum(marg.reshape(ncol, nsec, -1), "sec", nsec)
-        marg = scatter_sum(marg.reshape(ncol, nrows, -1), "rows", nrows)
-        mixed = weigh(marg, labels[c])
-        mixed = collect(mixed, "rows", nrows, 1).reshape(ncol, -1)
-        mixed = collect(mixed, "sec", nsec, 1).reshape(ncol, -1)
-        mixed = collect(mixed, "sub", nsub, 1).reshape(ncol, -1)
-        datas.append(data)
-        mixes.append(mixed)
-
-    total = jnp.zeros((ncol, nfeat), jnp.float32)
-    mix_sum = 0.0
-    for data, mixed in zip(datas, mixes):
-        total = back(mixed, data, total)
-        mix_sum = mix_sum + jnp.sum(mixed.astype(jnp.float32), axis=1, keepdims=True)
-    total = (total - 7.5 * mix_sum) * SCALE
+        for du in range(nsub):
+            for ds in range(nsec):
+                while (c, du, ds) not in mixed:
+                    due += boundary()
+                total = back(after(mixed[c, du, ds], *older), data[c, du, ds], total)
+                older, due = due, boundary(total)
+    total = total * SCALE
 
     sketch_f = sketch_t.astype(jnp.float32)
     grad = total[rank:] + LAM * own_weights
     sketched = total[:rank] + LAM * sketch_f
+    block = sketched.astype(jnp.bfloat16)
+    wide = {d: shift(block, "rows", nrows, -d) for d in range(1, nrows)} if nrows <= 4 else None
     left = jnp.concatenate([LAM * sketch_f + sketched, grad], axis=0)
     prods = lax.dot_general(
         left, sketched, (((1,), (1,)), ((), ())), precision=lax.Precision.HIGHEST
     )
     prods = all_sum(all_sum(all_sum(prods, "sub", nsub), "sec", nsec), "rows", nrows)
+    if wide:
+        prods = after(prods, *[wide[d] for d in (1, nrows - 1)])
     inner = prods[:rank]
     inner = 0.5 * (inner + inner.T)
     factor = jnp.linalg.cholesky(inner)
@@ -245,13 +317,12 @@
     )
     step = (grad - jnp.dot(coef.T, sketched, precision=lax.Precision.HIGHEST)) / LAM
 
-    def spread(x):
-        parts = collect(x, "rows", nrows, 0)
+    def spread(x, rest=None):
+        parts = collect(x, "rows", nrows, 0) if rest is None else jnp.stack([x] + rest, axis=0)
         parts = roll_to(parts, 0, nrows, (nrows - z) % nrows)
         return jnp.moveaxis(parts, 0, 1).reshape(x.shape[0], -1).astype(jnp.float32)
 
-    wide = spread(sketched.astype(jnp.bfloat16))
-    return (spread(step)[0], wide.T)
+    return (spread(step)[0], spread(block, wide and [wide[d] for d in range(1, nrows)]).T)
 
 
 def solution(mesh):

time: 280 us -> 243 us (0.87)
  starting transfers between devices: 64.3 us -> 39.9 us
  waiting for transfers between devices: 60.8 us -> 42.5 us
  Pallas kernels: 108 us -> 125 us
  local copies, waits for them, and re-layouts: 19.7 us -> 12.9 us
  other arithmetic: 23.2 us -> 17.9 us
    ppermute x49 -> x31, waiting for transfers between devices: 48.4 us -> 9.15 us  [shift(): return lax.ppermute(x, axis, [(i, (i + by) % size) for i in range(size)])]
    ppermute x49 -> x31, starting transfers between devices: 62.8 us -> 35.9 us  [shift(): return lax.ppermute(x, axis, [(i, (i + by) % size) for i in range(size)])]
    ppermute x4, waiting for transfers between devices: 12.4 us -> 33.3 us  [all_sum(): x = x + lax.ppermute(x, axis, [(i, i ^ step) for i in range(size)])]
    pallas_call x4 -> x8, Pallas kernels: 29.8 us -> 39.8 us  [back(): pl.pallas_call(back_body, grid=(nfeat // fb, count // kb), in_specs=[pl.B...]
    pallas_call x4 -> x8, Pallas kernels: 78 us -> 85.7 us  [make_table(): pl.pallas_call(functools.partial(table_body, unroll=64, pitch=pitch), gri...]
    slice x17 -> x5, local copies, waits for them, and re-layouts: 3.58 us -> 0.1 us  [the longest x4 0.08 us: split(): return x[:, at * width:(at + 1) * width]]
    add x12 -> x6, other arithmetic: 3.29 us -> 0.24 us  [the longest x2 0.12 us: advance(): held, come = scatter_rows(sum(from_sec[c][1:], from_sec[c][0]), nrows)]
    unnamed x58 -> x16, local copies, waits for them, and re-layouts: 5.89 us -> 6.08 us
  transfers between devices with their start and end apart: 53 -> 35, of which waited for: 19 -> 9; matrix products, arithmetic and copies ran while one was open for 7% -> 12% of each run, Pallas kernels for 0% -> 39%
where the time goes in v2:
time: 243 us; the launch traced here: 242 us
  Pallas kernels  125 us (51%)
  waiting for transfers between devices  42.5 us (17%)
  starting transfers between devices  39.9 us (16%)
  other arithmetic  17.9 us (7%)
  local copies, waits for them, and re-layouts  12.9 us (5%)
    pallas_call x8, Pallas kernels, make_table(): pl.pallas_call(functools.partial(table_body, unroll=64, pitch=pitch), gri...  85.7 us
    pallas_call x8, Pallas kernels, back(): pl.pallas_call(back_body, grid=(nfeat // fb, count // kb), in_specs=[pl.B...  39.8 us
    ppermute x31, starting transfers between devices, shift(): return lax.ppermute(x, axis, [(i, (i + by) % size) for i in range(size)])  35.9 us
    ppermute x4, waiting for transfers between devices, all_sum(): x = x + lax.ppermute(x, axis, [(i, i ^ step) for i in range(size)])  33.3 us
    ppermute x31, waiting for transfers between devices, shift(): return lax.ppermute(x, axis, [(i, (i + by) % size) for i in range(size)])  9.15 us
    another operation x3, other arithmetic, local(): factor = jnp.linalg.cholesky(inner)  6.52 us
    unnamed x16, local copies, waits for them, and re-layouts  6.08 us
    another operation x2, other arithmetic, local(): lax.linalg.triangular_solve(factor, middle, left_side=True, lower=True, t...  5.55 us
  transfers between devices with their start and end apart: 35, of which 9 were waited for; matrix products, arithmetic and copies ran while one was open for 12% of the time, Pallas kernels for 39%

profile of v2, /device:TPU:0, one launch (start us, length us, event | category | flops | bytes accessed | tf_op | source)
XLA Modules:
  0.0 241.9 jit_solution(18400116455263393129)
XLA Ops:
  1.4 5.1 %collective-permute-start = (s32[2,2,2,256]{3,2,1,0:T(2,128)S(1)}, s32[2,2,2,256]{3,2,1,0:T(2,128)S(1)}, u32[]{:S(2)}, u32[]{:S(2)}) collective-permute-start(s32[2,2,2,256]{3,2,1,0:T(2,128)S(1)} %fusion.39), channel_id=1, source_target_pairs={{0,12},{4,0},{8,4},{12,8},{1,13},{5,1},{9,5},{13,9},{2,14},{6,2},{... | collective-permute-start | bytes 24584 | tf_op jit(solution)/shard_map/ppermute | solution.py:135
  12.1 10.6 %make_table.8 = (bf16[1024,4096]{1,0:T(8,128)(2,1)}, f32[65,1024]{1,0:T(8,128)S(1)}) custom-call(s32[1024]{0:T(1024)S(1)} %bitcast.100, f32[552,128]{1,0:T(8,128)S(1)} %fusion.15.tab_ref, f32[32,128]{1,0:T(8,128)S(1)} %fusion.35.a_ref, bf16[65,4096]{1,0:T(8,128)(2,1)S(1)} %pad_maximum_fusion.feat_ref), custom_call_target="tpu_custom_call" | custom-call | flops 6291456000 | bytes 8388608 | tf_op jit(solution)/shard_map/make_table/pallas_call | solution.py:75
  22.8 10.7 %make_table.9 = (bf16[1024,4096]{1,0:T(8,128)(2,1)}, f32[65,1024]{1,0:T(8,128)S(1)}) custom-call(s32[1024]{0:T(1024)S(1)} %bitcast.99, f32[552,128]{1,0:T(8,128)S(1)} %fusion.15.tab_ref, f32[32,128]{1,0:T(8,128)S(1)} %fusion.35.a_ref, bf16[65,4096]{1,0:T(8,128)(2,1)S(1)} %pad_maximum_fusion.feat_ref), custom_call_target="tpu_custom_call" | custom-call | flops 6291456000 | bytes 8388608 | tf_op jit(solution)/shard_map/make_table/pallas_call | solution.py:75
  34.0 10.7 %make_table.10 = (bf16[1024,4096]{1,0:T(8,128)(2,1)}, f32[65,1024]{1,0:T(8,128)S(1)}) custom-call(s32[1024]{0:T(1024)S(1)} %bitcast.98, f32[552,128]{1,0:T(8,128)S(1)} %fusion.15.tab_ref, f32[32,128]{1,0:T(8,128)S(1)} %fusion.35.a_ref, bf16[65,4096]{1,0:T(8,128)(2,1)S(1)} %pad_maximum_fusion.feat_ref), custom_call_target="tpu_custom_call" | custom-call | flops 6291456000 | bytes 8388608 | tf_op jit(solution)/shard_map/make_table/pallas_call | solution.py:75
  46.3 10.7 %make_table.11 = (bf16[1024,4096]{1,0:T(8,128)(2,1)}, f32[65,1024]{1,0:T(8,128)S(1)}) custom-call(s32[1024]{0:T(1024)S(1)} %bitcast.97, f32[552,128]{1,0:T(8,128)S(1)} %fusion.15.tab_ref, f32[32,128]{1,0:T(8,128)S(1)} %fusion.35.a_ref, bf16[65,4096]{1,0:T(8,128)(2,1)S(1)} %pad_maximum_fusion.feat_ref), custom_call_target="tpu_custom_call" | custom-call | flops 6291456000 | bytes 8388608 | tf_op jit(solution)/shard_map/make_table/pallas_call | solution.py:75
  61.6 4.9 %collective-permute-done.7 = f32[65,256]{1,0:T(8,128)S(1)} collective-permute-done((f32[65,256]{1,0:T(8,128)S(1)}, f32[65,256]{1,0:T(8,128)S(1)}, u32[]{:S(2)}, u32[]{:S(2)}) %collective-permute-start.7) | collective-permute-done | bytes 66592 | tf_op jit(solution)/shard_map/ppermute | solution.py:135
  71.0 10.7 %make_table.12 = (bf16[1024,4096]{1,0:T(8,128)(2,1)}, f32[65,1024]{1,0:T(8,128)S(1)}) custom-call(s32[1024]{0:T(1024)S(1)} %bitcast.96, f32[552,128]{1,0:T(8,128)S(1)} %fusion.15.tab_ref, f32[32,128]{1,0:T(8,128)S(1)} %fusion.35.a_ref, bf16[65,4096]{1,0:T(8,128)(2,1)S(1)} %pad_maximum_fusion.feat_ref), custom_call_target="tpu_custom_call" | custom-call | flops 6291456000 | bytes 8388608 | tf_op jit(solution)/shard_map/make_table/pallas_call | solution.py:75
  82.4 10.7 %make_table.13 = (bf16[1024,4096]{1,0:T(8,128)(2,1)}, f32[65,1024]{1,0:T(8,128)S(1)}) custom-call(s32[1024]{0:T(1024)S(1)} %bitcast.95, f32[552,128]{1,0:T(8,128)S(1)} %fusion.15.tab_ref, f32[32,128]{1,0:T(8,128)S(1)} %fusion.35.a_ref, bf16[65,4096]{1,0:T(8,128)(2,1)S(1)} %pad_maximum_fusion.feat_ref), custom_call_target="tpu_custom_call" | custom-call | flops 6291456000 | bytes 8388608 | tf_op jit(solution)/shard_map/make_table/pallas_call | solution.py:75
  93.7 10.7 %make_table.14 = (bf16[1024,4096]{1,0:T(8,128)(2,1)}, f32[65,1024]{1,0:T(8,128)S(1)}) custom-call(s32[1024]{0:T(1024)S(1)} %bitcast.94, f32[552,128]{1,0:T(8,128)S(1)} %fusion.15.tab_ref, f32[32,128]{1,0:T(8,128)S(1)} %fusion.35.a_ref, bf16[65,4096]{1,0:T(8,128)(2,1)S(1)} %pad_maximum_fusion.feat_ref), custom_call_target="tpu_custom_call" | custom-call | flops 6291456000 | bytes 8388608 | tf_op jit(solution)/shard_map/make_table/pallas_call | solution.py:75
  106.0 10.7 %make_table.15 = (bf16[1024,4096]{1,0:T(8,128)(2,1)}, f32[65,1024]{1,0:T(8,128)S(1)}) custom-call(s32[1024]{0:T(1024)S(1)} %bitcast.93, f32[552,128]{1,0:T(8,128)S(1)} %fusion.15.tab_ref, f32[32,128]{1,0:T(8,128)S(1)} %fusion.35.a_ref, bf16[65,4096]{1,0:T(8,128)(2,1)S(1)} %pad_maximum_fusion.feat_ref), custom_call_target="tpu_custom_call" | custom-call | flops 6291456000 | bytes 8388608 | tf_op jit(solution)/shard_map/make_table/pallas_call | solution.py:75
  120.9 5.0 %back.8.old_ref = f32[65,4096]{1,0:T(8,128)S(1)} custom-call(bf16[65,1024]{1,0:T(8,128)(2,1)S(1)} %pad_maximum_fusion.3.mix_ref, bf16[1024,4096]{1,0:T(8,128)(2,1)} %get-tuple-element.50.data_ref, f32[65,4096]{1,0:T(8,128)S(1)} %broadcast_in_dim.6.old_ref), custom_call_target="tpu_custom_call" | custom-call | flops 545259520 | bytes 8388608 | tf_op jit(solution)/shard_map/back/pallas_call | solution.py:116
  131.8 5.0 %back.9.old_ref = f32[65,4096]{1,0:T(8,128)S(1)} custom-call(bf16[65,1024]{1,0:T(8,128)(2,1)S(1)} %collective-permute-done.18.mix_ref, bf16[1024,4096]{1,0:T(8,128)(2,1)} %get-tuple-element.53.data_ref, f32[65,4096]{1,0:T(8,128)S(1)} %back.8.old_ref), custom_call_target="tpu_custom_call" | custom-call | flops 545259520 | bytes 8388608 | tf_op jit(solution)/shard_map/back/pallas_call | solution.py:116
  137.5 5.0 %back.10.old_ref = f32[65,4096]{1,0:T(8,128)S(1)} custom-call(bf16[65,1024]{1,0:T(8,128)(2,1)S(1)} %get-tuple-element.55.mix_ref, bf16[1024,4096]{1,0:T(8,128)(2,1)} %get-tuple-element.56.data_ref, f32[65,4096]{1,0:T(8,128)S(1)} %back.9.old_ref), custom_call_target="tpu_custom_call" | custom-call | flops 545259520 | bytes 8388608 | tf_op jit(solution)/shard_map/back/pallas_call | solution.py:116
  143.3 5.0 %back.11.old_ref = f32[65,4096]{1,0:T(8,128)S(1)} custom-call(bf16[65,1024]{1,0:T(8,128)(2,1)S(1)} %get-tuple-element.63.mix_ref, bf16[1024,4096]{1,0:T(8,128)(2,1)} %get-tuple-element.64.data_ref, f32[65,4096]{1,0:T(8,128)S(1)} %back.10.old_ref), custom_call_target="tpu_custom_call" | custom-call | flops 545259520 | bytes 8388608 | tf_op jit(solution)/shard_map/back/pallas_call | solution.py:116
  148.3 5.0 %back.12.old_ref = f32[65,4096]{1,0:T(8,128)S(1)} custom-call(bf16[65,1024]{1,0:T(8,128)(2,1)S(1)} %pad_maximum_fusion.4.mix_ref, bf16[1024,4096]{1,0:T(8,128)(2,1)} %get-tuple-element.62.data_ref, f32[65,4096]{1,0:T(8,128)S(1)} %back.11.old_ref), custom_call_target="tpu_custom_call" | custom-call | flops 545259520 | bytes 8388608 | tf_op jit(solution)/shard_map/back/pallas_call | solution.py:116
  153.2 5.0 %back.13.old_ref = f32[65,4096]{1,0:T(8,128)S(1)} custom-call(bf16[65,1024]{1,0:T(8,128)(2,1)S(1)} %collective-permute-done.23.mix_ref, bf16[1024,4096]{1,0:T(8,128)(2,1)} %get-tuple-element.60.data_ref, f32[65,4096]{1,0:T(8,128)S(1)} %back.12.old_ref), custom_call_target="tpu_custom_call" | custom-call | flops 545259520 | bytes 8388608 | tf_op jit(solution)/shard_map/back/pallas_call | solution.py:116
  158.2 5.0 %back.14.old_ref = f32[65,4096]{1,0:T(8,128)S(1)} custom-call(bf16[65,1024]{1,0:T(8,128)(2,1)S(1)} %get-tuple-element.74.mix_ref, bf16[1024,4096]{1,0:T(8,128)(2,1)} %get-tuple-element.59.data_ref, f32[65,4096]{1,0:T(8,128)S(1)} %back.13.old_ref), custom_call_target="tpu_custom_call" | custom-call | flops 545259520 | bytes 8388608 | tf_op jit(solution)/shard_map/back/pallas_call | solution.py:116
  163.2 5.1 %back.15 = f32[65,4096]{1,0:T(8,128)S(1)} custom-call(bf16[65,1024]{1,0:T(8,128)(2,1)S(1)} %get-tuple-element.75.mix_ref, bf16[1024,4096]{1,0:T(8,128)(2,1)} %get-tuple-element.58.data_ref, f32[65,4096]{1,0:T(8,128)S(1)} %back.14.old_ref), custom_call_target="tpu_custom_call" | custom-call | flops 545259520 | bytes 8388608 | tf_op jit(solution)/shard_map/back/pallas_call | solution.py:116
  169.7 3.8 %collective-permute-start.29 = (bf16[64,4096]{1,0:T(8,128)(2,1)}, bf16[64,4096]{1,0:T(8,128)(2,1)S(1)}, u32[]{:S(2)}, u32[]{:S(2)}) collective-permute-start(bf16[64,4096]{1,0:T(8,128)(2,1)} %get-tuple-element.67), channel_id=1, source_target_pairs={{0,12},{4,0},{8,4},{12,8},{1,13},{5,1},{9,5},{13,9},{2,14},{6,2},{... | collective-permute-start | bytes 1572872 | tf_op jit(solution)/shard_map/ppermute | solution.py:135
  179.9 16.3 %collective-permute-done.27 = f32[65,64]{0,1:T(8,128)S(1)} collective-permute-done((f32[65,64]{0,1:T(8,128)S(1)}, f32[65,64]{0,1:T(8,128)S(1)}, u32[]{:S(2)}, u32[]{:S(2)}) %collective-permute-start.27) | collective-permute-done | bytes 16672 | tf_op jit(solution)/shard_map/ppermute | solution.py:167
  199.1 13.4 %collective-permute-done.28 = f32[65,64]{0,1:T(8,128)S(1)} collective-permute-done((f32[65,64]{0,1:T(8,128)S(1)}, f32[65,64]{0,1:T(8,128)S(1)}, u32[]{:S(2)}, u32[]{:S(2)}) %collective-permute-start.28) | collective-permute-done | bytes 16672 | tf_op jit(solution)/shard_map/ppermute | solution.py:167
  212.9 5.8 %cholesky.16 = f32[64,64]{1,0:T(8,128)S(1)} custom-call(f32[64,64]{1,0:T(8,128)S(1)} %fusion.33), custom_call_target="Cholesky" | custom-call | tf_op jit(solution)/shard_map/jit(cholesky)/cholesky | solution.py:313
  220.1 4.9 %custom-call.8 = f32[1,64,64]{1,2,0:T(8,128)S(1)} custom-call(f32[1,64,64]{2,1,0:T(8,128)S(1)} %fusion.28), custom_call_target="InvertDiagBlocksLowerTriangular" | custom-call | tf_op jit(solution)/shard_map/triangular_solve | solution.py:315
  226.2 3.7 %collective-permute-start.31 = (f32[1,4096]{1,0:T(1,128)S(1)}, f32[1,4096]{1,0:T(1,128)S(1)}, u32[]{:S(2)}, u32[]{:S(2)}) collective-permute-start(f32[1,4096]{1,0:T(1,128)S(1)} %get-tuple-element.91), channel_id=1, source_target_pairs={{0,12},{4,0},{8,4},{12,8},{1,13},{5,1},{9,5},{13,9},{2,14},{6,2},{... | collective-permute-start | bytes 49160 | tf_op jit(solution)/shard_map/ppermute | solution.py:135
  (143 shorter events, 57.3 us)
Async XLA Ops:
  1.4 8.9 %collective-permute-start = (s32[2,2,2,256]{3,2,1,0:T(2,128)S(1)}, s32[2,2,2,256]{3,2,1,0:T(2,128)S(1)}, u32[]{:S(2)}, u32[]{:S(2)}) collective-permute-start(s32[2,2,2,256]{3,2,1,0:T(2,128)S(1)} %fusion.39), channel_id=1, source_target_pairs={{0,12},{4,0},{8,4},{12,8},{1,13},{5,1},{9,5},{13,9},{2,14},{6,2},{... | collective-permute-start | bytes 24584 | tf_op jit(solution)/shard_map/ppermute | solution.py:135
  22.8 11.2 %collective-permute-start.3 = (f32[65,1024]{1,0:T(8,128)S(1)}, f32[65,1024]{1,0:T(8,128)S(1)}, u32[]{:S(2)}, u32[]{:S(2)}) collective-permute-start(f32[65,1024]{1,0:T(8,128)S(1)} %get-tuple-element.34), channel_id=1, source_target_pairs={{0,1},{1,0},{2,3},{3,2},{4,5},{5,4},{6,7},{7,6},{8,9},{9,8},{10,11... | collective-permute-start | bytes 798728 | tf_op jit(solution)/shard_map/ppermute | solution.py:135
  33.5 11.2 %collective-permute-start.4 = (f32[65,1024]{1,0:T(8,128)S(1)}, f32[65,1024]{1,0:T(8,128)S(1)}, u32[]{:S(2)}, u32[]{:S(2)}) collective-permute-start(f32[65,1024]{1,0:T(8,128)S(1)} %get-tuple-element.36), channel_id=1, source_target_pairs={{0,1},{1,0},{2,3},{3,2},{4,5},{5,4},{6,7},{7,6},{8,9},{9,8},{10,11... | collective-permute-start | bytes 798728 | tf_op jit(solution)/shard_map/ppermute | solution.py:135
  44.8 12.2 %collective-permute-start.5 = (f32[65,1024]{1,0:T(8,128)S(1)}, f32[65,1024]{1,0:T(8,128)S(1)}, u32[]{:S(2)}, u32[]{:S(2)}) collective-permute-start(f32[65,1024]{1,0:T(8,128)S(1)} %add.295), channel_id=1, source_target_pairs={{0,2},{2,0},{1,3},{3,1},{4,6},{6,4},{5,7},{7,5},{8,10},{10,8},{9,1... | collective-permute-start | bytes 798728 | tf_op jit(solution)/shard_map/ppermute | solution.py:135
  66.6 15.1 %collective-permute-start.12 = (bf16[65,256]{1,0:T(8,128)(2,1)S(1)}, bf16[65,256]{1,0:T(8,128)(2,1)S(1)}, u32[]{:S(2)}, u32[]{:S(2)}) collective-permute-start(bf16[65,256]{1,0:T(8,128)(2,1)S(1)} %pad_maximum_fusion.5), channel_id=1, source_target_pairs={{0,4},{4,8},{8,12},{12,0},{1,5},{5,9},{9,13},{13,1},{2,6},{6,10},{... | collective-permute-start | bytes 99848 | tf_op jit(solution)/shard_map/ppermute | solution.py:135
  66.7 15.0 %collective-permute-start.11 = (bf16[65,256]{1,0:T(8,128)(2,1)S(1)}, bf16[65,256]{1,0:T(8,128)(2,1)S(1)}, u32[]{:S(2)}, u32[]{:S(2)}) collective-permute-start(bf16[65,256]{1,0:T(8,128)(2,1)S(1)} %pad_maximum_fusion.5), channel_id=1, source_target_pairs={{0,8},{4,12},{8,0},{12,4},{1,9},{5,13},{9,1},{13,5},{2,10},{6,14},... | collective-permute-start | bytes 99848 | tf_op jit(solution)/shard_map/ppermute | solution.py:135
  68.1 13.6 %collective-permute-start.10 = (bf16[65,256]{1,0:T(8,128)(2,1)S(1)}, bf16[65,256]{1,0:T(8,128)(2,1)S(1)}, u32[]{:S(2)}, u32[]{:S(2)}) collective-permute-start(bf16[65,256]{1,0:T(8,128)(2,1)S(1)} %pad_maximum_fusion.5), channel_id=1, source_target_pairs={{0,12},{4,0},{8,4},{12,8},{1,13},{5,1},{9,5},{13,9},{2,14},{6,2},{... | collective-permute-start | bytes 99848 | tf_op jit(solution)/shard_map/ppermute | solution.py:135
  81.7 12.0 %collective-permute-start.9 = (f32[65,1024]{1,0:T(8,128)S(1)}, f32[65,1024]{1,0:T(8,128)S(1)}, u32[]{:S(2)}, u32[]{:S(2)}) collective-permute-start(f32[65,1024]{1,0:T(8,128)S(1)} %get-tuple-element.42), channel_id=1, source_target_pairs={{0,1},{1,0},{2,3},{3,2},{4,5},{5,4},{6,7},{7,6},{8,9},{9,8},{10,11... | collective-permute-start | bytes 798728 | tf_op jit(solution)/shard_map/ppermute | solution.py:135
  81.8 11.6 %collective-permute-start.18 = (bf16[65,1024]{1,0:T(8,128)(2,1)S(1)}, bf16[65,1024]{1,0:T(8,128)(2,1)S(1)}, u32[]{:S(2)}, u32[]{:S(2)}) collective-permute-start(bf16[65,1024]{1,0:T(8,128)(2,1)S(1)} %pad_maximum_fusion.3.mix_ref), channel_id=1, source_target_pairs={{0,2},{2,0},{1,3},{3,1},{4,6},{6,4},{5,7},{7,5},{8,10},{10,8},{9,1... | collective-permute-start | bytes 399368 | tf_op jit(solution)/shard_map/ppermute | solution.py:135
  93.1 11.3 %collective-permute-start.13 = (f32[65,1024]{1,0:T(8,128)S(1)}, f32[65,1024]{1,0:T(8,128)S(1)}, u32[]{:S(2)}, u32[]{:S(2)}) collective-permute-start(f32[65,1024]{1,0:T(8,128)S(1)} %get-tuple-element.44), channel_id=1, source_target_pairs={{0,1},{1,0},{2,3},{3,2},{4,5},{5,4},{6,7},{7,6},{8,9},{9,8},{10,11... | collective-permute-start | bytes 798728 | tf_op jit(solution)/shard_map/ppermute | solution.py:135
  93.4 27.4 %collective-permute-start.22 = (bf16[65,2048]{1,0:T(8,128)(2,1)S(1)}, bf16[65,2048]{1,0:T(8,128)(2,1)S(1)}, u32[]{:S(2)}, u32[]{:S(2)}) collective-permute-start(bf16[65,2048]{1,0:T(8,128)(2,1)S(1)} %pad_maximum_fusion.1), channel_id=1, source_target_pairs={{0,1},{1,0},{2,3},{3,2},{4,5},{5,4},{6,7},{7,6},{8,9},{9,8},{10,11... | collective-permute-start | bytes 798728 | tf_op jit(solution)/shard_map/ppermute | solution.py:135
  104.5 12.3 %collective-permute-start.14 = (f32[65,1024]{1,0:T(8,128)S(1)}, f32[65,1024]{1,0:T(8,128)S(1)}, u32[]{:S(2)}, u32[]{:S(2)}) collective-permute-start(f32[65,1024]{1,0:T(8,128)S(1)} %add.305), channel_id=1, source_target_pairs={{0,2},{2,0},{1,3},{3,1},{4,6},{6,4},{5,7},{7,5},{8,10},{10,8},{9,1... | collective-permute-start | bytes 798728 | tf_op jit(solution)/shard_map/ppermute | solution.py:135
  116.9 9.0 %collective-permute-start.15 = (f32[65,256]{1,0:T(8,128)S(1)}, f32[65,256]{1,0:T(8,128)S(1)}, u32[]{:S(2)}, u32[]{:S(2)}) collective-permute-start(f32[65,256]{1,0:T(8,128)S(1)} %get-tuple-element.76), channel_id=1, source_target_pairs={{0,4},{4,8},{8,12},{12,0},{1,5},{5,9},{9,13},{13,1},{2,6},{6,10},{... | collective-permute-start | bytes 199688 | tf_op jit(solution)/shard_map/ppermute | solution.py:135
  117.0 8.8 %collective-permute-start.17 = (f32[65,256]{1,0:T(8,128)S(1)}, f32[65,256]{1,0:T(8,128)S(1)}, u32[]{:S(2)}, u32[]{:S(2)}) collective-permute-start(f32[65,256]{1,0:T(8,128)S(1)} %get-tuple-element.77), channel_id=1, source_target_pairs={{0,12},{4,0},{8,4},{12,8},{1,13},{5,1},{9,5},{13,9},{2,14},{6,2},{... | collective-permute-start | bytes 199688 | tf_op jit(solution)/shard_map/ppermute | solution.py:135
  127.1 9.7 %collective-permute-start.21 = (bf16[65,256]{1,0:T(8,128)(2,1)S(1)}, bf16[65,256]{1,0:T(8,128)(2,1)S(1)}, u32[]{:S(2)}, u32[]{:S(2)}) collective-permute-start(bf16[65,256]{1,0:T(8,128)(2,1)S(1)} %pad_maximum_fusion.6), channel_id=1, source_target_pairs={{0,4},{4,8},{8,12},{12,0},{1,5},{5,9},{9,13},{13,1},{2,6},{6,10},{... | collective-permute-start | bytes 99848 | tf_op jit(solution)/shard_map/ppermute | solution.py:135
  127.2 9.6 %collective-permute-start.20 = (bf16[65,256]{1,0:T(8,128)(2,1)S(1)}, bf16[65,256]{1,0:T(8,128)(2,1)S(1)}, u32[]{:S(2)}, u32[]{:S(2)}) collective-permute-start(bf16[65,256]{1,0:T(8,128)(2,1)S(1)} %pad_maximum_fusion.6), channel_id=1, source_target_pairs={{0,8},{4,12},{8,0},{12,4},{1,9},{5,13},{9,1},{13,5},{2,10},{6,14},... | collective-permute-start | bytes 99848 | tf_op jit(solution)/shard_map/ppermute | solution.py:135
  169.7 42.9 %collective-permute-start.30 = (bf16[64,4096]{1,0:T(8,128)(2,1)}, bf16[64,4096]{1,0:T(8,128)(2,1)S(1)}, u32[]{:S(2)}, u32[]{:S(2)}) collective-permute-start(bf16[64,4096]{1,0:T(8,128)(2,1)} %get-tuple-element.67), channel_id=1, source_target_pairs={{0,4},{4,8},{8,12},{12,0},{1,5},{5,9},{9,13},{13,1},{2,6},{6,10},{... | collective-permute-start | bytes 1572872 | tf_op jit(solution)/shard_map/ppermute | solution.py:135
  169.7 42.9 %collective-permute-start.29 = (bf16[64,4096]{1,0:T(8,128)(2,1)}, bf16[64,4096]{1,0:T(8,128)(2,1)S(1)}, u32[]{:S(2)}, u32[]{:S(2)}) collective-permute-start(bf16[64,4096]{1,0:T(8,128)(2,1)} %get-tuple-element.67), channel_id=1, source_target_pairs={{0,12},{4,0},{8,4},{12,8},{1,13},{5,1},{9,5},{13,9},{2,14},{6,2},{... | collective-permute-start | bytes 1572872 | tf_op jit(solution)/shard_map/ppermute | solution.py:135
  179.9 16.3 %collective-permute-start.27 = (f32[65,64]{0,1:T(8,128)S(1)}, f32[65,64]{0,1:T(8,128)S(1)}, u32[]{:S(2)}, u32[]{:S(2)}) collective-permute-start(f32[65,64]{0,1:T(8,128)S(1)} %add.315), channel_id=1, source_target_pairs={{0,4},{4,0},{8,12},{12,8},{1,5},{5,1},{9,13},{13,9},{2,6},{6,2},{1... | collective-permute-start | bytes 49928 | tf_op jit(solution)/shard_map/ppermute | solution.py:167
  196.1 16.4 %collective-permute-start.28 = (f32[65,64]{0,1:T(8,128)S(1)}, f32[65,64]{0,1:T(8,128)S(1)}, u32[]{:S(2)}, u32[]{:S(2)}) collective-permute-start(f32[65,64]{0,1:T(8,128)S(1)} %add.316), channel_id=1, source_target_pairs={{0,8},{4,12},{8,0},{12,4},{1,9},{5,13},{9,1},{13,5},{2,10},{6,14},... | collective-permute-start | bytes 49928 | tf_op jit(solution)/shard_map/ppermute | solution.py:167
  198.5 32.2 %collective-permute-start.34 = (bf16[64,4096]{1,0:T(8,128)(2,1)}, bf16[64,4096]{1,0:T(8,128)(2,1)S(1)}, u32[]{:S(2)}, u32[]{:S(2)}) collective-permute-start(bf16[64,4096]{1,0:T(8,128)(2,1)} %get-tuple-element.67), channel_id=1, source_target_pairs={{0,8},{4,12},{8,0},{12,4},{1,9},{5,13},{9,1},{13,5},{2,10},{6,14},... | collective-permute-start | bytes 1572872 | tf_op jit(solution)/shard_map/ppermute | solution.py:135
  226.0 15.1 %collective-permute-start.33 = (f32[1,4096]{1,0:T(1,128)S(1)}, f32[1,4096]{1,0:T(1,128)S(1)}, u32[]{:S(2)}, u32[]{:S(2)}) collective-permute-start(f32[1,4096]{1,0:T(1,128)S(1)} %get-tuple-element.91), channel_id=1, source_target_pairs={{0,4},{4,8},{8,12},{12,0},{1,5},{5,9},{9,13},{13,1},{2,6},{6,10},{... | collective-permute-start | bytes 49160 | tf_op jit(solution)/shard_map/ppermute | solution.py:135
  226.1 15.1 %collective-permute-start.32 = (f32[1,4096]{1,0:T(1,128)S(1)}, f32[1,4096]{1,0:T(1,128)S(1)}, u32[]{:S(2)}, u32[]{:S(2)}) collective-permute-start(f32[1,4096]{1,0:T(1,128)S(1)} %get-tuple-element.91), channel_id=1, source_target_pairs={{0,8},{4,12},{8,0},{12,4},{1,9},{5,13},{9,1},{13,5},{2,10},{6,14},... | collective-permute-start | bytes 49160 | tf_op jit(solution)/shard_map/ppermute | solution.py:135
  226.2 15.0 %collective-permute-start.31 = (f32[1,4096]{1,0:T(1,128)S(1)}, f32[1,4096]{1,0:T(1,128)S(1)}, u32[]{:S(2)}, u32[]{:S(2)}) collective-permute-start(f32[1,4096]{1,0:T(1,128)S(1)} %get-tuple-element.91), channel_id=1, source_target_pairs={{0,12},{4,0},{8,4},{12,8},{1,13},{5,1},{9,5},{13,9},{2,14},{6,2},{... | collective-permute-start | bytes 49160 | tf_op jit(solution)/shard_map/ppermute | solution.py:135
  (13 other events, 80.8 us)

commit v3 on v2

--- a/solution.py
+++ b/solution.py
@@ -60,16 +60,16 @@
     lax.fori_loop(0, nrow // unroll, samples, 0)
     for r in range(nsub):
         data_ref[:, r * LANES : (r + 1) * LANES] = scr[pl.ds(r * pitch, nrow), :].astype(jnp.bfloat16)
-    marg_ref[...] = SCALE * lax.dot_general(
-        feat_ref[...], data_ref[...], (((1,), (1,)), ((), ())), preferred_element_type=jnp.float32
+    marg = lax.dot_general(
+        data_ref[...], feat_ref[...], (((1,), (1,)), ((), ())), preferred_element_type=jnp.float32
     )
-
-
-def make_table(starts, tab, part, feats):
+    marg_ref[...] = SCALE * marg.T[: marg_ref.shape[0]]
+
+
+def make_table(starts, tab, part, feats, ncol):
     count = starts.shape[0]
     nsub = part.shape[0]
     nfeat = nsub * LANES
-    ncol = feats.shape[0]
     nrow = min(256, count)
     pitch = nrow + 8
     return pl.pallas_call(
@@ -80,7 +80,7 @@
             in_specs=[
                 pl.BlockSpec(tab.shape, lambda i, s: (0, 0)),
                 pl.BlockSpec(part.shape, lambda i, s: (0, 0)),
-                pl.BlockSpec((ncol, nfeat), lambda i, s: (0, 0)),
+                pl.BlockSpec(feats.shape, lambda i, s: (0, 0)),
             ],
             out_specs=[
                 pl.BlockSpec((nrow, nfeat), lambda i, s: (i, 0)),
@@ -100,35 +100,97 @@
     )(starts, tab, part, feats)
 
 
-def back_body(mix_ref, data_ref, old_ref, out_ref):
-    @pl.when(pl.program_id(1) == 0)
-    def _():
-        out_ref[...] = old_ref[...]
-
-    out_ref[...] += jnp.dot(mix_ref[...], data_ref[...], preferred_element_type=jnp.float32)
-
-
-def back(mixed, data, total):
-    ncol, count = mixed.shape
-    nfeat = data.shape[1]
-    kb = min(1024, count)
-    fb = min(4096, nfeat)
+def back_body(*refs, nblk):
+    mixes, datas, (old_ref, out_ref) = refs[:nblk], refs[nblk : 2 * nblk], refs[2 * nblk :]
+    total = old_ref[...]
+    for mix_ref, data_ref in zip(mixes, datas):
+        total += jnp.dot(mix_ref[...], data_ref[...], preferred_element_type=jnp.float32)
+    out_ref[...] = total
+
+
+def back(mixes, datas, old, half):
+    nblk = len(mixes)
+    ncol, count = mixes[0].shape
+    width = old.shape[1]
+    tile = min(512, width)
+    steps = width // tile
+    at = half * steps
     return pl.pallas_call(
-        back_body,
-        grid=(nfeat // fb, count // kb),
-        in_specs=[
-            pl.BlockSpec((ncol, kb), lambda f, k: (0, k)),
-            pl.BlockSpec((kb, fb), lambda f, k: (k, f)),
-            pl.BlockSpec((ncol, fb), lambda f, k: (0, f)),
-        ],
-        out_specs=pl.BlockSpec((ncol, fb), lambda f, k: (0, f)),
-        out_shape=jax.ShapeDtypeStruct((ncol, nfeat), jnp.float32),
+        functools.partial(back_body, nblk=nblk),
+        grid=(steps,),
+        in_specs=[pl.BlockSpec((ncol, count), lambda f: (0, 0))] * nblk
+        + [pl.BlockSpec((count, tile), lambda f: (0, at + f))] * nblk
+        + [pl.BlockSpec((ncol, tile), lambda f: (0, f))],
+        out_specs=pl.BlockSpec((ncol, tile), lambda f: (0, f)),
+        out_shape=jax.ShapeDtypeStruct((ncol, width), jnp.float32),
         compiler_params=pltpu.CompilerParams(vmem_limit_bytes=48 << 20),
         cost_estimate=pl.CostEstimate(
-            flops=2 * count * nfeat * ncol, bytes_accessed=count * nfeat * 2, transcendentals=0
+            flops=2 * count * width * ncol * nblk, bytes_accessed=count * width * 2 * nblk, transcendentals=0
         ),
         name="back",
-    )(mixed, data, total)
+    )(*mixes, *datas, old)
+
+
+def solve_body(prod_ref, grad_ref, *refs):
+    step_ref = refs[-1]
+    rank = prod_ref.shape[1]
+    inner = prod_ref[:rank, :]
+    mat = 0.5 * (inner + inner.T)
+    rhs = prod_ref[rank : rank + 1, :]
+    eye = (
+        lax.broadcasted_iota(jnp.int32, (rank, rank), 0) == lax.broadcasted_iota(jnp.int32, (rank, rank), 1)
+    ).astype(jnp.float32)
+    col = jnp.sum(eye * rhs, axis=1, keepdims=True)
+    row_of = lax.broadcasted_iota(jnp.int32, (rank, 1), 0)
+    for k in range(rank):
+        lead = mat[k : k + 1, :] / mat[k : k + 1, k : k + 1]
+        head = col[k : k + 1, :] / mat[k : k + 1, k : k + 1]
+        by = jnp.where(row_of == k, 0.0, mat[:, k : k + 1])
+        mat = jnp.where(row_of == k, lead, mat - by * lead)
+        col = jnp.where(row_of == k, head, col - by * head)
+    at = 0
+    for ref in refs[:-1]:
+        width = ref.shape[1]
+        fit = jnp.sum(ref[...] * col, axis=0, keepdims=True)
+        step_ref[:, at : at + width] = (grad_ref[:, at : at + width] - fit) * (1.0 / LAM)
+        at += width
+
+
+def solve(prods, grad, halves):
+    return pl.pallas_call(
+        solve_body,
+        out_shape=jax.ShapeDtypeStruct(grad.shape, jnp.float32),
+        compiler_params=pltpu.CompilerParams(vmem_limit_bytes=32 << 20),
+        name="solve",
+    )(prods, grad, *halves)
+
+
+def place_body(at_ref, *refs, size):
+    for d in range(size):
+
+        @pl.when(pl.program_id(0) == d)
+        def _():
+            refs[-1][...] = refs[d][...].astype(jnp.float32)
+
+
+def place(z, parts, half, nhalf, old=None):
+    size = len(parts)
+    rank, width = parts[0].shape
+    extra = [] if old is None else [old]
+    return pl.pallas_call(
+        functools.partial(place_body, size=size),
+        grid_spec=pltpu.PrefetchScalarGridSpec(
+            num_scalar_prefetch=1,
+            grid=(size,),
+            in_specs=[pl.BlockSpec((rank, width), lambda d, at: (0, 0))] * size
+            + [pl.BlockSpec(memory_space=pl.ANY)] * len(extra),
+            out_specs=pl.BlockSpec((rank, width), lambda d, at: (0, lax.rem(at[0] + d, size) * nhalf + half)),
+        ),
+        out_shape=jax.ShapeDtypeStruct((rank, width * nhalf * size), jnp.float32),
+        input_output_aliases={1 + size: 0} if extra else {},
+        compiler_params=pltpu.CompilerParams(vmem_limit_bytes=32 << 20),
+        name="place",
+    )(z.reshape(1), *parts, *extra)
 
 
 def shift(x, axis, size, by):
@@ -161,12 +223,12 @@
 
 
 def all_sum(x, axis, size):
-    if size & (size - 1) == 0 and size <= 4:
-        step = 1
-        while step < size:
-            x = x + lax.ppermute(x, axis, [(i, i ^ step) for i in range(size)])
-            step *= 2
-        return x
+    if size == 2:
+        return x + shift(x, axis, size, 1)
+    if size == 4:
+        one, two, three = (shift(x, axis, size, -d) for d in (1, 2, 3))
+        even = lax.axis_index(axis) % 2 == 0
+        return (x + jnp.where(even, one, three)) + (two + jnp.where(even, three, one))
     return lax.psum(x, axis)
 
 
@@ -225,6 +287,7 @@
     own_weights = lax.dynamic_slice_in_dim(weights, own, nfeat, 0)[None]
     feats = jnp.concatenate([sketch_t, own_weights.astype(jnp.bfloat16)], axis=0)
     ncol = rank + 1
+    padded = jnp.pad(feats, ((0, -ncol % LANES), (0, 0)))
 
     order = [(c, du, ds) for c in range(nchunk) for du in reversed(range(nsub)) for ds in reversed(range(nsec))]
     data, marg, from_sub, from_sec, mixed, stage = {}, {}, {}, {}, {}, {}
@@ -269,7 +332,7 @@
     last = []
     for c, du, ds in order:
         begin = after(starts[c, ds, du].reshape(-1), *last, *older)
-        data[c, du, ds], marg[c, du, ds] = make_table(begin, tab, part, feats)
+        data[c, du, ds], marg[c, du, ds] = make_table(begin, tab, part, padded, ncol)
         last = [marg[c, du, ds]]
         older, due = due, boundary()
         if du:
@@ -286,43 +349,82 @@
                 if (c, du, ds) == order[-1]:
                     due += boundary()
 
-    total = jnp.zeros((ncol, nfeat), jnp.float32)
-    for c in range(nchunk):
-        for du in range(nsub):
-            for ds in range(nsec):
-                while (c, du, ds) not in mixed:
-                    due += boundary()
-                total = back(after(mixed[c, du, ds], *older), data[c, du, ds], total)
-                older, due = due, boundary(total)
-    total = total * SCALE
-
+    nhalf = 2
+    width = nfeat // nhalf
+    totals = [jnp.zeros((ncol, width), jnp.float32)] * nhalf
     sketch_f = sketch_t.astype(jnp.float32)
-    grad = total[rank:] + LAM * own_weights
-    sketched = total[:rank] + LAM * sketch_f
-    block = sketched.astype(jnp.bfloat16)
-    wide = {d: shift(block, "rows", nrows, -d) for d in range(1, nrows)} if nrows <= 4 else None
-    left = jnp.concatenate([LAM * sketch_f + sketched, grad], axis=0)
-    prods = lax.dot_general(
-        left, sketched, (((1,), (1,)), ((), ())), precision=lax.Precision.HIGHEST
+    grads, parts, blocks, wide, lefts = [None] * nhalf, [None] * nhalf, [None] * nhalf, [None] * nhalf, [None] * nhalf
+
+    def product(c, dus, half):
+        names = [(c, du, ds) for du in dus for ds in range(nsec)]
+        while any(name not in mixed for name in names):
+            due.extend(boundary())
+        mixes = [mixed[name] for name in names]
+        mixes[0] = after(mixes[0], *older)
+        totals[half] = back(mixes, [data[name] for name in names], totals[half], half)
+
+    def close(half, *deps):
+        total = totals[half] * SCALE
+        cut = slice(half * width, (half + 1) * width)
+        grads[half] = total[rank:] + LAM * own_weights[:, cut]
+        parts[half] = total[:rank] + LAM * sketch_f[:, cut]
+        lefts[half] = jnp.concatenate([LAM * sketch_f[:, cut] + parts[half], grads[half]], axis=0)
+        blocks[half] = parts[half].astype(jnp.bfloat16)
+
+    def send(half, ds, *deps):
+        block = after(blocks[half], *deps)
+        wide[half] = wide[half] or {0: blocks[half]}
+        for d in ds:
+            wide[half][d] = shift(block, "rows", nrows, -d)
+
+    plan = [(0, [du], half) for half in range(nhalf) for du in range(nsub)]
+    for c, dus, half in plan[:-1]:
+        product(c, dus, half)
+        older, due = due, boundary(totals[half])
+    product(nchunk - 1, range(nsub), 0)
+    close(0)
+    direct = nrows <= 4
+    if direct:
+        send(0, range(1, nrows))
+    c, dus, half = plan[-1]
+    older = [totals[0]]
+    product(c, dus, half)
+    older = [wide[0][1]] if direct else []
+    product(nchunk - 1, range(nsub), 1)
+    close(1)
+    if direct:
+        send(1, [1])
+
+    prods = sum(
+        lax.dot_general(left, part, (((1,), (1,)), ((), ())), precision=lax.Precision.HIGHEST)
+        for left, part in zip(lefts, parts)
     )
-    prods = all_sum(all_sum(all_sum(prods, "sub", nsub), "sec", nsec), "rows", nrows)
-    if wide:
-        prods = after(prods, *[wide[d] for d in (1, nrows - 1)])
-    inner = prods[:rank]
-    inner = 0.5 * (inner + inner.T)
-    factor = jnp.linalg.cholesky(inner)
-    middle = lax.linalg.triangular_solve(factor, prods[rank:].T, left_side=True, lower=True)
-    coef = lax.linalg.triangular_solve(
-        factor, middle, left_side=True, lower=True, transpose_a=True
-    )
-    step = (grad - jnp.dot(coef.T, sketched, precision=lax.Precision.HIGHEST)) / LAM
-
-    def spread(x, rest=None):
-        parts = collect(x, "rows", nrows, 0) if rest is None else jnp.stack([x] + rest, axis=0)
-        parts = roll_to(parts, 0, nrows, (nrows - z) % nrows)
+    prods = all_sum(prods, "sub", nsub)
+    if direct:
+        prods = after(prods, wide[0][nrows - 1])
+    prods = all_sum(prods, "sec", nsec)
+    if direct:
+        prods = after(prods, *wide[0].values(), wide[1][1])
+    prods = all_sum(prods, "rows", nrows)
+    if direct:
+        send(1, range(2, nrows), prods)
+    step = solve(prods, jnp.concatenate(grads, axis=1), parts)
+
+    def spread(x):
+        parts = roll_to(collect(x, "rows", nrows, 0), 0, nrows, (nrows - z) % nrows)
         return jnp.moveaxis(parts, 0, 1).reshape(x.shape[0], -1).astype(jnp.float32)
 
-    return (spread(step)[0], spread(block, wide and [wide[d] for d in range(1, nrows)]).T)
+    if direct:
+        step = after(step, wide[1][nrows - 1])
+    step = spread(step)[0]
+    if direct:
+        wide[1][0] = after(wide[1][0], step)
+        out = None
+        for half in range(nhalf):
+            out = place(z, [wide[half][d] for d in range(nrows)], half, nhalf, out)
+    else:
+        out = spread(jnp.concatenate(blocks, axis=1))
+    return (step, out.T)
 
 
 def solution(mesh):

time: 243 us -> 212 us (0.87)
  waiting for transfers between devices: 42.5 us -> 24.6 us
  other arithmetic: 17.9 us -> 3.93 us
  local copies, waits for them, and re-layouts: 12.9 us -> 1.59 us
  Pallas kernels: 125 us -> 133 us
  starting transfers between devices: 39.9 us -> 46 us
    ppermute x4 -> x0, waiting for transfers between devices: 33.3 us -> none  [all_sum(): x = x + lax.ppermute(x, axis, [(i, i ^ step) for i in range(size)])]
    ppermute x31 -> x39, waiting for transfers between devices: 9.15 us -> 24.6 us  [shift(): return lax.ppermute(x, axis, [(i, (i + by) % size) for i in range(size)])]
    another operation x9 -> x4, other arithmetic: 12.1 us -> 0.05 us  [the longest x3 6.52 us: local(): factor = jnp.linalg.cholesky(inner)]
    ppermute x31 -> x39, starting transfers between devices: 35.9 us -> 46 us  [shift(): return lax.ppermute(x, axis, [(i, (i + by) % size) for i in range(size)])]
    pallas_call x8 -> x9, Pallas kernels: 39.8 us -> 48.2 us  [the longest x6 34.9 us: back(): pl.pallas_call(functools.partial(back_body, nblk=nblk), grid=(steps,), in...]
    unnamed x16 -> x13, local copies, waits for them, and re-layouts: 6.08 us -> 0.07 us
    ppermute x4 -> x0, starting transfers between devices: 3.96 us -> none  [all_sum(): x = x + lax.ppermute(x, axis, [(i, i ^ step) for i in range(size)])]
    unnamed x2 -> x0, other arithmetic: 3.21 us -> none
  transfers between devices with their start and end apart: 35 -> 39, of which waited for: 9 -> 12; matrix products, arithmetic and copies ran while one was open for 12% -> 3% of each run, Pallas kernels for 39% -> 53%
where the time goes in v3:
time: 212 us; the launch traced here: 211 us
  Pallas kernels  133 us (63%)
  starting transfers between devices  46 us (22%)
  waiting for transfers between devices  24.6 us (12%)
  other arithmetic  3.93 us (2%)
    pallas_call x8, Pallas kernels, make_table(): pl.pallas_call(functools.partial(table_body, unroll=64, pitch=pitch), gri...  84.5 us
    ppermute x39, starting transfers between devices, shift(): return lax.ppermute(x, axis, [(i, (i + by) % size) for i in range(size)])  46 us
    pallas_call x6, Pallas kernels, back(): pl.pallas_call(functools.partial(back_body, nblk=nblk), grid=(steps,), in...  34.9 us
    ppermute x39, waiting for transfers between devices, shift(): return lax.ppermute(x, axis, [(i, (i + by) % size) for i in range(size)])  24.6 us
    pallas_call x1, Pallas kernels, solve(): pl.pallas_call(solve_body, out_shape=jax.ShapeDtypeStruct(grad.shape, jnp...  9.57 us
  transfers between devices with their start and end apart: 39, of which 12 were waited for; matrix products, arithmetic and copies ran while one was open for 3% of the time, Pallas kernels for 53%

profile of v3, /device:TPU:0, one launch (start us, length us, event | category | flops | bytes accessed | tf_op | source)
XLA Modules:
  0.0 211.1 jit_solution(18378277549945524507)
XLA Ops:
  1.4 3.1 %collective-permute-start.2 = (s32[2,2,2,256]{3,2,1,0:T(2,128)S(1)}, s32[2,2,2,256]{3,2,1,0:T(2,128)S(1)}, u32[]{:S(2)}, u32[]{:S(2)}) collective-permute-start(s32[2,2,2,256]{3,2,1,0:T(2,128)S(1)} %fusion.40), channel_id=1, source_target_pairs={{0,4},{4,8},{8,12},{12,0},{1,5},{5,9},{9,13},{13,1},{2,6},{6,10},{... | collective-permute-start | bytes 24584 | tf_op jit(solution)/shard_map/ppermute | solution.py:197
  4.5 2.6 %collective-permute-start.1 = (s32[2,2,2,256]{3,2,1,0:T(2,128)S(1)}, s32[2,2,2,256]{3,2,1,0:T(2,128)S(1)}, u32[]{:S(2)}, u32[]{:S(2)}) collective-permute-start(s32[2,2,2,256]{3,2,1,0:T(2,128)S(1)} %fusion.40), channel_id=1, source_target_pairs={{0,8},{4,12},{8,0},{12,4},{1,9},{5,13},{9,1},{13,5},{2,10},{6,14},... | collective-permute-start | bytes 24584 | tf_op jit(solution)/shard_map/ppermute | solution.py:197
  11.6 10.6 %make_table.8 = (bf16[1024,4096]{1,0:T(8,128)(2,1)}, f32[65,1024]{1,0:T(8,128)S(1)}) custom-call(s32[1024]{0:T(1024)S(1)} %bitcast.55, f32[552,128]{1,0:T(8,128)S(1)} %fusion.21.tab_ref, f32[32,128]{1,0:T(8,128)S(1)} %fusion.36.a_ref, bf16[128,4096]{1,0:T(8,128)(2,1)S(1)} %fusion.2.feat_ref), custom_call_target="tpu_custom_call" | custom-call | flops 6291456000 | bytes 8388608 | tf_op jit(solution)/shard_map/make_table/pallas_call | solution.py:75
  22.3 10.5 %make_table.9 = (bf16[1024,4096]{1,0:T(8,128)(2,1)}, f32[65,1024]{1,0:T(8,128)S(1)}) custom-call(s32[1024]{0:T(1024)S(1)} %bitcast.54, f32[552,128]{1,0:T(8,128)S(1)} %fusion.21.tab_ref, f32[32,128]{1,0:T(8,128)S(1)} %fusion.36.a_ref, bf16[128,4096]{1,0:T(8,128)(2,1)S(1)} %fusion.2.feat_ref), custom_call_target="tpu_custom_call" | custom-call | flops 6291456000 | bytes 8388608 | tf_op jit(solution)/shard_map/make_table/pallas_call | solution.py:75
  33.3 10.6 %make_table.10 = (bf16[1024,4096]{1,0:T(8,128)(2,1)}, f32[65,1024]{1,0:T(8,128)S(1)}) custom-call(s32[1024]{0:T(1024)S(1)} %bitcast.53, f32[552,128]{1,0:T(8,128)S(1)} %fusion.21.tab_ref, f32[32,128]{1,0:T(8,128)S(1)} %fusion.36.a_ref, bf16[128,4096]{1,0:T(8,128)(2,1)S(1)} %fusion.2.feat_ref), custom_call_target="tpu_custom_call" | custom-call | flops 6291456000 | bytes 8388608 | tf_op jit(solution)/shard_map/make_table/pallas_call | solution.py:75
  45.5 10.6 %make_table.11 = (bf16[1024,4096]{1,0:T(8,128)(2,1)}, f32[65,1024]{1,0:T(8,128)S(1)}) custom-call(s32[1024]{0:T(1024)S(1)} %bitcast.52, f32[552,128]{1,0:T(8,128)S(1)} %fusion.21.tab_ref, f32[32,128]{1,0:T(8,128)S(1)} %fusion.36.a_ref, bf16[128,4096]{1,0:T(8,128)(2,1)S(1)} %fusion.2.feat_ref), custom_call_target="tpu_custom_call" | custom-call | flops 6291456000 | bytes 8388608 | tf_op jit(solution)/shard_map/make_table/pallas_call | solution.py:75
  60.0 3.1 %collective-permute-done.6 = f32[65,256]{1,0:T(8,128)S(1)} collective-permute-done((f32[65,256]{1,0:T(8,128)S(1)}, f32[65,256]{1,0:T(8,128)S(1)}, u32[]{:S(2)}, u32[]{:S(2)}) %collective-permute-start.6) | collective-permute-done | bytes 66592 | tf_op jit(solution)/shard_map/ppermute | solution.py:197
  65.3 2.5 %collective-permute-start.10 = (bf16[65,256]{1,0:T(8,128)(2,1)S(1)}, bf16[65,256]{1,0:T(8,128)(2,1)S(1)}, u32[]{:S(2)}, u32[]{:S(2)}) collective-permute-start(bf16[65,256]{1,0:T(8,128)(2,1)S(1)} %pad_maximum_fusion.4), channel_id=1, source_target_pairs={{0,12},{4,0},{8,4},{12,8},{1,13},{5,1},{9,5},{13,9},{2,14},{6,2},{... | collective-permute-start | bytes 99848 | tf_op jit(solution)/shard_map/ppermute | solution.py:197
  68.5 10.5 %make_table.12 = (bf16[1024,4096]{1,0:T(8,128)(2,1)}, f32[65,1024]{1,0:T(8,128)S(1)}) custom-call(s32[1024]{0:T(1024)S(1)} %bitcast.51, f32[552,128]{1,0:T(8,128)S(1)} %fusion.21.tab_ref, f32[32,128]{1,0:T(8,128)S(1)} %fusion.36.a_ref, bf16[128,4096]{1,0:T(8,128)(2,1)S(1)} %fusion.2.feat_ref), custom_call_target="tpu_custom_call" | custom-call | flops 6291456000 | bytes 8388608 | tf_op jit(solution)/shard_map/make_table/pallas_call | solution.py:75
  79.6 10.5 %make_table.13 = (bf16[1024,4096]{1,0:T(8,128)(2,1)}, f32[65,1024]{1,0:T(8,128)S(1)}) custom-call(s32[1024]{0:T(1024)S(1)} %bitcast.50, f32[552,128]{1,0:T(8,128)S(1)} %fusion.21.tab_ref, f32[32,128]{1,0:T(8,128)S(1)} %fusion.36.a_ref, bf16[128,4096]{1,0:T(8,128)(2,1)S(1)} %fusion.2.feat_ref), custom_call_target="tpu_custom_call" | custom-call | flops 6291456000 | bytes 8388608 | tf_op jit(solution)/shard_map/make_table/pallas_call | solution.py:75
  90.8 10.6 %make_table.14 = (bf16[1024,4096]{1,0:T(8,128)(2,1)}, f32[65,1024]{1,0:T(8,128)S(1)}) custom-call(s32[1024]{0:T(1024)S(1)} %bitcast.49, f32[552,128]{1,0:T(8,128)S(1)} %fusion.21.tab_ref, f32[32,128]{1,0:T(8,128)S(1)} %fusion.36.a_ref, bf16[128,4096]{1,0:T(8,128)(2,1)S(1)} %fusion.2.feat_ref), custom_call_target="tpu_custom_call" | custom-call | flops 6291456000 | bytes 8388608 | tf_op jit(solution)/shard_map/make_table/pallas_call | solution.py:75
  103.0 10.6 %make_table.15 = (bf16[1024,4096]{1,0:T(8,128)(2,1)}, f32[65,1024]{1,0:T(8,128)S(1)}) custom-call(s32[1024]{0:T(1024)S(1)} %bitcast.48, f32[552,128]{1,0:T(8,128)S(1)} %fusion.21.tab_ref, f32[32,128]{1,0:T(8,128)S(1)} %fusion.36.a_ref, bf16[128,4096]{1,0:T(8,128)(2,1)S(1)} %fusion.2.feat_ref), custom_call_target="tpu_custom_call" | custom-call | flops 6291456000 | bytes 8388608 | tf_op jit(solution)/shard_map/make_table/pallas_call | solution.py:75
  113.6 3.7 %collective-permute-start.17 = (f32[65,256]{1,0:T(8,128)S(1)}, f32[65,256]{1,0:T(8,128)S(1)}, u32[]{:S(2)}, u32[]{:S(2)}) collective-permute-start(f32[65,256]{1,0:T(8,128)S(1)} %get-tuple-element.93), channel_id=1, source_target_pairs={{0,12},{4,0},{8,4},{12,8},{1,13},{5,1},{9,5},{13,9},{2,14},{6,2},{... | collective-permute-start | bytes 199688 | tf_op jit(solution)/shard_map/ppermute | solution.py:197
  118.1 4.9 %back.6.refs_4_ = f32[65,2048]{1,0:T(8,128)S(1)} custom-call(bf16[65,1024]{1,0:T(8,128)(2,1)S(1)} %pad_maximum_fusion.2.refs_0_, bf16[65,1024]{1,0:T(8,128)(2,1)S(1)} %collective-permute-done.18.refs_1_, bf16[1024,4096]{1,0:T(8,128)(2,1)} %get-tuple-element.55.refs_2_, bf16[1024,4096]{1,0:T(8,128)(2,1)} %get-tuple-element.56.refs_3_, ...), custom_call_target="tpu_custom_call" | custom-call | flops 545259520 | bytes 8388608 | tf_op jit(solution)/shard_map/back/pallas_call | solution.py:118
  129.3 4.9 %back.7.refs_8_ = f32[65,2048]{1,0:T(8,128)S(1)} custom-call(bf16[65,1024]{1,0:T(8,128)(2,1)S(1)} %get-tuple-element.70.refs_0_, bf16[65,1024]{1,0:T(8,128)(2,1)S(1)} %get-tuple-element.90.refs_1_, bf16[1024,4096]{1,0:T(8,128)(2,1)} %get-tuple-element.59.refs_2_, bf16[1024,4096]{1,0:T(8,128)(2,1)} %get-tuple-element.60.refs_3_, f32[65,2048]{1,0:T(8,128)S(1)} %back.6.refs_4_), custom_call_target="tpu_custom_call" | custom-call | flops 545259520 | bytes 8388608 | tf_op jit(solution)/shard_map/back/pallas_call | solution.py:118
  134.9 4.9 %back.8.refs_4_ = f32[65,2048]{1,0:T(8,128)S(1)} custom-call(bf16[65,1024]{1,0:T(8,128)(2,1)S(1)} %pad_maximum_fusion.2.refs_0_, bf16[65,1024]{1,0:T(8,128)(2,1)S(1)} %collective-permute-done.18.refs_1_, bf16[1024,4096]{1,0:T(8,128)(2,1)} %get-tuple-element.55.refs_2_, bf16[1024,4096]{1,0:T(8,128)(2,1)} %get-tuple-element.56.refs_3_, ...), custom_call_target="tpu_custom_call" | custom-call | flops 545259520 | bytes 8388608 | tf_op jit(solution)/shard_map/back/pallas_call | solution.py:118
  141.5 7.6 %back.9 = f32[65,2048]{1,0:T(8,128)S(1)} custom-call(bf16[65,1024]{1,0:T(8,128)(2,1)S(1)} %pad_maximum_fusion.3.refs_0_, bf16[65,1024]{1,0:T(8,128)(2,1)S(1)} %collective-permute-done.23.refs_1_, bf16[65,1024]{1,0:T(8,128)(2,1)S(1)} %get-tuple-element.89.refs_2_, bf16[65,1024]{1,0:T(8,128)(2,1)S(1)} %get-tuple-element.88.refs_3_, ...), custom_call_target="tpu_custom_call" | custom-call | flops 1090519040 | bytes 16777216 | tf_op jit(solution)/shard_map/back/pallas_call | solution.py:118
  153.1 4.9 %back.10.refs_8_ = f32[65,2048]{1,0:T(8,128)S(1)} custom-call(bf16[65,1024]{1,0:T(8,128)(2,1)S(1)} %get-tuple-element.70.refs_0_, bf16[65,1024]{1,0:T(8,128)(2,1)S(1)} %get-tuple-element.90.refs_1_, bf16[1024,4096]{1,0:T(8,128)(2,1)} %get-tuple-element.59.refs_2_, bf16[1024,4096]{1,0:T(8,128)(2,1)} %get-tuple-element.60.refs_3_, f32[65,2048]{1,0:T(8,128)S(1)} %back.8.refs_4_), custom_call_target="tpu_custom_call" | custom-call | flops 545259520 | bytes 8388608 | tf_op jit(solution)/shard_map/back/pallas_call | solution.py:118
  158.0 5.9 %collective-permute-done.25.refs_1_ = bf16[64,2048]{1,0:T(8,128)(2,1)S(1)} collective-permute-done((bf16[64,2048]{1,0:T(8,128)(2,1)S(1)}, bf16[64,2048]{1,0:T(8,128)(2,1)S(1)}, u32[]{:S(2)}, u32[]{:S(2)}) %collective-permute-start.25) | collective-permute-done | bytes 262176 | tf_op jit(solution)/shard_map/ppermute | solution.py:197
  163.9 7.6 %back.11 = f32[65,2048]{1,0:T(8,128)S(1)} custom-call(bf16[65,1024]{1,0:T(8,128)(2,1)S(1)} %pad_maximum_fusion.3.refs_0_, bf16[65,1024]{1,0:T(8,128)(2,1)S(1)} %collective-permute-done.23.refs_1_, bf16[65,1024]{1,0:T(8,128)(2,1)S(1)} %get-tuple-element.89.refs_2_, bf16[65,1024]{1,0:T(8,128)(2,1)S(1)} %get-tuple-element.88.refs_3_, ...), custom_call_target="tpu_custom_call" | custom-call | flops 1090519040 | bytes 16777216 | tf_op jit(solution)/shard_map/back/pallas_call | solution.py:118
  176.0 2.5 %collective-permute-done.28 = f32[65,64]{1,0:T(8,128)S(1)} collective-permute-done((f32[65,64]{1,0:T(8,128)S(1)}, f32[65,64]{1,0:T(8,128)S(1)}, u32[]{:S(2)}, u32[]{:S(2)}) %collective-permute-start.28) | collective-permute-done | bytes 16672 | tf_op jit(solution)/shard_map/ppermute | solution.py:197
  179.7 3.7 %collective-permute-start.32 = (f32[65,64]{1,0:T(8,128)S(1)}, f32[65,64]{1,0:T(8,128)S(1)}, u32[]{:S(2)}, u32[]{:S(2)}) collective-permute-start(f32[65,64]{1,0:T(8,128)S(1)} %add.321), channel_id=1, source_target_pairs={{0,4},{4,8},{8,12},{12,0},{1,5},{5,9},{9,13},{13,1},{2,6},{6,10},{... | collective-permute-start | bytes 49928 | tf_op jit(solution)/shard_map/ppermute | solution.py:197
  187.5 2.8 %collective-permute-start.38 = (bf16[64,2048]{1,0:T(8,128)(2,1)S(1)}, bf16[64,2048]{1,0:T(8,128)(2,1)S(1)}, u32[]{:S(2)}, u32[]{:S(2)}) collective-permute-start(bf16[64,2048]{1,0:T(8,128)(2,1)S(1)} %get-tuple-element.75.refs_0_), channel_id=1, source_target_pairs={{0,8},{4,12},{8,0},{12,4},{1,9},{5,13},{9,1},{13,5},{2,10},{6,14},... | collective-permute-start | bytes 786440 | tf_op jit(solution)/shard_map/ppermute | solution.py:197
  190.3 9.6 %solve.1 = f32[1,4096]{1,0:T(1,128)S(1)} custom-call(f32[65,64]{1,0:T(8,128)S(1)} %add_add_fusion.2.prod_ref, f32[1,4096]{1,0:T(1,128)S(1)} %pad_maximum_fusion.6.grad_ref, f32[64,2048]{1,0:T(8,128)S(1)} %get-tuple-element.79.refs_0_, f32[64,2048]{1,0:T(8,128)S(1)} %get-tuple-element.77.refs_1_), custom_call_target="tpu_custom_call" | custom-call | tf_op jit(solution)/shard_map/solve/pallas_call | solution.py:160
  (136 shorter events, 51.1 us)
Async XLA Ops:
  1.4 10.0 %collective-permute-start.2 = (s32[2,2,2,256]{3,2,1,0:T(2,128)S(1)}, s32[2,2,2,256]{3,2,1,0:T(2,128)S(1)}, u32[]{:S(2)}, u32[]{:S(2)}) collective-permute-start(s32[2,2,2,256]{3,2,1,0:T(2,128)S(1)} %fusion.40), channel_id=1, source_target_pairs={{0,4},{4,8},{8,12},{12,0},{1,5},{5,9},{9,13},{13,1},{2,6},{6,10},{... | collective-permute-start | bytes 24584 | tf_op jit(solution)/shard_map/ppermute | solution.py:197
  22.2 11.0 %collective-permute-start.3 = (f32[65,1024]{1,0:T(8,128)S(1)}, f32[65,1024]{1,0:T(8,128)S(1)}, u32[]{:S(2)}, u32[]{:S(2)}) collective-permute-start(f32[65,1024]{1,0:T(8,128)S(1)} %get-tuple-element.39), channel_id=1, source_target_pairs={{0,1},{1,0},{2,3},{3,2},{4,5},{5,4},{6,7},{7,6},{8,9},{9,8},{10,11... | collective-permute-start | bytes 798728 | tf_op jit(solution)/shard_map/ppermute | solution.py:197
  32.8 11.1 %collective-permute-start.4 = (f32[65,1024]{1,0:T(8,128)S(1)}, f32[65,1024]{1,0:T(8,128)S(1)}, u32[]{:S(2)}, u32[]{:S(2)}) collective-permute-start(f32[65,1024]{1,0:T(8,128)S(1)} %get-tuple-element.41), channel_id=1, source_target_pairs={{0,1},{1,0},{2,3},{3,2},{4,5},{5,4},{6,7},{7,6},{8,9},{9,8},{10,11... | collective-permute-start | bytes 798728 | tf_op jit(solution)/shard_map/ppermute | solution.py:197
  43.9 12.1 %collective-permute-start.5 = (f32[65,1024]{1,0:T(8,128)S(1)}, f32[65,1024]{1,0:T(8,128)S(1)}, u32[]{:S(2)}, u32[]{:S(2)}) collective-permute-start(f32[65,1024]{1,0:T(8,128)S(1)} %add.297), channel_id=1, source_target_pairs={{0,2},{2,0},{1,3},{3,1},{4,6},{6,4},{5,7},{7,5},{8,10},{10,8},{9,1... | collective-permute-start | bytes 798728 | tf_op jit(solution)/shard_map/ppermute | solution.py:197
  56.1 7.0 %collective-permute-start.6 = (f32[65,256]{1,0:T(8,128)S(1)}, f32[65,256]{1,0:T(8,128)S(1)}, u32[]{:S(2)}, u32[]{:S(2)}) collective-permute-start(f32[65,256]{1,0:T(8,128)S(1)} %get-tuple-element.97), channel_id=1, source_target_pairs={{0,4},{4,8},{8,12},{12,0},{1,5},{5,9},{9,13},{13,1},{2,6},{6,10},{... | collective-permute-start | bytes 199688 | tf_op jit(solution)/shard_map/ppermute | solution.py:197
  56.8 8.3 %collective-permute-start.7 = (f32[65,256]{1,0:T(8,128)S(1)}, f32[65,256]{1,0:T(8,128)S(1)}, u32[]{:S(2)}, u32[]{:S(2)}) collective-permute-start(f32[65,256]{1,0:T(8,128)S(1)} %get-tuple-element.96), channel_id=1, source_target_pairs={{0,8},{4,12},{8,0},{12,4},{1,9},{5,13},{9,1},{13,5},{2,10},{6,14},... | collective-permute-start | bytes 199688 | tf_op jit(solution)/shard_map/ppermute | solution.py:197
  65.3 13.7 %collective-permute-start.10 = (bf16[65,256]{1,0:T(8,128)(2,1)S(1)}, bf16[65,256]{1,0:T(8,128)(2,1)S(1)}, u32[]{:S(2)}, u32[]{:S(2)}) collective-permute-start(bf16[65,256]{1,0:T(8,128)(2,1)S(1)} %pad_maximum_fusion.4), channel_id=1, source_target_pairs={{0,12},{4,0},{8,4},{12,8},{1,13},{5,1},{9,5},{13,9},{2,14},{6,2},{... | collective-permute-start | bytes 99848 | tf_op jit(solution)/shard_map/ppermute | solution.py:197
  67.8 11.2 %collective-permute-start.11 = (bf16[65,256]{1,0:T(8,128)(2,1)S(1)}, bf16[65,256]{1,0:T(8,128)(2,1)S(1)}, u32[]{:S(2)}, u32[]{:S(2)}) collective-permute-start(bf16[65,256]{1,0:T(8,128)(2,1)S(1)} %pad_maximum_fusion.4), channel_id=1, source_target_pairs={{0,8},{4,12},{8,0},{12,4},{1,9},{5,13},{9,1},{13,5},{2,10},{6,14},... | collective-permute-start | bytes 99848 | tf_op jit(solution)/shard_map/ppermute | solution.py:197
  68.3 10.7 %collective-permute-start.12 = (bf16[65,256]{1,0:T(8,128)(2,1)S(1)}, bf16[65,256]{1,0:T(8,128)(2,1)S(1)}, u32[]{:S(2)}, u32[]{:S(2)}) collective-permute-start(bf16[65,256]{1,0:T(8,128)(2,1)S(1)} %pad_maximum_fusion.4), channel_id=1, source_target_pairs={{0,4},{4,8},{8,12},{12,0},{1,5},{5,9},{9,13},{13,1},{2,6},{6,10},{... | collective-permute-start | bytes 99848 | tf_op jit(solution)/shard_map/ppermute | solution.py:197
  79.0 11.8 %collective-permute-start.9 = (f32[65,1024]{1,0:T(8,128)S(1)}, f32[65,1024]{1,0:T(8,128)S(1)}, u32[]{:S(2)}, u32[]{:S(2)}) collective-permute-start(f32[65,1024]{1,0:T(8,128)S(1)} %get-tuple-element.47), channel_id=1, source_target_pairs={{0,1},{1,0},{2,3},{3,2},{4,5},{5,4},{6,7},{7,6},{8,9},{9,8},{10,11... | collective-permute-start | bytes 798728 | tf_op jit(solution)/shard_map/ppermute | solution.py:197
  79.0 11.3 %collective-permute-start.18 = (bf16[65,1024]{1,0:T(8,128)(2,1)S(1)}, bf16[65,1024]{1,0:T(8,128)(2,1)S(1)}, u32[]{:S(2)}, u32[]{:S(2)}) collective-permute-start(bf16[65,1024]{1,0:T(8,128)(2,1)S(1)} %pad_maximum_fusion.2.refs_0_), channel_id=1, source_target_pairs={{0,2},{2,0},{1,3},{3,1},{4,6},{6,4},{5,7},{7,5},{8,10},{10,8},{9,1... | collective-permute-start | bytes 399368 | tf_op jit(solution)/shard_map/ppermute | solution.py:197
  90.2 12.8 %collective-permute-start.13 = (f32[65,1024]{1,0:T(8,128)S(1)}, f32[65,1024]{1,0:T(8,128)S(1)}, u32[]{:S(2)}, u32[]{:S(2)}) collective-permute-start(f32[65,1024]{1,0:T(8,128)S(1)} %get-tuple-element.49), channel_id=1, source_target_pairs={{0,1},{1,0},{2,3},{3,2},{4,5},{5,4},{6,7},{7,6},{8,9},{9,8},{10,11... | collective-permute-start | bytes 798728 | tf_op jit(solution)/shard_map/ppermute | solution.py:197
  90.4 27.6 %collective-permute-start.22 = (bf16[65,2048]{1,0:T(8,128)(2,1)S(1)}, bf16[65,2048]{1,0:T(8,128)(2,1)S(1)}, u32[]{:S(2)}, u32[]{:S(2)}) collective-permute-start(bf16[65,2048]{1,0:T(8,128)(2,1)S(1)} %pad_maximum_fusion), channel_id=1, source_target_pairs={{0,1},{1,0},{2,3},{3,2},{4,5},{5,4},{6,7},{7,6},{8,9},{9,8},{10,11... | collective-permute-start | bytes 798728 | tf_op jit(solution)/shard_map/ppermute | solution.py:197
  101.4 12.1 %collective-permute-start.14 = (f32[65,1024]{1,0:T(8,128)S(1)}, f32[65,1024]{1,0:T(8,128)S(1)}, u32[]{:S(2)}, u32[]{:S(2)}) collective-permute-start(f32[65,1024]{1,0:T(8,128)S(1)} %add.307), channel_id=1, source_target_pairs={{0,2},{2,0},{1,3},{3,1},{4,6},{6,4},{5,7},{7,5},{8,10},{10,8},{9,1... | collective-permute-start | bytes 798728 | tf_op jit(solution)/shard_map/ppermute | solution.py:197
  113.6 9.4 %collective-permute-start.17 = (f32[65,256]{1,0:T(8,128)S(1)}, f32[65,256]{1,0:T(8,128)S(1)}, u32[]{:S(2)}, u32[]{:S(2)}) collective-permute-start(f32[65,256]{1,0:T(8,128)S(1)} %get-tuple-element.93), channel_id=1, source_target_pairs={{0,12},{4,0},{8,4},{12,8},{1,13},{5,1},{9,5},{13,9},{2,14},{6,2},{... | collective-permute-start | bytes 199688 | tf_op jit(solution)/shard_map/ppermute | solution.py:197
  117.3 7.7 %collective-permute-start.16 = (f32[65,256]{1,0:T(8,128)S(1)}, f32[65,256]{1,0:T(8,128)S(1)}, u32[]{:S(2)}, u32[]{:S(2)}) collective-permute-start(f32[65,256]{1,0:T(8,128)S(1)} %get-tuple-element.94), channel_id=1, source_target_pairs={{0,8},{4,12},{8,0},{12,4},{1,9},{5,13},{9,1},{13,5},{2,10},{6,14},... | collective-permute-start | bytes 199688 | tf_op jit(solution)/shard_map/ppermute | solution.py:197
  118.0 7.0 %collective-permute-start.15 = (f32[65,256]{1,0:T(8,128)S(1)}, f32[65,256]{1,0:T(8,128)S(1)}, u32[]{:S(2)}, u32[]{:S(2)}) collective-permute-start(f32[65,256]{1,0:T(8,128)S(1)} %get-tuple-element.92), channel_id=1, source_target_pairs={{0,4},{4,8},{8,12},{12,0},{1,5},{5,9},{9,13},{13,1},{2,6},{6,10},{... | collective-permute-start | bytes 199688 | tf_op jit(solution)/shard_map/ppermute | solution.py:197
  125.1 9.2 %collective-permute-start.21 = (bf16[65,256]{1,0:T(8,128)(2,1)S(1)}, bf16[65,256]{1,0:T(8,128)(2,1)S(1)}, u32[]{:S(2)}, u32[]{:S(2)}) collective-permute-start(bf16[65,256]{1,0:T(8,128)(2,1)S(1)} %pad_maximum_fusion.5), channel_id=1, source_target_pairs={{0,4},{4,8},{8,12},{12,0},{1,5},{5,9},{9,13},{13,1},{2,6},{6,10},{... | collective-permute-start | bytes 99848 | tf_op jit(solution)/shard_map/ppermute | solution.py:197
  126.0 8.3 %collective-permute-start.20 = (bf16[65,256]{1,0:T(8,128)(2,1)S(1)}, bf16[65,256]{1,0:T(8,128)(2,1)S(1)}, u32[]{:S(2)}, u32[]{:S(2)}) collective-permute-start(bf16[65,256]{1,0:T(8,128)(2,1)S(1)} %pad_maximum_fusion.5), channel_id=1, source_target_pairs={{0,8},{4,12},{8,0},{12,4},{1,9},{5,13},{9,1},{13,5},{2,10},{6,14},... | collective-permute-start | bytes 99848 | tf_op jit(solution)/shard_map/ppermute | solution.py:197
  149.4 14.6 %collective-permute-start.25 = (bf16[64,2048]{1,0:T(8,128)(2,1)S(1)}, bf16[64,2048]{1,0:T(8,128)(2,1)S(1)}, u32[]{:S(2)}, u32[]{:S(2)}) collective-permute-start(bf16[64,2048]{1,0:T(8,128)(2,1)S(1)} %convert_element_type.77.refs_0_), channel_id=1, source_target_pairs={{0,12},{4,0},{8,4},{12,8},{1,13},{5,1},{9,5},{13,9},{2,14},{6,2},{... | collective-permute-start | bytes 786440 | tf_op jit(solution)/shard_map/ppermute | solution.py:197
  150.4 24.0 %collective-permute-start.27 = (bf16[64,2048]{1,0:T(8,128)(2,1)S(1)}, bf16[64,2048]{1,0:T(8,128)(2,1)S(1)}, u32[]{:S(2)}, u32[]{:S(2)}) collective-permute-start(bf16[64,2048]{1,0:T(8,128)(2,1)S(1)} %convert_element_type.77.refs_0_), channel_id=1, source_target_pairs={{0,4},{4,8},{8,12},{12,0},{1,5},{5,9},{9,13},{13,1},{2,6},{6,10},{... | collective-permute-start | bytes 786440 | tf_op jit(solution)/shard_map/ppermute | solution.py:197
  151.4 27.0 %collective-permute-start.29 = (bf16[64,2048]{1,0:T(8,128)(2,1)S(1)}, bf16[64,2048]{1,0:T(8,128)(2,1)S(1)}, u32[]{:S(2)}, u32[]{:S(2)}) collective-permute-start(bf16[64,2048]{1,0:T(8,128)(2,1)S(1)} %convert_element_type.77.refs_0_), channel_id=1, source_target_pairs={{0,8},{4,12},{8,0},{12,4},{1,9},{5,13},{9,1},{13,5},{2,10},{6,14},... | collective-permute-start | bytes 786440 | tf_op jit(solution)/shard_map/ppermute | solution.py:197
  187.4 12.5 %collective-permute-start.34 = (bf16[64,2048]{1,0:T(8,128)(2,1)S(1)}, bf16[64,2048]{1,0:T(8,128)(2,1)S(1)}, u32[]{:S(2)}, u32[]{:S(2)}) collective-permute-start(bf16[64,2048]{1,0:T(8,128)(2,1)S(1)} %get-tuple-element.75.refs_0_), channel_id=1, source_target_pairs={{0,4},{4,8},{8,12},{12,0},{1,5},{5,9},{9,13},{13,1},{2,6},{6,10},{... | collective-permute-start | bytes 786440 | tf_op jit(solution)/shard_map/ppermute | solution.py:197
  187.5 21.8 %collective-permute-start.38 = (bf16[64,2048]{1,0:T(8,128)(2,1)S(1)}, bf16[64,2048]{1,0:T(8,128)(2,1)S(1)}, u32[]{:S(2)}, u32[]{:S(2)}) collective-permute-start(bf16[64,2048]{1,0:T(8,128)(2,1)S(1)} %get-tuple-element.75.refs_0_), channel_id=1, source_target_pairs={{0,8},{4,12},{8,0},{12,4},{1,9},{5,13},{9,1},{13,5},{2,10},{6,14},... | collective-permute-start | bytes 786440 | tf_op jit(solution)/shard_map/ppermute | solution.py:197
  (18 other events, 247.3 us)

commit v4 on v3

--- a/solution.py
+++ b/solution.py
@@ -15,6 +15,7 @@
 LAM = 0.05
 SCALE = 1.0 / 1024.0
 LANES = 128
+LEVEL = jnp.float8_e4m3fn
 
 
 def window_table(length):
@@ -33,8 +34,12 @@
     return (high * 256 + seeds * (SHIFT % 256) + first) % PRIME
 
 
-def table_body(start_ref, tab_ref, a_ref, feat_ref, data_ref, marg_ref, scr, *, unroll, pitch):
-    nrow, nfeat = data_ref.shape
+def whole_vmem():
+    return pl.BlockSpec(memory_space=pltpu.VMEM)
+
+
+def table_body(start_ref, tab_ref, a_ref, feat_ref, data_ref, marg_ref, scr, wide, *, unroll, pitch):
+    nrow, nfeat = wide.shape
     nsub = nfeat // LANES
     high = min(8, nsub)
     lane = lax.broadcasted_iota(jnp.int32, (high, LANES), 1)
@@ -59,9 +64,12 @@
 
     lax.fori_loop(0, nrow // unroll, samples, 0)
     for r in range(nsub):
-        data_ref[:, r * LANES : (r + 1) * LANES] = scr[pl.ds(r * pitch, nrow), :].astype(jnp.bfloat16)
+        cut = slice(r * LANES, (r + 1) * LANES)
+        level = scr[pl.ds(r * pitch, nrow), :]
+        wide[:, cut] = level.astype(jnp.bfloat16)
+        data_ref[pl.ds(pl.multiple_of(base, nrow), nrow), cut] = level.astype(LEVEL)
     marg = lax.dot_general(
-        data_ref[...], feat_ref[...], (((1,), (1,)), ((), ())), preferred_element_type=jnp.float32
+        wide[...], feat_ref[...], (((1,), (1,)), ((), ())), preferred_element_type=jnp.float32
     )
     marg_ref[...] = SCALE * marg.T[: marg_ref.shape[0]]
 
@@ -83,16 +91,19 @@
                 pl.BlockSpec(feats.shape, lambda i, s: (0, 0)),
             ],
             out_specs=[
-                pl.BlockSpec((nrow, nfeat), lambda i, s: (i, 0)),
+                whole_vmem(),
                 pl.BlockSpec((ncol, nrow), lambda i, s: (0, i)),
             ],
-            scratch_shapes=[pltpu.VMEM((nsub * pitch, LANES), jnp.float32)],
+            scratch_shapes=[
+                pltpu.VMEM((nsub * pitch, LANES), jnp.float32),
+                pltpu.VMEM((nrow, nfeat), jnp.bfloat16),
+            ],
         ),
         out_shape=[
-            jax.ShapeDtypeStruct((count, nfeat), jnp.bfloat16),
+            pltpu.VMEM((count, nfeat), LEVEL),
             jax.ShapeDtypeStruct((ncol, count), jnp.float32),
         ],
-        compiler_params=pltpu.CompilerParams(vmem_limit_bytes=48 << 20),
+        compiler_params=pltpu.CompilerParams(vmem_limit_bytes=12 << 20),
         cost_estimate=pl.CostEstimate(
             flops=count * nfeat * 1500, bytes_accessed=count * nfeat * 2, transcendentals=0
         ),
@@ -100,32 +111,29 @@
     )(starts, tab, part, feats)
 
 
-def back_body(*refs, nblk):
+def back_body(*refs, nblk, tile, half):
     mixes, datas, (old_ref, out_ref) = refs[:nblk], refs[nblk : 2 * nblk], refs[2 * nblk :]
-    total = old_ref[...]
-    for mix_ref, data_ref in zip(mixes, datas):
-        total += jnp.dot(mix_ref[...], data_ref[...], preferred_element_type=jnp.float32)
-    out_ref[...] = total
+    width = out_ref.shape[1]
+    for at in range(0, width, tile):
+        total = old_ref[:, at : at + tile]
+        for mix_ref, data_ref in zip(mixes, datas):
+            level = data_ref[:, half * width + at : half * width + at + tile].astype(jnp.bfloat16)
+            total += jnp.dot(mix_ref[...], level, preferred_element_type=jnp.float32)
+        out_ref[:, at : at + tile] = total
 
 
 def back(mixes, datas, old, half):
     nblk = len(mixes)
     ncol, count = mixes[0].shape
     width = old.shape[1]
-    tile = min(512, width)
-    steps = width // tile
-    at = half * steps
     return pl.pallas_call(
-        functools.partial(back_body, nblk=nblk),
-        grid=(steps,),
-        in_specs=[pl.BlockSpec((ncol, count), lambda f: (0, 0))] * nblk
-        + [pl.BlockSpec((count, tile), lambda f: (0, at + f))] * nblk
-        + [pl.BlockSpec((ncol, tile), lambda f: (0, f))],
-        out_specs=pl.BlockSpec((ncol, tile), lambda f: (0, f)),
+        functools.partial(back_body, nblk=nblk, tile=min(512, width), half=half),
+        in_specs=[whole_vmem()] * (2 * nblk + 1),
+        out_specs=whole_vmem(),
         out_shape=jax.ShapeDtypeStruct((ncol, width), jnp.float32),
-        compiler_params=pltpu.CompilerParams(vmem_limit_bytes=48 << 20),
+        compiler_params=pltpu.CompilerParams(vmem_limit_bytes=12 << 20),
         cost_estimate=pl.CostEstimate(
-            flops=2 * count * width * ncol * nblk, bytes_accessed=count * width * 2 * nblk, transcendentals=0
+            flops=2 * count * width * ncol * nblk, bytes_accessed=count * width * nblk, transcendentals=0
         ),
         name="back",
     )(*mixes, *datas, old)
@@ -160,7 +168,7 @@
     return pl.pallas_call(
         solve_body,
         out_shape=jax.ShapeDtypeStruct(grad.shape, jnp.float32),
-        compiler_params=pltpu.CompilerParams(vmem_limit_bytes=32 << 20),
+        compiler_params=pltpu.CompilerParams(vmem_limit_bytes=8 << 20),
         name="solve",
     )(prods, grad, *halves)
 
@@ -188,7 +196,7 @@
         ),
         out_shape=jax.ShapeDtypeStruct((rank, width * nhalf * size), jnp.float32),
         input_output_aliases={1 + size: 0} if extra else {},
-        compiler_params=pltpu.CompilerParams(vmem_limit_bytes=32 << 20),
+        compiler_params=pltpu.CompilerParams(vmem_limit_bytes=8 << 20),
         name="place",
     )(z.reshape(1), *parts, *extra)
 
@@ -300,17 +308,17 @@
             return come or [held]
         if at == 1:
             held, come = stage[c]
-            held = after(weigh(sum(come, held), labels[c]), *deps)
-            stage[c] = collect_rows(held, nrows)
+            held = after(held, *deps)
+            come = [after(x, *deps) for x in come]
+            stage[c] = collect_rows(weigh(sum(come, held), labels[c]), nrows)
             return stage[c]
         if at == 2:
-            mixed[c, 0, 0] = after(jnp.concatenate(stage[c], axis=1), *deps)
+            mixed[c, 0, 0] = jnp.concatenate([after(x, *deps) for x in stage[c]], axis=1)
             for ds in range(1, nsec):
                 mixed[c, 0, ds] = shift(mixed[c, 0, 0], "sec", nsec, -ds)
             return [mixed[c, 0, ds] for ds in range(1, nsec)]
         if at == 3:
-            half = jnp.concatenate([mixed[c, 0, ds] for ds in range(nsec)], axis=1)
-            half = after(half, *deps)
+            half = jnp.concatenate([after(mixed[c, 0, ds], *deps) for ds in range(nsec)], axis=1)
             for du in range(1, nsub):
                 come = shift(half, "sub", nsub, -du)
                 for ds in range(nsec):
@@ -334,7 +342,7 @@
         begin = after(starts[c, ds, du].reshape(-1), *last, *older)
         data[c, du, ds], marg[c, du, ds] = make_table(begin, tab, part, padded, ncol)
         last = [marg[c, du, ds]]
-        older, due = due, boundary()
+        older, due = due, boundary(*last)
         if du:
             from_sub[c, du, ds] = shift(marg[c, du, ds], "sub", nsub, du)
             due.append(from_sub[c, du, ds])
@@ -389,8 +397,10 @@
     c, dus, half = plan[-1]
     older = [totals[0]]
     product(c, dus, half)
-    older = [wide[0][1]] if direct else []
-    product(nchunk - 1, range(nsub), 1)
+    older = []
+    for du in range(nsub):
+        product(nchunk - 1, [du], 1)
+        older = [wide[0][1]] if direct else []
     close(1)
     if direct:
         send(1, [1])
@@ -399,6 +409,8 @@
         lax.dot_general(left, part, (((1,), (1,)), ((), ())), precision=lax.Precision.HIGHEST)
         for left, part in zip(lefts, parts)
     )
+    if direct:
+        prods = after(prods, wide[0][1])
     prods = all_sum(prods, "sub", nsub)
     if direct:
         prods = after(prods, wide[0][nrows - 1])

time: 212 us -> 192 us (0.906)
  Pallas kernels: 133 us -> 103 us
  waiting for transfers between devices: 24.6 us -> 34.2 us
    pallas_call x6 -> x7, Pallas kernels: 34.9 us -> 12.5 us  [back(): pl.pallas_call(functools.partial(back_body, nblk=nblk, tile=min(512, widt...]
    ppermute x39, waiting for transfers between devices: 24.6 us -> 34.2 us  [shift(): return lax.ppermute(x, axis, [(i, (i + by) % size) for i in range(size)])]
    pallas_call x8, Pallas kernels: 84.5 us -> 77.6 us  [make_table(): pl.pallas_call(functools.partial(table_body, unroll=64, pitch=pitch), gri...]
  transfers between devices with their start and end apart: 39 -> 39, of which waited for: 12 -> 15; matrix products, arithmetic and copies ran while one was open for 3% -> 3% of each run, Pallas kernels for 53% -> 41%
where the time goes in v4:
time: 192 us; the launch traced here: 191 us
  Pallas kernels  103 us (54%)
  starting transfers between devices  44.9 us (23%)
  waiting for transfers between devices  34.2 us (18%)
  other arithmetic  3.92 us (2%)
  local copies, waits for them, and re-layouts  2.33 us (1%)
    pallas_call x8, Pallas kernels, make_table(): pl.pallas_call(functools.partial(table_body, unroll=64, pitch=pitch), gri...  77.6 us
    ppermute x39, starting transfers between devices, shift(): return lax.ppermute(x, axis, [(i, (i + by) % size) for i in range(size)])  44.9 us
    ppermute x39, waiting for transfers between devices, shift(): return lax.ppermute(x, axis, [(i, (i + by) % size) for i in range(size)])  34.2 us
    pallas_call x7, Pallas kernels, back(): pl.pallas_call(functools.partial(back_body, nblk=nblk, tile=min(512, widt...  12.5 us
    pallas_call x1, Pallas kernels, solve(): pl.pallas_call(solve_body, out_shape=jax.ShapeDtypeStruct(grad.shape, jnp...  9.57 us
  transfers between devices with their start and end apart: 39, of which 15 were waited for; matrix products, arithmetic and copies ran while one was open for 3% of the time, Pallas kernels for 41%

profile of v4, /device:TPU:0, one launch (start us, length us, event | category | flops | bytes accessed | tf_op | source)
XLA Modules:
  0.0 191.2 jit_solution(6756402982674087668)
XLA Ops:
  1.4 3.1 %collective-permute-start.2 = (s32[2,2,2,256]{3,2,1,0:T(2,128)S(1)}, s32[2,2,2,256]{3,2,1,0:T(2,128)S(1)}, u32[]{:S(2)}, u32[]{:S(2)}) collective-permute-start(s32[2,2,2,256]{3,2,1,0:T(2,128)S(1)} %fusion.36), channel_id=1, source_target_pairs={{0,4},{4,8},{8,12},{12,0},{1,5},{5,9},{9,13},{13,1},{2,6},{6,10},{... | collective-permute-start | bytes 24584 | tf_op jit(solution)/shard_map/ppermute | solution.py:205
  4.5 2.6 %collective-permute-start.1 = (s32[2,2,2,256]{3,2,1,0:T(2,128)S(1)}, s32[2,2,2,256]{3,2,1,0:T(2,128)S(1)}, u32[]{:S(2)}, u32[]{:S(2)}) collective-permute-start(s32[2,2,2,256]{3,2,1,0:T(2,128)S(1)} %fusion.36), channel_id=1, source_target_pairs={{0,8},{4,12},{8,0},{12,4},{1,9},{5,13},{9,1},{13,5},{2,10},{6,14},... | collective-permute-start | bytes 24584 | tf_op jit(solution)/shard_map/ppermute | solution.py:205
  12.3 9.7 %make_table.8 = (f8e4m3fn[1024,4096]{1,0:T(32,128)(4,1)S(1)}, f32[65,1024]{1,0:T(8,128)S(1)}) custom-call(s32[1024]{0:T(1024)S(1)} %bitcast.55, f32[552,128]{1,0:T(8,128)S(1)} %fusion.21.tab_ref, f32[32,128]{1,0:T(8,128)S(1)} %fusion.32.a_ref, bf16[128,4096]{1,0:T(8,128)(2,1)S(1)} %fusion.2.feat_ref), custom_call_target="tpu_custom_call" | custom-call | flops 6291456000 | bytes 8388608 | tf_op jit(solution)/shard_map/make_table/pallas_call | solution.py:83
  22.1 9.7 %make_table.9 = (f8e4m3fn[1024,4096]{1,0:T(32,128)(4,1)S(1)}, f32[65,1024]{1,0:T(8,128)S(1)}) custom-call(s32[1024]{0:T(1024)S(1)} %bitcast.54, f32[552,128]{1,0:T(8,128)S(1)} %fusion.21.tab_ref, f32[32,128]{1,0:T(8,128)S(1)} %fusion.32.a_ref, bf16[128,4096]{1,0:T(8,128)(2,1)S(1)} %fusion.2.feat_ref), custom_call_target="tpu_custom_call" | custom-call | flops 6291456000 | bytes 8388608 | tf_op jit(solution)/shard_map/make_table/pallas_call | solution.py:83
  32.4 9.7 %make_table.10 = (f8e4m3fn[1024,4096]{1,0:T(32,128)(4,1)S(1)}, f32[65,1024]{1,0:T(8,128)S(1)}) custom-call(s32[1024]{0:T(1024)S(1)} %bitcast.53, f32[552,128]{1,0:T(8,128)S(1)} %fusion.21.tab_ref, f32[32,128]{1,0:T(8,128)S(1)} %fusion.32.a_ref, bf16[128,4096]{1,0:T(8,128)(2,1)S(1)} %fusion.2.feat_ref), custom_call_target="tpu_custom_call" | custom-call | flops 6291456000 | bytes 8388608 | tf_op jit(solution)/shard_map/make_table/pallas_call | solution.py:83
  43.7 9.7 %make_table.11 = (f8e4m3fn[1024,4096]{1,0:T(32,128)(4,1)S(1)}, f32[65,1024]{1,0:T(8,128)S(1)}) custom-call(s32[1024]{0:T(1024)S(1)} %bitcast.52, f32[552,128]{1,0:T(8,128)S(1)} %fusion.21.tab_ref, f32[32,128]{1,0:T(8,128)S(1)} %fusion.32.a_ref, bf16[128,4096]{1,0:T(8,128)(2,1)S(1)} %fusion.2.feat_ref), custom_call_target="tpu_custom_call" | custom-call | flops 6291456000 | bytes 8388608 | tf_op jit(solution)/shard_map/make_table/pallas_call | solution.py:83
  53.5 9.7 %make_table.12 = (f8e4m3fn[1024,4096]{1,0:T(32,128)(4,1)S(1)}, f32[65,1024]{1,0:T(8,128)S(1)}) custom-call(s32[1024]{0:T(1024)S(1)} %bitcast.51, f32[552,128]{1,0:T(8,128)S(1)} %fusion.21.tab_ref, f32[32,128]{1,0:T(8,128)S(1)} %fusion.32.a_ref, bf16[128,4096]{1,0:T(8,128)(2,1)S(1)} %fusion.2.feat_ref), custom_call_target="tpu_custom_call" | custom-call | flops 6291456000 | bytes 8388608 | tf_op jit(solution)/shard_map/make_table/pallas_call | solution.py:83
  67.2 9.7 %make_table.13 = (f8e4m3fn[1024,4096]{1,0:T(32,128)(4,1)S(1)}, f32[65,1024]{1,0:T(8,128)S(1)}) custom-call(s32[1024]{0:T(1024)S(1)} %bitcast.50, f32[552,128]{1,0:T(8,128)S(1)} %fusion.21.tab_ref, f32[32,128]{1,0:T(8,128)S(1)} %fusion.32.a_ref, bf16[128,4096]{1,0:T(8,128)(2,1)S(1)} %fusion.2.feat_ref), custom_call_target="tpu_custom_call" | custom-call | flops 6291456000 | bytes 8388608 | tf_op jit(solution)/shard_map/make_table/pallas_call | solution.py:83
  79.3 1.9 %collective-permute-start.12 = (bf16[65,256]{1,0:T(8,128)(2,1)S(1)}, bf16[65,256]{1,0:T(8,128)(2,1)S(1)}, u32[]{:S(2)}, u32[]{:S(2)}) collective-permute-start(bf16[65,256]{1,0:T(8,128)(2,1)S(1)} %pad_maximum_fusion.2), channel_id=1, source_target_pairs={{0,4},{4,8},{8,12},{12,0},{1,5},{5,9},{9,13},{13,1},{2,6},{6,10},{... | collective-permute-start | bytes 99848 | tf_op jit(solution)/shard_map/ppermute | solution.py:205
  81.2 9.7 %make_table.14 = (f8e4m3fn[1024,4096]{1,0:T(32,128)(4,1)S(1)}, f32[65,1024]{1,0:T(8,128)S(1)}) custom-call(s32[1024]{0:T(1024)S(1)} %bitcast.49, f32[552,128]{1,0:T(8,128)S(1)} %fusion.21.tab_ref, f32[32,128]{1,0:T(8,128)S(1)} %fusion.32.a_ref, bf16[128,4096]{1,0:T(8,128)(2,1)S(1)} %fusion.2.feat_ref), custom_call_target="tpu_custom_call" | custom-call | flops 6291456000 | bytes 8388608 | tf_op jit(solution)/shard_map/make_table/pallas_call | solution.py:83
  93.2 9.7 %make_table.15 = (f8e4m3fn[1024,4096]{1,0:T(32,128)(4,1)S(1)}, f32[65,1024]{1,0:T(8,128)S(1)}) custom-call(s32[1024]{0:T(1024)S(1)} %bitcast.48, f32[552,128]{1,0:T(8,128)S(1)} %fusion.21.tab_ref, f32[32,128]{1,0:T(8,128)S(1)} %fusion.32.a_ref, bf16[128,4096]{1,0:T(8,128)(2,1)S(1)} %fusion.2.feat_ref), custom_call_target="tpu_custom_call" | custom-call | flops 6291456000 | bytes 8388608 | tf_op jit(solution)/shard_map/make_table/pallas_call | solution.py:83
  103.0 2.0 %collective-permute-start.18 = (f32[65,256]{1,0:T(8,128)S(1)}, f32[65,256]{1,0:T(8,128)S(1)}, u32[]{:S(2)}, u32[]{:S(2)}) collective-permute-start(f32[65,256]{1,0:T(8,128)S(1)} %get-tuple-element.129), channel_id=1, source_target_pairs={{0,12},{4,0},{8,4},{12,8},{1,13},{5,1},{9,5},{13,9},{2,14},{6,2},{... | collective-permute-start | bytes 199688 | tf_op jit(solution)/shard_map/ppermute | solution.py:205
  107.8 4.5 %collective-permute-done.17 = f32[65,256]{1,0:T(8,128)S(1)} collective-permute-done((f32[65,256]{1,0:T(8,128)S(1)}, f32[65,256]{1,0:T(8,128)S(1)}, u32[]{:S(2)}, u32[]{:S(2)}) %collective-permute-start.17) | collective-permute-done | bytes 66592 | tf_op jit(solution)/shard_map/ppermute | solution.py:205
  113.6 1.9 %collective-permute-start.22 = (bf16[65,256]{1,0:T(8,128)(2,1)S(1)}, bf16[65,256]{1,0:T(8,128)(2,1)S(1)}, u32[]{:S(2)}, u32[]{:S(2)}) collective-permute-start(bf16[65,256]{1,0:T(8,128)(2,1)S(1)} %pad_maximum_fusion.3), channel_id=1, source_target_pairs={{0,4},{4,8},{8,12},{12,0},{1,5},{5,9},{9,13},{13,1},{2,6},{6,10},{... | collective-permute-start | bytes 99848 | tf_op jit(solution)/shard_map/ppermute | solution.py:205
  121.5 3.0 %collective-permute-done.23.refs_1_ = bf16[65,1024]{1,0:T(8,128)(2,1)S(1)} collective-permute-done((bf16[65,1024]{1,0:T(8,128)(2,1)S(1)}, bf16[65,1024]{1,0:T(8,128)(2,1)S(1)}, u32[]{:S(2)}, u32[]{:S(2)}) %collective-permute-start.23) | collective-permute-done | bytes 133152 | tf_op jit(solution)/shard_map/ppermute | solution.py:205
  126.3 3.0 %back.10 = f32[65,2048]{1,0:T(8,128)S(1)} custom-call(bf16[65,1024]{1,0:T(8,128)(2,1)S(1)} %constant_dynamic-update-slice_fusion.4.refs_0_, bf16[65,1024]{1,0:T(8,128)(2,1)S(1)} %collective-permute-done.23.refs_1_, bf16[65,1024]{1,0:T(8,128)(2,1)S(1)} %get-tuple-element.104.refs_2_.refs_0_, bf16[65,1024]{1,0:T(8,128)(2,1)S(1)} %get-tuple-element.124.refs_3_.refs_1_, ...), custom_call_target="tpu_custom_call" | custom-call | flops 1090519040 | bytes 8388608 | tf_op jit(solution)/shard_map/back/pallas_call | solution.py:129
  135.9 9.0 %collective-permute-done.25.refs_1_ = bf16[64,2048]{1,0:T(8,128)(2,1)S(1)} collective-permute-done((bf16[64,2048]{1,0:T(8,128)(2,1)S(1)}, bf16[64,2048]{1,0:T(8,128)(2,1)S(1)}, u32[]{:S(2)}, u32[]{:S(2)}) %collective-permute-start.25) | collective-permute-done | bytes 262176 | tf_op jit(solution)/shard_map/ppermute | solution.py:205
  149.9 3.4 %collective-permute-done.28 = f32[65,64]{1,0:T(8,128)S(1)} collective-permute-done((f32[65,64]{1,0:T(8,128)S(1)}, f32[65,64]{1,0:T(8,128)S(1)}, u32[]{:S(2)}, u32[]{:S(2)}) %collective-permute-start.28) | collective-permute-done | bytes 16672 | tf_op jit(solution)/shard_map/ppermute | solution.py:205
  153.3 1.9 collective-permute-done.29.refs_2_
  157.0 2.8 %collective-permute-start.33 = (f32[65,64]{1,0:T(8,128)S(1)}, f32[65,64]{1,0:T(8,128)S(1)}, u32[]{:S(2)}, u32[]{:S(2)}) collective-permute-start(f32[65,64]{1,0:T(8,128)S(1)} %add.321), channel_id=1, source_target_pairs={{0,8},{4,12},{8,0},{12,4},{1,9},{5,13},{9,1},{13,5},{2,10},{6,14},... | collective-permute-start | bytes 49928 | tf_op jit(solution)/shard_map/ppermute | solution.py:205
  159.8 3.5 %collective-permute-start.32 = (f32[65,64]{1,0:T(8,128)S(1)}, f32[65,64]{1,0:T(8,128)S(1)}, u32[]{:S(2)}, u32[]{:S(2)}) collective-permute-start(f32[65,64]{1,0:T(8,128)S(1)} %add.321), channel_id=1, source_target_pairs={{0,4},{4,8},{8,12},{12,0},{1,5},{5,9},{9,13},{13,1},{2,6},{6,10},{... | collective-permute-start | bytes 49928 | tf_op jit(solution)/shard_map/ppermute | solution.py:205
  167.6 2.9 %collective-permute-start.38 = (bf16[64,2048]{1,0:T(8,128)(2,1)S(1)}, bf16[64,2048]{1,0:T(8,128)(2,1)S(1)}, u32[]{:S(2)}, u32[]{:S(2)}) collective-permute-start(bf16[64,2048]{1,0:T(8,128)(2,1)S(1)} %get-tuple-element.111.refs_0_), channel_id=1, source_target_pairs={{0,8},{4,12},{8,0},{12,4},{1,9},{5,13},{9,1},{13,5},{2,10},{6,14},... | collective-permute-start | bytes 786440 | tf_op jit(solution)/shard_map/ppermute | solution.py:205
  170.5 9.6 %solve.1 = f32[1,4096]{1,0:T(1,128)S(1)} custom-call(f32[65,64]{1,0:T(8,128)S(1)} %add_add_fusion.4.prod_ref, f32[1,4096]{1,0:T(1,128)S(1)} %pad_maximum_fusion.4.grad_ref, f32[64,2048]{1,0:T(8,128)S(1)} %get-tuple-element.115.refs_0_, f32[64,2048]{1,0:T(8,128)S(1)} %get-tuple-element.113.refs_1_), custom_call_target="tpu_custom_call" | custom-call | tf_op jit(solution)/shard_map/solve/pallas_call | solution.py:168
  181.1 2.0 %collective-permute-start.36 = (f32[1,4096]{1,0:T(1,128)S(1)}, f32[1,4096]{1,0:T(1,128)S(1)}, u32[]{:S(2)}, u32[]{:S(2)}) collective-permute-start(f32[1,4096]{1,0:T(1,128)S(1)} %solve.1), channel_id=1, source_target_pairs={{0,8},{4,12},{8,0},{12,4},{1,9},{5,13},{9,1},{13,5},{2,10},{6,14},... | collective-permute-start | bytes 49160 | tf_op jit(solution)/shard_map/ppermute | solution.py:205
  (141 shorter events, 55.1 us)
Async XLA Ops:
  1.4 10.7 %collective-permute-start.2 = (s32[2,2,2,256]{3,2,1,0:T(2,128)S(1)}, s32[2,2,2,256]{3,2,1,0:T(2,128)S(1)}, u32[]{:S(2)}, u32[]{:S(2)}) collective-permute-start(s32[2,2,2,256]{3,2,1,0:T(2,128)S(1)} %fusion.36), channel_id=1, source_target_pairs={{0,4},{4,8},{8,12},{12,0},{1,5},{5,9},{9,13},{13,1},{2,6},{6,10},{... | collective-permute-start | bytes 24584 | tf_op jit(solution)/shard_map/ppermute | solution.py:205
  4.5 7.7 %collective-permute-start.1 = (s32[2,2,2,256]{3,2,1,0:T(2,128)S(1)}, s32[2,2,2,256]{3,2,1,0:T(2,128)S(1)}, u32[]{:S(2)}, u32[]{:S(2)}) collective-permute-start(s32[2,2,2,256]{3,2,1,0:T(2,128)S(1)} %fusion.36), channel_id=1, source_target_pairs={{0,8},{4,12},{8,0},{12,4},{1,9},{5,13},{9,1},{13,5},{2,10},{6,14},... | collective-permute-start | bytes 24584 | tf_op jit(solution)/shard_map/ppermute | solution.py:205
  22.0 10.4 %collective-permute-start.3 = (f32[65,1024]{1,0:T(8,128)S(1)}, f32[65,1024]{1,0:T(8,128)S(1)}, u32[]{:S(2)}, u32[]{:S(2)}) collective-permute-start(f32[65,1024]{1,0:T(8,128)S(1)} %get-tuple-element.57), channel_id=1, source_target_pairs={{0,1},{1,0},{2,3},{3,2},{4,5},{5,4},{6,7},{7,6},{8,9},{9,8},{10,11... | collective-permute-start | bytes 798728 | tf_op jit(solution)/shard_map/ppermute | solution.py:205
  31.8 10.3 %collective-permute-start.4 = (f32[65,1024]{1,0:T(8,128)S(1)}, f32[65,1024]{1,0:T(8,128)S(1)}, u32[]{:S(2)}, u32[]{:S(2)}) collective-permute-start(f32[65,1024]{1,0:T(8,128)S(1)} %get-tuple-element.59), channel_id=1, source_target_pairs={{0,1},{1,0},{2,3},{3,2},{4,5},{5,4},{6,7},{7,6},{8,9},{9,8},{10,11... | collective-permute-start | bytes 798728 | tf_op jit(solution)/shard_map/ppermute | solution.py:205
  42.2 11.3 %collective-permute-start.5 = (f32[65,1024]{1,0:T(8,128)S(1)}, f32[65,1024]{1,0:T(8,128)S(1)}, u32[]{:S(2)}, u32[]{:S(2)}) collective-permute-start(f32[65,1024]{1,0:T(8,128)S(1)} %add.297), channel_id=1, source_target_pairs={{0,2},{2,0},{1,3},{3,1},{4,6},{6,4},{5,7},{7,5},{8,10},{10,8},{9,1... | collective-permute-start | bytes 798728 | tf_op jit(solution)/shard_map/ppermute | solution.py:205
  63.2 18.1 %collective-permute-start.9 = (f32[65,1024]{1,0:T(8,128)S(1)}, f32[65,1024]{1,0:T(8,128)S(1)}, u32[]{:S(2)}, u32[]{:S(2)}) collective-permute-start(f32[65,1024]{1,0:T(8,128)S(1)} %get-tuple-element.65), channel_id=1, source_target_pairs={{0,1},{1,0},{2,3},{3,2},{4,5},{5,4},{6,7},{7,6},{8,9},{9,8},{10,11... | collective-permute-start | bytes 798728 | tf_op jit(solution)/shard_map/ppermute | solution.py:205
  63.3 13.7 %collective-permute-start.6 = (f32[65,256]{1,0:T(8,128)S(1)}, f32[65,256]{1,0:T(8,128)S(1)}, u32[]{:S(2)}, u32[]{:S(2)}) collective-permute-start(f32[65,256]{1,0:T(8,128)S(1)} %get-tuple-element.135), channel_id=1, source_target_pairs={{0,4},{4,8},{8,12},{12,0},{1,5},{5,9},{9,13},{13,1},{2,6},{6,10},{... | collective-permute-start | bytes 199688 | tf_op jit(solution)/shard_map/ppermute | solution.py:205
  64.1 12.9 %collective-permute-start.7 = (f32[65,256]{1,0:T(8,128)S(1)}, f32[65,256]{1,0:T(8,128)S(1)}, u32[]{:S(2)}, u32[]{:S(2)}) collective-permute-start(f32[65,256]{1,0:T(8,128)S(1)} %get-tuple-element.134), channel_id=1, source_target_pairs={{0,8},{4,12},{8,0},{12,4},{1,9},{5,13},{9,1},{13,5},{2,10},{6,14},... | collective-permute-start | bytes 199688 | tf_op jit(solution)/shard_map/ppermute | solution.py:205
  65.7 11.3 %collective-permute-start.8 = (f32[65,256]{1,0:T(8,128)S(1)}, f32[65,256]{1,0:T(8,128)S(1)}, u32[]{:S(2)}, u32[]{:S(2)}) collective-permute-start(f32[65,256]{1,0:T(8,128)S(1)} %get-tuple-element.133), channel_id=1, source_target_pairs={{0,12},{4,0},{8,4},{12,8},{1,13},{5,1},{9,5},{13,9},{2,14},{6,2},{... | collective-permute-start | bytes 199688 | tf_op jit(solution)/shard_map/ppermute | solution.py:205
  76.9 14.7 %collective-permute-start.13 = (f32[65,1024]{1,0:T(8,128)S(1)}, f32[65,1024]{1,0:T(8,128)S(1)}, u32[]{:S(2)}, u32[]{:S(2)}) collective-permute-start(f32[65,1024]{1,0:T(8,128)S(1)} %get-tuple-element.67), channel_id=1, source_target_pairs={{0,1},{1,0},{2,3},{3,2},{4,5},{5,4},{6,7},{7,6},{8,9},{9,8},{10,11... | collective-permute-start | bytes 798728 | tf_op jit(solution)/shard_map/ppermute | solution.py:205
  77.1 14.4 %collective-permute-start.10 = (bf16[65,256]{1,0:T(8,128)(2,1)S(1)}, bf16[65,256]{1,0:T(8,128)(2,1)S(1)}, u32[]{:S(2)}, u32[]{:S(2)}) collective-permute-start(bf16[65,256]{1,0:T(8,128)(2,1)S(1)} %pad_maximum_fusion.2), channel_id=1, source_target_pairs={{0,12},{4,0},{8,4},{12,8},{1,13},{5,1},{9,5},{13,9},{2,14},{6,2},{... | collective-permute-start | bytes 99848 | tf_op jit(solution)/shard_map/ppermute | solution.py:205
  78.4 13.2 %collective-permute-start.11 = (bf16[65,256]{1,0:T(8,128)(2,1)S(1)}, bf16[65,256]{1,0:T(8,128)(2,1)S(1)}, u32[]{:S(2)}, u32[]{:S(2)}) collective-permute-start(bf16[65,256]{1,0:T(8,128)(2,1)S(1)} %pad_maximum_fusion.2), channel_id=1, source_target_pairs={{0,8},{4,12},{8,0},{12,4},{1,9},{5,13},{9,1},{13,5},{2,10},{6,14},... | collective-permute-start | bytes 99848 | tf_op jit(solution)/shard_map/ppermute | solution.py:205
  79.3 12.3 %collective-permute-start.12 = (bf16[65,256]{1,0:T(8,128)(2,1)S(1)}, bf16[65,256]{1,0:T(8,128)(2,1)S(1)}, u32[]{:S(2)}, u32[]{:S(2)}) collective-permute-start(bf16[65,256]{1,0:T(8,128)(2,1)S(1)} %pad_maximum_fusion.2), channel_id=1, source_target_pairs={{0,4},{4,8},{8,12},{12,0},{1,5},{5,9},{9,13},{13,1},{2,6},{6,10},{... | collective-permute-start | bytes 99848 | tf_op jit(solution)/shard_map/ppermute | solution.py:205
  91.0 12.0 %collective-permute-start.14 = (f32[65,1024]{1,0:T(8,128)S(1)}, f32[65,1024]{1,0:T(8,128)S(1)}, u32[]{:S(2)}, u32[]{:S(2)}) collective-permute-start(f32[65,1024]{1,0:T(8,128)S(1)} %add.307), channel_id=1, source_target_pairs={{0,2},{2,0},{1,3},{3,1},{4,6},{6,4},{5,7},{7,5},{8,10},{10,8},{9,1... | collective-permute-start | bytes 798728 | tf_op jit(solution)/shard_map/ppermute | solution.py:205
  91.6 11.3 %collective-permute-start.15 = (bf16[65,1024]{1,0:T(8,128)(2,1)S(1)}, bf16[65,1024]{1,0:T(8,128)(2,1)S(1)}, u32[]{:S(2)}, u32[]{:S(2)}) collective-permute-start(bf16[65,1024]{1,0:T(8,128)(2,1)S(1)} %constant_dynamic-update-slice_fusion.refs_0_), channel_id=1, source_target_pairs={{0,2},{2,0},{1,3},{3,1},{4,6},{6,4},{5,7},{7,5},{8,10},{10,8},{9,1... | collective-permute-start | bytes 399368 | tf_op jit(solution)/shard_map/ppermute | solution.py:205
  105.0 7.2 %collective-permute-start.17 = (f32[65,256]{1,0:T(8,128)S(1)}, f32[65,256]{1,0:T(8,128)S(1)}, u32[]{:S(2)}, u32[]{:S(2)}) collective-permute-start(f32[65,256]{1,0:T(8,128)S(1)} %get-tuple-element.130), channel_id=1, source_target_pairs={{0,8},{4,12},{8,0},{12,4},{1,9},{5,13},{9,1},{13,5},{2,10},{6,14},... | collective-permute-start | bytes 199688 | tf_op jit(solution)/shard_map/ppermute | solution.py:205
  106.0 9.5 %collective-permute-start.19 = (bf16[65,2048]{1,0:T(8,128)(2,1)S(1)}, bf16[65,2048]{1,0:T(8,128)(2,1)S(1)}, u32[]{:S(2)}, u32[]{:S(2)}) collective-permute-start(bf16[65,2048]{1,0:T(8,128)(2,1)S(1)} %pad_maximum_fusion), channel_id=1, source_target_pairs={{0,1},{1,0},{2,3},{3,2},{4,5},{5,4},{6,7},{7,6},{8,9},{9,8},{10,11... | collective-permute-start | bytes 798728 | tf_op jit(solution)/shard_map/ppermute | solution.py:205
  129.5 15.3 %collective-permute-start.25 = (bf16[64,2048]{1,0:T(8,128)(2,1)S(1)}, bf16[64,2048]{1,0:T(8,128)(2,1)S(1)}, u32[]{:S(2)}, u32[]{:S(2)}) collective-permute-start(bf16[64,2048]{1,0:T(8,128)(2,1)S(1)} %convert_element_type.77.refs_0_), channel_id=1, source_target_pairs={{0,12},{4,0},{8,4},{12,8},{1,13},{5,1},{9,5},{13,9},{2,14},{6,2},{... | collective-permute-start | bytes 786440 | tf_op jit(solution)/shard_map/ppermute | solution.py:205
  131.0 18.3 %collective-permute-start.27 = (bf16[64,2048]{1,0:T(8,128)(2,1)S(1)}, bf16[64,2048]{1,0:T(8,128)(2,1)S(1)}, u32[]{:S(2)}, u32[]{:S(2)}) collective-permute-start(bf16[64,2048]{1,0:T(8,128)(2,1)S(1)} %convert_element_type.77.refs_0_), channel_id=1, source_target_pairs={{0,4},{4,8},{8,12},{12,0},{1,5},{5,9},{9,13},{13,1},{2,6},{6,10},{... | collective-permute-start | bytes 786440 | tf_op jit(solution)/shard_map/ppermute | solution.py:205
  131.6 23.6 %collective-permute-start.29 = (bf16[64,2048]{1,0:T(8,128)(2,1)S(1)}, bf16[64,2048]{1,0:T(8,128)(2,1)S(1)}, u32[]{:S(2)}, u32[]{:S(2)}) collective-permute-start(bf16[64,2048]{1,0:T(8,128)(2,1)S(1)} %convert_element_type.77.refs_0_), channel_id=1, source_target_pairs={{0,8},{4,12},{8,0},{12,4},{1,9},{5,13},{9,1},{13,5},{2,10},{6,14},... | collective-permute-start | bytes 786440 | tf_op jit(solution)/shard_map/ppermute | solution.py:205
  146.6 10.3 %collective-permute-start.30 = (bf16[64,2048]{1,0:T(8,128)(2,1)S(1)}, bf16[64,2048]{1,0:T(8,128)(2,1)S(1)}, u32[]{:S(2)}, u32[]{:S(2)}) collective-permute-start(bf16[64,2048]{1,0:T(8,128)(2,1)S(1)} %get-tuple-element.111.refs_0_), channel_id=1, source_target_pairs={{0,12},{4,0},{8,4},{12,8},{1,13},{5,1},{9,5},{13,9},{2,14},{6,2},{... | collective-permute-start | bytes 786440 | tf_op jit(solution)/shard_map/ppermute | solution.py:205
  157.0 8.5 %collective-permute-start.33 = (f32[65,64]{1,0:T(8,128)S(1)}, f32[65,64]{1,0:T(8,128)S(1)}, u32[]{:S(2)}, u32[]{:S(2)}) collective-permute-start(f32[65,64]{1,0:T(8,128)S(1)} %add.321), channel_id=1, source_target_pairs={{0,8},{4,12},{8,0},{12,4},{1,9},{5,13},{9,1},{13,5},{2,10},{6,14},... | collective-permute-start | bytes 49928 | tf_op jit(solution)/shard_map/ppermute | solution.py:205
  167.3 12.8 %collective-permute-start.34 = (bf16[64,2048]{1,0:T(8,128)(2,1)S(1)}, bf16[64,2048]{1,0:T(8,128)(2,1)S(1)}, u32[]{:S(2)}, u32[]{:S(2)}) collective-permute-start(bf16[64,2048]{1,0:T(8,128)(2,1)S(1)} %get-tuple-element.111.refs_0_), channel_id=1, source_target_pairs={{0,4},{4,8},{8,12},{12,0},{1,5},{5,9},{9,13},{13,1},{2,6},{6,10},{... | collective-permute-start | bytes 786440 | tf_op jit(solution)/shard_map/ppermute | solution.py:205
  167.6 21.8 %collective-permute-start.38 = (bf16[64,2048]{1,0:T(8,128)(2,1)S(1)}, bf16[64,2048]{1,0:T(8,128)(2,1)S(1)}, u32[]{:S(2)}, u32[]{:S(2)}) collective-permute-start(bf16[64,2048]{1,0:T(8,128)(2,1)S(1)} %get-tuple-element.111.refs_0_), channel_id=1, source_target_pairs={{0,8},{4,12},{8,0},{12,4},{1,9},{5,13},{9,1},{13,5},{2,10},{6,14},... | collective-permute-start | bytes 786440 | tf_op jit(solution)/shard_map/ppermute | solution.py:205
  (17 other events, 201.0 us)

commit v5 on v4

--- a/solution.py
+++ b/solution.py
@@ -81,7 +81,7 @@
     nrow = min(256, count)
     pitch = nrow + 8
     return pl.pallas_call(
-        functools.partial(table_body, unroll=64, pitch=pitch),
+        functools.partial(table_body, unroll=min(128, nrow), pitch=pitch),
         grid_spec=pltpu.PrefetchScalarGridSpec(
             num_scalar_prefetch=1,
             grid=(count // nrow,),

time: 192 us -> 187 us (0.974)
  Pallas kernels: 103 us -> 98.7 us
    pallas_call x8, Pallas kernels: 77.6 us -> 72.9 us  [make_table(): pl.pallas_call(functools.partial(table_body, unroll=min(128, nrow), pitch...]
  transfers between devices with their start and end apart: 39 -> 39, of which waited for: 15 -> 16; matrix products, arithmetic and copies ran while one was open for 3% -> 3% of each run, Pallas kernels for 41% -> 40%
where the time goes in v5:
time: 187 us
  Pallas kernels  98.7 us (53%)
  starting transfers between devices  44.7 us (24%)
  waiting for transfers between devices  34.6 us (19%)
  other arithmetic  3.92 us (2%)
  local copies, waits for them, and re-layouts  2.33 us (1%)
    pallas_call x8, Pallas kernels, make_table(): pl.pallas_call(functools.partial(table_body, unroll=min(128, nrow), pitch...  72.9 us
    ppermute x39, starting transfers between devices, shift(): return lax.ppermute(x, axis, [(i, (i + by) % size) for i in range(size)])  44.7 us
    ppermute x39, waiting for transfers between devices, shift(): return lax.ppermute(x, axis, [(i, (i + by) % size) for i in range(size)])  34.6 us
    pallas_call x7, Pallas kernels, back(): pl.pallas_call(functools.partial(back_body, nblk=nblk, tile=min(512, widt...  12.5 us
    pallas_call x1, Pallas kernels, solve(): pl.pallas_call(solve_body, out_shape=jax.ShapeDtypeStruct(grad.shape, jnp...  9.57 us
  transfers between devices with their start and end apart: 39, of which 16 were waited for; matrix products, arithmetic and copies ran while one was open for 3% of the time, Pallas kernels for 40%

profile of v5, /device:TPU:0, one launch (start us, length us, event | category | flops | bytes accessed | tf_op | source)
XLA Modules:
  0.0 186.7 jit_solution(6607969965609332894)
XLA Ops:
  1.4 3.1 %collective-permute-start.2 = (s32[2,2,2,256]{3,2,1,0:T(2,128)S(1)}, s32[2,2,2,256]{3,2,1,0:T(2,128)S(1)}, u32[]{:S(2)}, u32[]{:S(2)}) collective-permute-start(s32[2,2,2,256]{3,2,1,0:T(2,128)S(1)} %fusion.36), channel_id=1, source_target_pairs={{0,4},{4,8},{8,12},{12,0},{1,5},{5,9},{9,13},{13,1},{2,6},{6,10},{... | collective-permute-start | bytes 24584 | tf_op jit(solution)/shard_map/ppermute | solution.py:205
  4.5 2.6 %collective-permute-start.1 = (s32[2,2,2,256]{3,2,1,0:T(2,128)S(1)}, s32[2,2,2,256]{3,2,1,0:T(2,128)S(1)}, u32[]{:S(2)}, u32[]{:S(2)}) collective-permute-start(s32[2,2,2,256]{3,2,1,0:T(2,128)S(1)} %fusion.36), channel_id=1, source_target_pairs={{0,8},{4,12},{8,0},{12,4},{1,9},{5,13},{9,1},{13,5},{2,10},{6,14},... | collective-permute-start | bytes 24584 | tf_op jit(solution)/shard_map/ppermute | solution.py:205
  12.3 9.1 %make_table.8 = (f8e4m3fn[1024,4096]{1,0:T(32,128)(4,1)S(1)}, f32[65,1024]{1,0:T(8,128)S(1)}) custom-call(s32[1024]{0:T(1024)S(1)} %bitcast.55, f32[552,128]{1,0:T(8,128)S(1)} %fusion.21.tab_ref, f32[32,128]{1,0:T(8,128)S(1)} %fusion.32.a_ref, bf16[128,4096]{1,0:T(8,128)(2,1)S(1)} %fusion.2.feat_ref), custom_call_target="tpu_custom_call" | custom-call | flops 6291456000 | bytes 8388608 | tf_op jit(solution)/shard_map/make_table/pallas_call | solution.py:83
  21.5 9.1 %make_table.9 = (f8e4m3fn[1024,4096]{1,0:T(32,128)(4,1)S(1)}, f32[65,1024]{1,0:T(8,128)S(1)}) custom-call(s32[1024]{0:T(1024)S(1)} %bitcast.54, f32[552,128]{1,0:T(8,128)S(1)} %fusion.21.tab_ref, f32[32,128]{1,0:T(8,128)S(1)} %fusion.32.a_ref, bf16[128,4096]{1,0:T(8,128)(2,1)S(1)} %fusion.2.feat_ref), custom_call_target="tpu_custom_call" | custom-call | flops 6291456000 | bytes 8388608 | tf_op jit(solution)/shard_map/make_table/pallas_call | solution.py:83
  31.2 9.1 %make_table.10 = (f8e4m3fn[1024,4096]{1,0:T(32,128)(4,1)S(1)}, f32[65,1024]{1,0:T(8,128)S(1)}) custom-call(s32[1024]{0:T(1024)S(1)} %bitcast.53, f32[552,128]{1,0:T(8,128)S(1)} %fusion.21.tab_ref, f32[32,128]{1,0:T(8,128)S(1)} %fusion.32.a_ref, bf16[128,4096]{1,0:T(8,128)(2,1)S(1)} %fusion.2.feat_ref), custom_call_target="tpu_custom_call" | custom-call | flops 6291456000 | bytes 8388608 | tf_op jit(solution)/shard_map/make_table/pallas_call | solution.py:83
  42.0 9.1 %make_table.11 = (f8e4m3fn[1024,4096]{1,0:T(32,128)(4,1)S(1)}, f32[65,1024]{1,0:T(8,128)S(1)}) custom-call(s32[1024]{0:T(1024)S(1)} %bitcast.52, f32[552,128]{1,0:T(8,128)S(1)} %fusion.21.tab_ref, f32[32,128]{1,0:T(8,128)S(1)} %fusion.32.a_ref, bf16[128,4096]{1,0:T(8,128)(2,1)S(1)} %fusion.2.feat_ref), custom_call_target="tpu_custom_call" | custom-call | flops 6291456000 | bytes 8388608 | tf_op jit(solution)/shard_map/make_table/pallas_call | solution.py:83
  51.1 9.1 %make_table.12 = (f8e4m3fn[1024,4096]{1,0:T(32,128)(4,1)S(1)}, f32[65,1024]{1,0:T(8,128)S(1)}) custom-call(s32[1024]{0:T(1024)S(1)} %bitcast.51, f32[552,128]{1,0:T(8,128)S(1)} %fusion.21.tab_ref, f32[32,128]{1,0:T(8,128)S(1)} %fusion.32.a_ref, bf16[128,4096]{1,0:T(8,128)(2,1)S(1)} %fusion.2.feat_ref), custom_call_target="tpu_custom_call" | custom-call | flops 6291456000 | bytes 8388608 | tf_op jit(solution)/shard_map/make_table/pallas_call | solution.py:83
  64.3 9.1 %make_table.13 = (f8e4m3fn[1024,4096]{1,0:T(32,128)(4,1)S(1)}, f32[65,1024]{1,0:T(8,128)S(1)}) custom-call(s32[1024]{0:T(1024)S(1)} %bitcast.50, f32[552,128]{1,0:T(8,128)S(1)} %fusion.21.tab_ref, f32[32,128]{1,0:T(8,128)S(1)} %fusion.32.a_ref, bf16[128,4096]{1,0:T(8,128)(2,1)S(1)} %fusion.2.feat_ref), custom_call_target="tpu_custom_call" | custom-call | flops 6291456000 | bytes 8388608 | tf_op jit(solution)/shard_map/make_table/pallas_call | solution.py:83
  75.8 1.9 %collective-permute-start.12 = (bf16[65,256]{1,0:T(8,128)(2,1)S(1)}, bf16[65,256]{1,0:T(8,128)(2,1)S(1)}, u32[]{:S(2)}, u32[]{:S(2)}) collective-permute-start(bf16[65,256]{1,0:T(8,128)(2,1)S(1)} %pad_maximum_fusion.2), channel_id=1, source_target_pairs={{0,4},{4,8},{8,12},{12,0},{1,5},{5,9},{9,13},{13,1},{2,6},{6,10},{... | collective-permute-start | bytes 99848 | tf_op jit(solution)/shard_map/ppermute | solution.py:205
  77.7 9.1 %make_table.14 = (f8e4m3fn[1024,4096]{1,0:T(32,128)(4,1)S(1)}, f32[65,1024]{1,0:T(8,128)S(1)}) custom-call(s32[1024]{0:T(1024)S(1)} %bitcast.49, f32[552,128]{1,0:T(8,128)S(1)} %fusion.21.tab_ref, f32[32,128]{1,0:T(8,128)S(1)} %fusion.32.a_ref, bf16[128,4096]{1,0:T(8,128)(2,1)S(1)} %fusion.2.feat_ref), custom_call_target="tpu_custom_call" | custom-call | flops 6291456000 | bytes 8388608 | tf_op jit(solution)/shard_map/make_table/pallas_call | solution.py:83
  89.1 9.1 %make_table.15 = (f8e4m3fn[1024,4096]{1,0:T(32,128)(4,1)S(1)}, f32[65,1024]{1,0:T(8,128)S(1)}) custom-call(s32[1024]{0:T(1024)S(1)} %bitcast.48, f32[552,128]{1,0:T(8,128)S(1)} %fusion.21.tab_ref, f32[32,128]{1,0:T(8,128)S(1)} %fusion.32.a_ref, bf16[128,4096]{1,0:T(8,128)(2,1)S(1)} %fusion.2.feat_ref), custom_call_target="tpu_custom_call" | custom-call | flops 6291456000 | bytes 8388608 | tf_op jit(solution)/shard_map/make_table/pallas_call | solution.py:83
  98.8 2.2 %collective-permute-start.18 = (f32[65,256]{1,0:T(8,128)S(1)}, f32[65,256]{1,0:T(8,128)S(1)}, u32[]{:S(2)}, u32[]{:S(2)}) collective-permute-start(f32[65,256]{1,0:T(8,128)S(1)} %get-tuple-element.129), channel_id=1, source_target_pairs={{0,12},{4,0},{8,4},{12,8},{1,13},{5,1},{9,5},{13,9},{2,14},{6,2},{... | collective-permute-start | bytes 199688 | tf_op jit(solution)/shard_map/ppermute | solution.py:205
  103.5 4.3 %collective-permute-done.17 = f32[65,256]{1,0:T(8,128)S(1)} collective-permute-done((f32[65,256]{1,0:T(8,128)S(1)}, f32[65,256]{1,0:T(8,128)S(1)}, u32[]{:S(2)}, u32[]{:S(2)}) %collective-permute-start.17) | collective-permute-done | bytes 66592 | tf_op jit(solution)/shard_map/ppermute | solution.py:205
  109.3 1.9 %collective-permute-start.22 = (bf16[65,256]{1,0:T(8,128)(2,1)S(1)}, bf16[65,256]{1,0:T(8,128)(2,1)S(1)}, u32[]{:S(2)}, u32[]{:S(2)}) collective-permute-start(bf16[65,256]{1,0:T(8,128)(2,1)S(1)} %pad_maximum_fusion.3), channel_id=1, source_target_pairs={{0,4},{4,8},{8,12},{12,0},{1,5},{5,9},{9,13},{13,1},{2,6},{6,10},{... | collective-permute-start | bytes 99848 | tf_op jit(solution)/shard_map/ppermute | solution.py:205
  117.2 3.1 %collective-permute-done.23.refs_1_ = bf16[65,1024]{1,0:T(8,128)(2,1)S(1)} collective-permute-done((bf16[65,1024]{1,0:T(8,128)(2,1)S(1)}, bf16[65,1024]{1,0:T(8,128)(2,1)S(1)}, u32[]{:S(2)}, u32[]{:S(2)}) %collective-permute-start.23) | collective-permute-done | bytes 133152 | tf_op jit(solution)/shard_map/ppermute | solution.py:205
  122.0 3.0 %back.10 = f32[65,2048]{1,0:T(8,128)S(1)} custom-call(bf16[65,1024]{1,0:T(8,128)(2,1)S(1)} %constant_dynamic-update-slice_fusion.4.refs_0_, bf16[65,1024]{1,0:T(8,128)(2,1)S(1)} %collective-permute-done.23.refs_1_, bf16[65,1024]{1,0:T(8,128)(2,1)S(1)} %get-tuple-element.104.refs_2_.refs_0_, bf16[65,1024]{1,0:T(8,128)(2,1)S(1)} %get-tuple-element.124.refs_3_.refs_1_, ...), custom_call_target="tpu_custom_call" | custom-call | flops 1090519040 | bytes 8388608 | tf_op jit(solution)/shard_map/back/pallas_call | solution.py:129
  131.6 9.0 %collective-permute-done.25.refs_1_ = bf16[64,2048]{1,0:T(8,128)(2,1)S(1)} collective-permute-done((bf16[64,2048]{1,0:T(8,128)(2,1)S(1)}, bf16[64,2048]{1,0:T(8,128)(2,1)S(1)}, u32[]{:S(2)}, u32[]{:S(2)}) %collective-permute-start.25) | collective-permute-done | bytes 262176 | tf_op jit(solution)/shard_map/ppermute | solution.py:205
  145.6 3.5 %collective-permute-done.28 = f32[65,64]{1,0:T(8,128)S(1)} collective-permute-done((f32[65,64]{1,0:T(8,128)S(1)}, f32[65,64]{1,0:T(8,128)S(1)}, u32[]{:S(2)}, u32[]{:S(2)}) %collective-permute-start.28) | collective-permute-done | bytes 16672 | tf_op jit(solution)/shard_map/ppermute | solution.py:205
  152.7 2.8 %collective-permute-start.33 = (f32[65,64]{1,0:T(8,128)S(1)}, f32[65,64]{1,0:T(8,128)S(1)}, u32[]{:S(2)}, u32[]{:S(2)}) collective-permute-start(f32[65,64]{1,0:T(8,128)S(1)} %add.321), channel_id=1, source_target_pairs={{0,8},{4,12},{8,0},{12,4},{1,9},{5,13},{9,1},{13,5},{2,10},{6,14},... | collective-permute-start | bytes 49928 | tf_op jit(solution)/shard_map/ppermute | solution.py:205
  155.5 3.5 %collective-permute-start.32 = (f32[65,64]{1,0:T(8,128)S(1)}, f32[65,64]{1,0:T(8,128)S(1)}, u32[]{:S(2)}, u32[]{:S(2)}) collective-permute-start(f32[65,64]{1,0:T(8,128)S(1)} %add.321), channel_id=1, source_target_pairs={{0,4},{4,8},{8,12},{12,0},{1,5},{5,9},{9,13},{13,1},{2,6},{6,10},{... | collective-permute-start | bytes 49928 | tf_op jit(solution)/shard_map/ppermute | solution.py:205
  163.1 2.9 %collective-permute-start.38 = (bf16[64,2048]{1,0:T(8,128)(2,1)S(1)}, bf16[64,2048]{1,0:T(8,128)(2,1)S(1)}, u32[]{:S(2)}, u32[]{:S(2)}) collective-permute-start(bf16[64,2048]{1,0:T(8,128)(2,1)S(1)} %get-tuple-element.111.refs_0_), channel_id=1, source_target_pairs={{0,8},{4,12},{8,0},{12,4},{1,9},{5,13},{9,1},{13,5},{2,10},{6,14},... | collective-permute-start | bytes 786440 | tf_op jit(solution)/shard_map/ppermute | solution.py:205
  166.0 9.6 %solve.1 = f32[1,4096]{1,0:T(1,128)S(1)} custom-call(f32[65,64]{1,0:T(8,128)S(1)} %add_add_fusion.4.prod_ref, f32[1,4096]{1,0:T(1,128)S(1)} %pad_maximum_fusion.4.grad_ref, f32[64,2048]{1,0:T(8,128)S(1)} %get-tuple-element.115.refs_0_, f32[64,2048]{1,0:T(8,128)S(1)} %get-tuple-element.113.refs_1_), custom_call_target="tpu_custom_call" | custom-call | tf_op jit(solution)/shard_map/solve/pallas_call | solution.py:168
  176.6 2.0 %collective-permute-start.36 = (f32[1,4096]{1,0:T(1,128)S(1)}, f32[1,4096]{1,0:T(1,128)S(1)}, u32[]{:S(2)}, u32[]{:S(2)}) collective-permute-start(f32[1,4096]{1,0:T(1,128)S(1)} %solve.1), channel_id=1, source_target_pairs={{0,8},{4,12},{8,0},{12,4},{1,9},{5,13},{9,1},{13,5},{2,10},{6,14},... | collective-permute-start | bytes 49160 | tf_op jit(solution)/shard_map/ppermute | solution.py:205
  184.9 1.9 place.3
  (141 shorter events, 55.3 us)
Async XLA Ops:
  1.4 10.7 %collective-permute-start.2 = (s32[2,2,2,256]{3,2,1,0:T(2,128)S(1)}, s32[2,2,2,256]{3,2,1,0:T(2,128)S(1)}, u32[]{:S(2)}, u32[]{:S(2)}) collective-permute-start(s32[2,2,2,256]{3,2,1,0:T(2,128)S(1)} %fusion.36), channel_id=1, source_target_pairs={{0,4},{4,8},{8,12},{12,0},{1,5},{5,9},{9,13},{13,1},{2,6},{6,10},{... | collective-permute-start | bytes 24584 | tf_op jit(solution)/shard_map/ppermute | solution.py:205
  4.5 7.7 %collective-permute-start.1 = (s32[2,2,2,256]{3,2,1,0:T(2,128)S(1)}, s32[2,2,2,256]{3,2,1,0:T(2,128)S(1)}, u32[]{:S(2)}, u32[]{:S(2)}) collective-permute-start(s32[2,2,2,256]{3,2,1,0:T(2,128)S(1)} %fusion.36), channel_id=1, source_target_pairs={{0,8},{4,12},{8,0},{12,4},{1,9},{5,13},{9,1},{13,5},{2,10},{6,14},... | collective-permute-start | bytes 24584 | tf_op jit(solution)/shard_map/ppermute | solution.py:205
  21.5 9.8 %collective-permute-start.3 = (f32[65,1024]{1,0:T(8,128)S(1)}, f32[65,1024]{1,0:T(8,128)S(1)}, u32[]{:S(2)}, u32[]{:S(2)}) collective-permute-start(f32[65,1024]{1,0:T(8,128)S(1)} %get-tuple-element.57), channel_id=1, source_target_pairs={{0,1},{1,0},{2,3},{3,2},{4,5},{5,4},{6,7},{7,6},{8,9},{9,8},{10,11... | collective-permute-start | bytes 798728 | tf_op jit(solution)/shard_map/ppermute | solution.py:205
  30.7 9.7 %collective-permute-start.4 = (f32[65,1024]{1,0:T(8,128)S(1)}, f32[65,1024]{1,0:T(8,128)S(1)}, u32[]{:S(2)}, u32[]{:S(2)}) collective-permute-start(f32[65,1024]{1,0:T(8,128)S(1)} %get-tuple-element.59), channel_id=1, source_target_pairs={{0,1},{1,0},{2,3},{3,2},{4,5},{5,4},{6,7},{7,6},{8,9},{9,8},{10,11... | collective-permute-start | bytes 798728 | tf_op jit(solution)/shard_map/ppermute | solution.py:205
  40.4 10.7 %collective-permute-start.5 = (f32[65,1024]{1,0:T(8,128)S(1)}, f32[65,1024]{1,0:T(8,128)S(1)}, u32[]{:S(2)}, u32[]{:S(2)}) collective-permute-start(f32[65,1024]{1,0:T(8,128)S(1)} %add.297), channel_id=1, source_target_pairs={{0,2},{2,0},{1,3},{3,1},{4,6},{6,4},{5,7},{7,5},{8,10},{10,8},{9,1... | collective-permute-start | bytes 798728 | tf_op jit(solution)/shard_map/ppermute | solution.py:205
  60.2 17.5 %collective-permute-start.9 = (f32[65,1024]{1,0:T(8,128)S(1)}, f32[65,1024]{1,0:T(8,128)S(1)}, u32[]{:S(2)}, u32[]{:S(2)}) collective-permute-start(f32[65,1024]{1,0:T(8,128)S(1)} %get-tuple-element.65), channel_id=1, source_target_pairs={{0,1},{1,0},{2,3},{3,2},{4,5},{5,4},{6,7},{7,6},{8,9},{9,8},{10,11... | collective-permute-start | bytes 798728 | tf_op jit(solution)/shard_map/ppermute | solution.py:205
  60.4 13.1 %collective-permute-start.6 = (f32[65,256]{1,0:T(8,128)S(1)}, f32[65,256]{1,0:T(8,128)S(1)}, u32[]{:S(2)}, u32[]{:S(2)}) collective-permute-start(f32[65,256]{1,0:T(8,128)S(1)} %get-tuple-element.135), channel_id=1, source_target_pairs={{0,4},{4,8},{8,12},{12,0},{1,5},{5,9},{9,13},{13,1},{2,6},{6,10},{... | collective-permute-start | bytes 199688 | tf_op jit(solution)/shard_map/ppermute | solution.py:205
  61.2 12.3 %collective-permute-start.7 = (f32[65,256]{1,0:T(8,128)S(1)}, f32[65,256]{1,0:T(8,128)S(1)}, u32[]{:S(2)}, u32[]{:S(2)}) collective-permute-start(f32[65,256]{1,0:T(8,128)S(1)} %get-tuple-element.134), channel_id=1, source_target_pairs={{0,8},{4,12},{8,0},{12,4},{1,9},{5,13},{9,1},{13,5},{2,10},{6,14},... | collective-permute-start | bytes 199688 | tf_op jit(solution)/shard_map/ppermute | solution.py:205
  62.7 10.7 %collective-permute-start.8 = (f32[65,256]{1,0:T(8,128)S(1)}, f32[65,256]{1,0:T(8,128)S(1)}, u32[]{:S(2)}, u32[]{:S(2)}) collective-permute-start(f32[65,256]{1,0:T(8,128)S(1)} %get-tuple-element.133), channel_id=1, source_target_pairs={{0,12},{4,0},{8,4},{12,8},{1,13},{5,1},{9,5},{13,9},{2,14},{6,2},{... | collective-permute-start | bytes 199688 | tf_op jit(solution)/shard_map/ppermute | solution.py:205
  73.4 14.1 %collective-permute-start.13 = (f32[65,1024]{1,0:T(8,128)S(1)}, f32[65,1024]{1,0:T(8,128)S(1)}, u32[]{:S(2)}, u32[]{:S(2)}) collective-permute-start(f32[65,1024]{1,0:T(8,128)S(1)} %get-tuple-element.67), channel_id=1, source_target_pairs={{0,1},{1,0},{2,3},{3,2},{4,5},{5,4},{6,7},{7,6},{8,9},{9,8},{10,11... | collective-permute-start | bytes 798728 | tf_op jit(solution)/shard_map/ppermute | solution.py:205
  73.6 13.9 %collective-permute-start.10 = (bf16[65,256]{1,0:T(8,128)(2,1)S(1)}, bf16[65,256]{1,0:T(8,128)(2,1)S(1)}, u32[]{:S(2)}, u32[]{:S(2)}) collective-permute-start(bf16[65,256]{1,0:T(8,128)(2,1)S(1)} %pad_maximum_fusion.2), channel_id=1, source_target_pairs={{0,12},{4,0},{8,4},{12,8},{1,13},{5,1},{9,5},{13,9},{2,14},{6,2},{... | collective-permute-start | bytes 99848 | tf_op jit(solution)/shard_map/ppermute | solution.py:205
  74.9 12.6 %collective-permute-start.11 = (bf16[65,256]{1,0:T(8,128)(2,1)S(1)}, bf16[65,256]{1,0:T(8,128)(2,1)S(1)}, u32[]{:S(2)}, u32[]{:S(2)}) collective-permute-start(bf16[65,256]{1,0:T(8,128)(2,1)S(1)} %pad_maximum_fusion.2), channel_id=1, source_target_pairs={{0,8},{4,12},{8,0},{12,4},{1,9},{5,13},{9,1},{13,5},{2,10},{6,14},... | collective-permute-start | bytes 99848 | tf_op jit(solution)/shard_map/ppermute | solution.py:205
  75.8 11.7 %collective-permute-start.12 = (bf16[65,256]{1,0:T(8,128)(2,1)S(1)}, bf16[65,256]{1,0:T(8,128)(2,1)S(1)}, u32[]{:S(2)}, u32[]{:S(2)}) collective-permute-start(bf16[65,256]{1,0:T(8,128)(2,1)S(1)} %pad_maximum_fusion.2), channel_id=1, source_target_pairs={{0,4},{4,8},{8,12},{12,0},{1,5},{5,9},{9,13},{13,1},{2,6},{6,10},{... | collective-permute-start | bytes 99848 | tf_op jit(solution)/shard_map/ppermute | solution.py:205
  86.9 11.8 %collective-permute-start.14 = (f32[65,1024]{1,0:T(8,128)S(1)}, f32[65,1024]{1,0:T(8,128)S(1)}, u32[]{:S(2)}, u32[]{:S(2)}) collective-permute-start(f32[65,1024]{1,0:T(8,128)S(1)} %add.307), channel_id=1, source_target_pairs={{0,2},{2,0},{1,3},{3,1},{4,6},{6,4},{5,7},{7,5},{8,10},{10,8},{9,1... | collective-permute-start | bytes 798728 | tf_op jit(solution)/shard_map/ppermute | solution.py:205
  87.6 11.1 %collective-permute-start.15 = (bf16[65,1024]{1,0:T(8,128)(2,1)S(1)}, bf16[65,1024]{1,0:T(8,128)(2,1)S(1)}, u32[]{:S(2)}, u32[]{:S(2)}) collective-permute-start(bf16[65,1024]{1,0:T(8,128)(2,1)S(1)} %constant_dynamic-update-slice_fusion.refs_0_), channel_id=1, source_target_pairs={{0,2},{2,0},{1,3},{3,1},{4,6},{6,4},{5,7},{7,5},{8,10},{10,8},{9,1... | collective-permute-start | bytes 399368 | tf_op jit(solution)/shard_map/ppermute | solution.py:205
  101.0 6.8 %collective-permute-start.17 = (f32[65,256]{1,0:T(8,128)S(1)}, f32[65,256]{1,0:T(8,128)S(1)}, u32[]{:S(2)}, u32[]{:S(2)}) collective-permute-start(f32[65,256]{1,0:T(8,128)S(1)} %get-tuple-element.130), channel_id=1, source_target_pairs={{0,8},{4,12},{8,0},{12,4},{1,9},{5,13},{9,1},{13,5},{2,10},{6,14},... | collective-permute-start | bytes 199688 | tf_op jit(solution)/shard_map/ppermute | solution.py:205
  101.8 9.5 %collective-permute-start.19 = (bf16[65,2048]{1,0:T(8,128)(2,1)S(1)}, bf16[65,2048]{1,0:T(8,128)(2,1)S(1)}, u32[]{:S(2)}, u32[]{:S(2)}) collective-permute-start(bf16[65,2048]{1,0:T(8,128)(2,1)S(1)} %pad_maximum_fusion), channel_id=1, source_target_pairs={{0,1},{1,0},{2,3},{3,2},{4,5},{5,4},{6,7},{7,6},{8,9},{9,8},{10,11... | collective-permute-start | bytes 798728 | tf_op jit(solution)/shard_map/ppermute | solution.py:205
  125.2 15.4 %collective-permute-start.25 = (bf16[64,2048]{1,0:T(8,128)(2,1)S(1)}, bf16[64,2048]{1,0:T(8,128)(2,1)S(1)}, u32[]{:S(2)}, u32[]{:S(2)}) collective-permute-start(bf16[64,2048]{1,0:T(8,128)(2,1)S(1)} %convert_element_type.77.refs_0_), channel_id=1, source_target_pairs={{0,12},{4,0},{8,4},{12,8},{1,13},{5,1},{9,5},{13,9},{2,14},{6,2},{... | collective-permute-start | bytes 786440 | tf_op jit(solution)/shard_map/ppermute | solution.py:205
  126.6 18.4 %collective-permute-start.27 = (bf16[64,2048]{1,0:T(8,128)(2,1)S(1)}, bf16[64,2048]{1,0:T(8,128)(2,1)S(1)}, u32[]{:S(2)}, u32[]{:S(2)}) collective-permute-start(bf16[64,2048]{1,0:T(8,128)(2,1)S(1)} %convert_element_type.77.refs_0_), channel_id=1, source_target_pairs={{0,4},{4,8},{8,12},{12,0},{1,5},{5,9},{9,13},{13,1},{2,6},{6,10},{... | collective-permute-start | bytes 786440 | tf_op jit(solution)/shard_map/ppermute | solution.py:205
  127.3 23.6 %collective-permute-start.29 = (bf16[64,2048]{1,0:T(8,128)(2,1)S(1)}, bf16[64,2048]{1,0:T(8,128)(2,1)S(1)}, u32[]{:S(2)}, u32[]{:S(2)}) collective-permute-start(bf16[64,2048]{1,0:T(8,128)(2,1)S(1)} %convert_element_type.77.refs_0_), channel_id=1, source_target_pairs={{0,8},{4,12},{8,0},{12,4},{1,9},{5,13},{9,1},{13,5},{2,10},{6,14},... | collective-permute-start | bytes 786440 | tf_op jit(solution)/shard_map/ppermute | solution.py:205
  142.4 10.3 %collective-permute-start.30 = (bf16[64,2048]{1,0:T(8,128)(2,1)S(1)}, bf16[64,2048]{1,0:T(8,128)(2,1)S(1)}, u32[]{:S(2)}, u32[]{:S(2)}) collective-permute-start(bf16[64,2048]{1,0:T(8,128)(2,1)S(1)} %get-tuple-element.111.refs_0_), channel_id=1, source_target_pairs={{0,12},{4,0},{8,4},{12,8},{1,13},{5,1},{9,5},{13,9},{2,14},{6,2},{... | collective-permute-start | bytes 786440 | tf_op jit(solution)/shard_map/ppermute | solution.py:205
  152.7 8.4 %collective-permute-start.33 = (f32[65,64]{1,0:T(8,128)S(1)}, f32[65,64]{1,0:T(8,128)S(1)}, u32[]{:S(2)}, u32[]{:S(2)}) collective-permute-start(f32[65,64]{1,0:T(8,128)S(1)} %add.321), channel_id=1, source_target_pairs={{0,8},{4,12},{8,0},{12,4},{1,9},{5,13},{9,1},{13,5},{2,10},{6,14},... | collective-permute-start | bytes 49928 | tf_op jit(solution)/shard_map/ppermute | solution.py:205
  163.0 12.6 %collective-permute-start.34 = (bf16[64,2048]{1,0:T(8,128)(2,1)S(1)}, bf16[64,2048]{1,0:T(8,128)(2,1)S(1)}, u32[]{:S(2)}, u32[]{:S(2)}) collective-permute-start(bf16[64,2048]{1,0:T(8,128)(2,1)S(1)} %get-tuple-element.111.refs_0_), channel_id=1, source_target_pairs={{0,4},{4,8},{8,12},{12,0},{1,5},{5,9},{9,13},{13,1},{2,6},{6,10},{... | collective-permute-start | bytes 786440 | tf_op jit(solution)/shard_map/ppermute | solution.py:205
  163.1 21.8 %collective-permute-start.38 = (bf16[64,2048]{1,0:T(8,128)(2,1)S(1)}, bf16[64,2048]{1,0:T(8,128)(2,1)S(1)}, u32[]{:S(2)}, u32[]{:S(2)}) collective-permute-start(bf16[64,2048]{1,0:T(8,128)(2,1)S(1)} %get-tuple-element.111.refs_0_), channel_id=1, source_target_pairs={{0,8},{4,12},{8,0},{12,4},{1,9},{5,13},{9,1},{13,5},{2,10},{6,14},... | collective-permute-start | bytes 786440 | tf_op jit(solution)/shard_map/ppermute | solution.py:205
  (17 other events, 197.4 us)

commit v6 on v5

--- a/solution.py
+++ b/solution.py
@@ -427,10 +427,10 @@
         return jnp.moveaxis(parts, 0, 1).reshape(x.shape[0], -1).astype(jnp.float32)
 
     if direct:
+        wide[1][0] = after(wide[1][0], step)
         step = after(step, wide[1][nrows - 1])
     step = spread(step)[0]
     if direct:
-        wide[1][0] = after(wide[1][0], step)
         out = None
         for half in range(nhalf):
             out = place(z, [wide[half][d] for d in range(nrows)], half, nhalf, out)

time: 187 us -> 185 us (0.989)
  waiting for transfers between devices: 34.6 us -> 32.7 us
  transfers between devices with their start and end apart: 39 -> 39, of which waited for: 16 -> 14; matrix products, arithmetic and copies ran while one was open for 3% -> 3% of each run, Pallas kernels for 40% -> 42%
where the time goes in v6:
time: 185 us
  Pallas kernels  98.8 us (53%)
  starting transfers between devices  44.8 us (24%)
  waiting for transfers between devices  32.7 us (18%)
  other arithmetic  3.92 us (2%)
  local copies, waits for them, and re-layouts  2.34 us (1%)
    pallas_call x8, Pallas kernels, make_table(): pl.pallas_call(functools.partial(table_body, unroll=min(128, nrow), pitch...  73 us
    ppermute x39, starting transfers between devices, shift(): return lax.ppermute(x, axis, [(i, (i + by) % size) for i in range(size)])  44.8 us
    ppermute x39, waiting for transfers between devices, shift(): return lax.ppermute(x, axis, [(i, (i + by) % size) for i in range(size)])  32.7 us
    pallas_call x7, Pallas kernels, back(): pl.pallas_call(functools.partial(back_body, nblk=nblk, tile=min(512, widt...  12.5 us
    pallas_call x1, Pallas kernels, solve(): pl.pallas_call(solve_body, out_shape=jax.ShapeDtypeStruct(grad.shape, jnp...  9.57 us
    pallas_call x2, Pallas kernels, place(): pl.pallas_call(functools.partial(place_body, size=size), grid_spec=pltpu....  3.71 us
  transfers between devices with their start and end apart: 39, of which 14 were waited for; matrix products, arithmetic and copies ran while one was open for 3% of the time, Pallas kernels for 42%

profile of v6, /device:TPU:0, one launch (start us, length us, event | category | flops | bytes accessed | tf_op | source)
XLA Modules:
  0.0 185.1 jit_solution(18127191408401680511)
XLA Ops:
  1.4 3.1 %collective-permute-start.2 = (s32[2,2,2,256]{3,2,1,0:T(2,128)S(1)}, s32[2,2,2,256]{3,2,1,0:T(2,128)S(1)}, u32[]{:S(2)}, u32[]{:S(2)}) collective-permute-start(s32[2,2,2,256]{3,2,1,0:T(2,128)S(1)} %fusion.36), channel_id=1, source_target_pairs={{0,4},{4,8},{8,12},{12,0},{1,5},{5,9},{9,13},{13,1},{2,6},{6,10},{... | collective-permute-start | bytes 24584 | tf_op jit(solution)/shard_map/ppermute | solution.py:205
  4.5 2.6 %collective-permute-start.1 = (s32[2,2,2,256]{3,2,1,0:T(2,128)S(1)}, s32[2,2,2,256]{3,2,1,0:T(2,128)S(1)}, u32[]{:S(2)}, u32[]{:S(2)}) collective-permute-start(s32[2,2,2,256]{3,2,1,0:T(2,128)S(1)} %fusion.36), channel_id=1, source_target_pairs={{0,8},{4,12},{8,0},{12,4},{1,9},{5,13},{9,1},{13,5},{2,10},{6,14},... | collective-permute-start | bytes 24584 | tf_op jit(solution)/shard_map/ppermute | solution.py:205
  12.3 9.1 %make_table.8 = (f8e4m3fn[1024,4096]{1,0:T(32,128)(4,1)S(1)}, f32[65,1024]{1,0:T(8,128)S(1)}) custom-call(s32[1024]{0:T(1024)S(1)} %bitcast.55, f32[552,128]{1,0:T(8,128)S(1)} %fusion.21.tab_ref, f32[32,128]{1,0:T(8,128)S(1)} %fusion.32.a_ref, bf16[128,4096]{1,0:T(8,128)(2,1)S(1)} %fusion.2.feat_ref), custom_call_target="tpu_custom_call" | custom-call | flops 6291456000 | bytes 8388608 | tf_op jit(solution)/shard_map/make_table/pallas_call | solution.py:83
  21.6 9.1 %make_table.9 = (f8e4m3fn[1024,4096]{1,0:T(32,128)(4,1)S(1)}, f32[65,1024]{1,0:T(8,128)S(1)}) custom-call(s32[1024]{0:T(1024)S(1)} %bitcast.54, f32[552,128]{1,0:T(8,128)S(1)} %fusion.21.tab_ref, f32[32,128]{1,0:T(8,128)S(1)} %fusion.32.a_ref, bf16[128,4096]{1,0:T(8,128)(2,1)S(1)} %fusion.2.feat_ref), custom_call_target="tpu_custom_call" | custom-call | flops 6291456000 | bytes 8388608 | tf_op jit(solution)/shard_map/make_table/pallas_call | solution.py:83
  31.2 9.1 %make_table.10 = (f8e4m3fn[1024,4096]{1,0:T(32,128)(4,1)S(1)}, f32[65,1024]{1,0:T(8,128)S(1)}) custom-call(s32[1024]{0:T(1024)S(1)} %bitcast.53, f32[552,128]{1,0:T(8,128)S(1)} %fusion.21.tab_ref, f32[32,128]{1,0:T(8,128)S(1)} %fusion.32.a_ref, bf16[128,4096]{1,0:T(8,128)(2,1)S(1)} %fusion.2.feat_ref), custom_call_target="tpu_custom_call" | custom-call | flops 6291456000 | bytes 8388608 | tf_op jit(solution)/shard_map/make_table/pallas_call | solution.py:83
  42.0 9.1 %make_table.11 = (f8e4m3fn[1024,4096]{1,0:T(32,128)(4,1)S(1)}, f32[65,1024]{1,0:T(8,128)S(1)}) custom-call(s32[1024]{0:T(1024)S(1)} %bitcast.52, f32[552,128]{1,0:T(8,128)S(1)} %fusion.21.tab_ref, f32[32,128]{1,0:T(8,128)S(1)} %fusion.32.a_ref, bf16[128,4096]{1,0:T(8,128)(2,1)S(1)} %fusion.2.feat_ref), custom_call_target="tpu_custom_call" | custom-call | flops 6291456000 | bytes 8388608 | tf_op jit(solution)/shard_map/make_table/pallas_call | solution.py:83
  51.1 9.1 %make_table.12 = (f8e4m3fn[1024,4096]{1,0:T(32,128)(4,1)S(1)}, f32[65,1024]{1,0:T(8,128)S(1)}) custom-call(s32[1024]{0:T(1024)S(1)} %bitcast.51, f32[552,128]{1,0:T(8,128)S(1)} %fusion.21.tab_ref, f32[32,128]{1,0:T(8,128)S(1)} %fusion.32.a_ref, bf16[128,4096]{1,0:T(8,128)(2,1)S(1)} %fusion.2.feat_ref), custom_call_target="tpu_custom_call" | custom-call | flops 6291456000 | bytes 8388608 | tf_op jit(solution)/shard_map/make_table/pallas_call | solution.py:83
  64.3 9.1 %make_table.13 = (f8e4m3fn[1024,4096]{1,0:T(32,128)(4,1)S(1)}, f32[65,1024]{1,0:T(8,128)S(1)}) custom-call(s32[1024]{0:T(1024)S(1)} %bitcast.50, f32[552,128]{1,0:T(8,128)S(1)} %fusion.21.tab_ref, f32[32,128]{1,0:T(8,128)S(1)} %fusion.32.a_ref, bf16[128,4096]{1,0:T(8,128)(2,1)S(1)} %fusion.2.feat_ref), custom_call_target="tpu_custom_call" | custom-call | flops 6291456000 | bytes 8388608 | tf_op jit(solution)/shard_map/make_table/pallas_call | solution.py:83
  75.8 1.9 %collective-permute-start.12 = (bf16[65,256]{1,0:T(8,128)(2,1)S(1)}, bf16[65,256]{1,0:T(8,128)(2,1)S(1)}, u32[]{:S(2)}, u32[]{:S(2)}) collective-permute-start(bf16[65,256]{1,0:T(8,128)(2,1)S(1)} %pad_maximum_fusion.2), channel_id=1, source_target_pairs={{0,4},{4,8},{8,12},{12,0},{1,5},{5,9},{9,13},{13,1},{2,6},{6,10},{... | collective-permute-start | bytes 99848 | tf_op jit(solution)/shard_map/ppermute | solution.py:205
  77.8 9.1 %make_table.14 = (f8e4m3fn[1024,4096]{1,0:T(32,128)(4,1)S(1)}, f32[65,1024]{1,0:T(8,128)S(1)}) custom-call(s32[1024]{0:T(1024)S(1)} %bitcast.49, f32[552,128]{1,0:T(8,128)S(1)} %fusion.21.tab_ref, f32[32,128]{1,0:T(8,128)S(1)} %fusion.32.a_ref, bf16[128,4096]{1,0:T(8,128)(2,1)S(1)} %fusion.2.feat_ref), custom_call_target="tpu_custom_call" | custom-call | flops 6291456000 | bytes 8388608 | tf_op jit(solution)/shard_map/make_table/pallas_call | solution.py:83
  89.2 9.1 %make_table.15 = (f8e4m3fn[1024,4096]{1,0:T(32,128)(4,1)S(1)}, f32[65,1024]{1,0:T(8,128)S(1)}) custom-call(s32[1024]{0:T(1024)S(1)} %bitcast.48, f32[552,128]{1,0:T(8,128)S(1)} %fusion.21.tab_ref, f32[32,128]{1,0:T(8,128)S(1)} %fusion.32.a_ref, bf16[128,4096]{1,0:T(8,128)(2,1)S(1)} %fusion.2.feat_ref), custom_call_target="tpu_custom_call" | custom-call | flops 6291456000 | bytes 8388608 | tf_op jit(solution)/shard_map/make_table/pallas_call | solution.py:83
  98.8 2.2 %collective-permute-start.18 = (f32[65,256]{1,0:T(8,128)S(1)}, f32[65,256]{1,0:T(8,128)S(1)}, u32[]{:S(2)}, u32[]{:S(2)}) collective-permute-start(f32[65,256]{1,0:T(8,128)S(1)} %get-tuple-element.129), channel_id=1, source_target_pairs={{0,12},{4,0},{8,4},{12,8},{1,13},{5,1},{9,5},{13,9},{2,14},{6,2},{... | collective-permute-start | bytes 199688 | tf_op jit(solution)/shard_map/ppermute | solution.py:205
  103.5 4.3 %collective-permute-done.17 = f32[65,256]{1,0:T(8,128)S(1)} collective-permute-done((f32[65,256]{1,0:T(8,128)S(1)}, f32[65,256]{1,0:T(8,128)S(1)}, u32[]{:S(2)}, u32[]{:S(2)}) %collective-permute-start.17) | collective-permute-done | bytes 66592 | tf_op jit(solution)/shard_map/ppermute | solution.py:205
  109.3 1.9 %collective-permute-start.22 = (bf16[65,256]{1,0:T(8,128)(2,1)S(1)}, bf16[65,256]{1,0:T(8,128)(2,1)S(1)}, u32[]{:S(2)}, u32[]{:S(2)}) collective-permute-start(bf16[65,256]{1,0:T(8,128)(2,1)S(1)} %pad_maximum_fusion.3), channel_id=1, source_target_pairs={{0,4},{4,8},{8,12},{12,0},{1,5},{5,9},{9,13},{13,1},{2,6},{6,10},{... | collective-permute-start | bytes 99848 | tf_op jit(solution)/shard_map/ppermute | solution.py:205
  117.3 3.0 %collective-permute-done.23.refs_1_ = bf16[65,1024]{1,0:T(8,128)(2,1)S(1)} collective-permute-done((bf16[65,1024]{1,0:T(8,128)(2,1)S(1)}, bf16[65,1024]{1,0:T(8,128)(2,1)S(1)}, u32[]{:S(2)}, u32[]{:S(2)}) %collective-permute-start.23) | collective-permute-done | bytes 133152 | tf_op jit(solution)/shard_map/ppermute | solution.py:205
  122.0 3.0 %back.10 = f32[65,2048]{1,0:T(8,128)S(1)} custom-call(bf16[65,1024]{1,0:T(8,128)(2,1)S(1)} %constant_dynamic-update-slice_fusion.4.refs_0_, bf16[65,1024]{1,0:T(8,128)(2,1)S(1)} %collective-permute-done.23.refs_1_, bf16[65,1024]{1,0:T(8,128)(2,1)S(1)} %get-tuple-element.104.refs_2_.refs_0_, bf16[65,1024]{1,0:T(8,128)(2,1)S(1)} %get-tuple-element.124.refs_3_.refs_1_, ...), custom_call_target="tpu_custom_call" | custom-call | flops 1090519040 | bytes 8388608 | tf_op jit(solution)/shard_map/back/pallas_call | solution.py:129
  131.6 9.0 %collective-permute-done.25.refs_1_ = bf16[64,2048]{1,0:T(8,128)(2,1)S(1)} collective-permute-done((bf16[64,2048]{1,0:T(8,128)(2,1)S(1)}, bf16[64,2048]{1,0:T(8,128)(2,1)S(1)}, u32[]{:S(2)}, u32[]{:S(2)}) %collective-permute-start.25) | collective-permute-done | bytes 262176 | tf_op jit(solution)/shard_map/ppermute | solution.py:205
  145.6 3.4 %collective-permute-done.28 = f32[65,64]{1,0:T(8,128)S(1)} collective-permute-done((f32[65,64]{1,0:T(8,128)S(1)}, f32[65,64]{1,0:T(8,128)S(1)}, u32[]{:S(2)}, u32[]{:S(2)}) %collective-permute-start.28) | collective-permute-done | bytes 16672 | tf_op jit(solution)/shard_map/ppermute | solution.py:205
  152.7 2.8 %collective-permute-start.33 = (f32[65,64]{1,0:T(8,128)S(1)}, f32[65,64]{1,0:T(8,128)S(1)}, u32[]{:S(2)}, u32[]{:S(2)}) collective-permute-start(f32[65,64]{1,0:T(8,128)S(1)} %add.321), channel_id=1, source_target_pairs={{0,8},{4,12},{8,0},{12,4},{1,9},{5,13},{9,1},{13,5},{2,10},{6,14},... | collective-permute-start | bytes 49928 | tf_op jit(solution)/shard_map/ppermute | solution.py:205
  155.5 3.5 %collective-permute-start.32 = (f32[65,64]{1,0:T(8,128)S(1)}, f32[65,64]{1,0:T(8,128)S(1)}, u32[]{:S(2)}, u32[]{:S(2)}) collective-permute-start(f32[65,64]{1,0:T(8,128)S(1)} %add.321), channel_id=1, source_target_pairs={{0,4},{4,8},{8,12},{12,0},{1,5},{5,9},{9,13},{13,1},{2,6},{6,10},{... | collective-permute-start | bytes 49928 | tf_op jit(solution)/shard_map/ppermute | solution.py:205
  163.1 2.9 %collective-permute-start.38 = (bf16[64,2048]{1,0:T(8,128)(2,1)S(1)}, bf16[64,2048]{1,0:T(8,128)(2,1)S(1)}, u32[]{:S(2)}, u32[]{:S(2)}) collective-permute-start(bf16[64,2048]{1,0:T(8,128)(2,1)S(1)} %get-tuple-element.111.refs_0_), channel_id=1, source_target_pairs={{0,8},{4,12},{8,0},{12,4},{1,9},{5,13},{9,1},{13,5},{2,10},{6,14},... | collective-permute-start | bytes 786440 | tf_op jit(solution)/shard_map/ppermute | solution.py:205
  166.0 9.6 %solve.1 = f32[1,4096]{1,0:T(1,128)S(1)} custom-call(f32[65,64]{1,0:T(8,128)S(1)} %add_add_fusion.4.prod_ref, f32[1,4096]{1,0:T(1,128)S(1)} %pad_maximum_fusion.4.grad_ref, f32[64,2048]{1,0:T(8,128)S(1)} %get-tuple-element.115.refs_0_, f32[64,2048]{1,0:T(8,128)S(1)} %get-tuple-element.113.refs_1_), custom_call_target="tpu_custom_call" | custom-call | tf_op jit(solution)/shard_map/solve/pallas_call | solution.py:168
  176.6 2.0 %collective-permute-start.36 = (f32[1,4096]{1,0:T(1,128)S(1)}, f32[1,4096]{1,0:T(1,128)S(1)}, u32[]{:S(2)}, u32[]{:S(2)}) collective-permute-start(f32[1,4096]{1,0:T(1,128)S(1)} %solve.1), channel_id=1, source_target_pairs={{0,8},{4,12},{8,0},{12,4},{1,9},{5,13},{9,1},{13,5},{2,10},{6,14},... | collective-permute-start | bytes 49160 | tf_op jit(solution)/shard_map/ppermute | solution.py:205
  180.4 2.1 %collective-permute-done.38.refs_2_ = bf16[64,2048]{1,0:T(8,128)(2,1)S(1)} collective-permute-done((bf16[64,2048]{1,0:T(8,128)(2,1)S(1)}, bf16[64,2048]{1,0:T(8,128)(2,1)S(1)}, u32[]{:S(2)}, u32[]{:S(2)}) %collective-permute-start.38) | collective-permute-done | bytes 262176 | tf_op jit(solution)/shard_map/ppermute | solution.py:205
  (141 shorter events, 53.5 us)
Async XLA Ops:
  1.4 10.7 %collective-permute-start.2 = (s32[2,2,2,256]{3,2,1,0:T(2,128)S(1)}, s32[2,2,2,256]{3,2,1,0:T(2,128)S(1)}, u32[]{:S(2)}, u32[]{:S(2)}) collective-permute-start(s32[2,2,2,256]{3,2,1,0:T(2,128)S(1)} %fusion.36), channel_id=1, source_target_pairs={{0,4},{4,8},{8,12},{12,0},{1,5},{5,9},{9,13},{13,1},{2,6},{6,10},{... | collective-permute-start | bytes 24584 | tf_op jit(solution)/shard_map/ppermute | solution.py:205
  21.5 9.8 %collective-permute-start.3 = (f32[65,1024]{1,0:T(8,128)S(1)}, f32[65,1024]{1,0:T(8,128)S(1)}, u32[]{:S(2)}, u32[]{:S(2)}) collective-permute-start(f32[65,1024]{1,0:T(8,128)S(1)} %get-tuple-element.57), channel_id=1, source_target_pairs={{0,1},{1,0},{2,3},{3,2},{4,5},{5,4},{6,7},{7,6},{8,9},{9,8},{10,11... | collective-permute-start | bytes 798728 | tf_op jit(solution)/shard_map/ppermute | solution.py:205
  30.7 9.7 %collective-permute-start.4 = (f32[65,1024]{1,0:T(8,128)S(1)}, f32[65,1024]{1,0:T(8,128)S(1)}, u32[]{:S(2)}, u32[]{:S(2)}) collective-permute-start(f32[65,1024]{1,0:T(8,128)S(1)} %get-tuple-element.59), channel_id=1, source_target_pairs={{0,1},{1,0},{2,3},{3,2},{4,5},{5,4},{6,7},{7,6},{8,9},{9,8},{10,11... | collective-permute-start | bytes 798728 | tf_op jit(solution)/shard_map/ppermute | solution.py:205
  40.4 10.7 %collective-permute-start.5 = (f32[65,1024]{1,0:T(8,128)S(1)}, f32[65,1024]{1,0:T(8,128)S(1)}, u32[]{:S(2)}, u32[]{:S(2)}) collective-permute-start(f32[65,1024]{1,0:T(8,128)S(1)} %add.297), channel_id=1, source_target_pairs={{0,2},{2,0},{1,3},{3,1},{4,6},{6,4},{5,7},{7,5},{8,10},{10,8},{9,1... | collective-permute-start | bytes 798728 | tf_op jit(solution)/shard_map/ppermute | solution.py:205
  60.3 17.5 %collective-permute-start.9 = (f32[65,1024]{1,0:T(8,128)S(1)}, f32[65,1024]{1,0:T(8,128)S(1)}, u32[]{:S(2)}, u32[]{:S(2)}) collective-permute-start(f32[65,1024]{1,0:T(8,128)S(1)} %get-tuple-element.65), channel_id=1, source_target_pairs={{0,1},{1,0},{2,3},{3,2},{4,5},{5,4},{6,7},{7,6},{8,9},{9,8},{10,11... | collective-permute-start | bytes 798728 | tf_op jit(solution)/shard_map/ppermute | solution.py:205
  60.4 13.1 %collective-permute-start.6 = (f32[65,256]{1,0:T(8,128)S(1)}, f32[65,256]{1,0:T(8,128)S(1)}, u32[]{:S(2)}, u32[]{:S(2)}) collective-permute-start(f32[65,256]{1,0:T(8,128)S(1)} %get-tuple-element.135), channel_id=1, source_target_pairs={{0,4},{4,8},{8,12},{12,0},{1,5},{5,9},{9,13},{13,1},{2,6},{6,10},{... | collective-permute-start | bytes 199688 | tf_op jit(solution)/shard_map/ppermute | solution.py:205
  61.2 12.4 %collective-permute-start.7 = (f32[65,256]{1,0:T(8,128)S(1)}, f32[65,256]{1,0:T(8,128)S(1)}, u32[]{:S(2)}, u32[]{:S(2)}) collective-permute-start(f32[65,256]{1,0:T(8,128)S(1)} %get-tuple-element.134), channel_id=1, source_target_pairs={{0,8},{4,12},{8,0},{12,4},{1,9},{5,13},{9,1},{13,5},{2,10},{6,14},... | collective-permute-start | bytes 199688 | tf_op jit(solution)/shard_map/ppermute | solution.py:205
  62.8 10.8 %collective-permute-start.8 = (f32[65,256]{1,0:T(8,128)S(1)}, f32[65,256]{1,0:T(8,128)S(1)}, u32[]{:S(2)}, u32[]{:S(2)}) collective-permute-start(f32[65,256]{1,0:T(8,128)S(1)} %get-tuple-element.133), channel_id=1, source_target_pairs={{0,12},{4,0},{8,4},{12,8},{1,13},{5,1},{9,5},{13,9},{2,14},{6,2},{... | collective-permute-start | bytes 199688 | tf_op jit(solution)/shard_map/ppermute | solution.py:205
  73.4 14.1 %collective-permute-start.13 = (f32[65,1024]{1,0:T(8,128)S(1)}, f32[65,1024]{1,0:T(8,128)S(1)}, u32[]{:S(2)}, u32[]{:S(2)}) collective-permute-start(f32[65,1024]{1,0:T(8,128)S(1)} %get-tuple-element.67), channel_id=1, source_target_pairs={{0,1},{1,0},{2,3},{3,2},{4,5},{5,4},{6,7},{7,6},{8,9},{9,8},{10,11... | collective-permute-start | bytes 798728 | tf_op jit(solution)/shard_map/ppermute | solution.py:205
  73.6 13.9 %collective-permute-start.10 = (bf16[65,256]{1,0:T(8,128)(2,1)S(1)}, bf16[65,256]{1,0:T(8,128)(2,1)S(1)}, u32[]{:S(2)}, u32[]{:S(2)}) collective-permute-start(bf16[65,256]{1,0:T(8,128)(2,1)S(1)} %pad_maximum_fusion.2), channel_id=1, source_target_pairs={{0,12},{4,0},{8,4},{12,8},{1,13},{5,1},{9,5},{13,9},{2,14},{6,2},{... | collective-permute-start | bytes 99848 | tf_op jit(solution)/shard_map/ppermute | solution.py:205
  74.9 12.6 %collective-permute-start.11 = (bf16[65,256]{1,0:T(8,128)(2,1)S(1)}, bf16[65,256]{1,0:T(8,128)(2,1)S(1)}, u32[]{:S(2)}, u32[]{:S(2)}) collective-permute-start(bf16[65,256]{1,0:T(8,128)(2,1)S(1)} %pad_maximum_fusion.2), channel_id=1, source_target_pairs={{0,8},{4,12},{8,0},{12,4},{1,9},{5,13},{9,1},{13,5},{2,10},{6,14},... | collective-permute-start | bytes 99848 | tf_op jit(solution)/shard_map/ppermute | solution.py:205
  75.8 11.8 %collective-permute-start.12 = (bf16[65,256]{1,0:T(8,128)(2,1)S(1)}, bf16[65,256]{1,0:T(8,128)(2,1)S(1)}, u32[]{:S(2)}, u32[]{:S(2)}) collective-permute-start(bf16[65,256]{1,0:T(8,128)(2,1)S(1)} %pad_maximum_fusion.2), channel_id=1, source_target_pairs={{0,4},{4,8},{8,12},{12,0},{1,5},{5,9},{9,13},{13,1},{2,6},{6,10},{... | collective-permute-start | bytes 99848 | tf_op jit(solution)/shard_map/ppermute | solution.py:205
  86.9 11.8 %collective-permute-start.14 = (f32[65,1024]{1,0:T(8,128)S(1)}, f32[65,1024]{1,0:T(8,128)S(1)}, u32[]{:S(2)}, u32[]{:S(2)}) collective-permute-start(f32[65,1024]{1,0:T(8,128)S(1)} %add.307), channel_id=1, source_target_pairs={{0,2},{2,0},{1,3},{3,1},{4,6},{6,4},{5,7},{7,5},{8,10},{10,8},{9,1... | collective-permute-start | bytes 798728 | tf_op jit(solution)/shard_map/ppermute | solution.py:205
  87.6 11.1 %collective-permute-start.15 = (bf16[65,1024]{1,0:T(8,128)(2,1)S(1)}, bf16[65,1024]{1,0:T(8,128)(2,1)S(1)}, u32[]{:S(2)}, u32[]{:S(2)}) collective-permute-start(bf16[65,1024]{1,0:T(8,128)(2,1)S(1)} %constant_dynamic-update-slice_fusion.refs_0_), channel_id=1, source_target_pairs={{0,2},{2,0},{1,3},{3,1},{4,6},{6,4},{5,7},{7,5},{8,10},{10,8},{9,1... | collective-permute-start | bytes 399368 | tf_op jit(solution)/shard_map/ppermute | solution.py:205
  101.8 9.5 %collective-permute-start.19 = (bf16[65,2048]{1,0:T(8,128)(2,1)S(1)}, bf16[65,2048]{1,0:T(8,128)(2,1)S(1)}, u32[]{:S(2)}, u32[]{:S(2)}) collective-permute-start(bf16[65,2048]{1,0:T(8,128)(2,1)S(1)} %pad_maximum_fusion), channel_id=1, source_target_pairs={{0,1},{1,0},{2,3},{3,2},{4,5},{5,4},{6,7},{7,6},{8,9},{9,8},{10,11... | collective-permute-start | bytes 798728 | tf_op jit(solution)/shard_map/ppermute | solution.py:205
  125.2 15.3 %collective-permute-start.25 = (bf16[64,2048]{1,0:T(8,128)(2,1)S(1)}, bf16[64,2048]{1,0:T(8,128)(2,1)S(1)}, u32[]{:S(2)}, u32[]{:S(2)}) collective-permute-start(bf16[64,2048]{1,0:T(8,128)(2,1)S(1)} %convert_element_type.77.refs_0_), channel_id=1, source_target_pairs={{0,12},{4,0},{8,4},{12,8},{1,13},{5,1},{9,5},{13,9},{2,14},{6,2},{... | collective-permute-start | bytes 786440 | tf_op jit(solution)/shard_map/ppermute | solution.py:205
  126.6 18.4 %collective-permute-start.27 = (bf16[64,2048]{1,0:T(8,128)(2,1)S(1)}, bf16[64,2048]{1,0:T(8,128)(2,1)S(1)}, u32[]{:S(2)}, u32[]{:S(2)}) collective-permute-start(bf16[64,2048]{1,0:T(8,128)(2,1)S(1)} %convert_element_type.77.refs_0_), channel_id=1, source_target_pairs={{0,4},{4,8},{8,12},{12,0},{1,5},{5,9},{9,13},{13,1},{2,6},{6,10},{... | collective-permute-start | bytes 786440 | tf_op jit(solution)/shard_map/ppermute | solution.py:205
  127.3 23.6 %collective-permute-start.29 = (bf16[64,2048]{1,0:T(8,128)(2,1)S(1)}, bf16[64,2048]{1,0:T(8,128)(2,1)S(1)}, u32[]{:S(2)}, u32[]{:S(2)}) collective-permute-start(bf16[64,2048]{1,0:T(8,128)(2,1)S(1)} %convert_element_type.77.refs_0_), channel_id=1, source_target_pairs={{0,8},{4,12},{8,0},{12,4},{1,9},{5,13},{9,1},{13,5},{2,10},{6,14},... | collective-permute-start | bytes 786440 | tf_op jit(solution)/shard_map/ppermute | solution.py:205
  142.4 10.3 %collective-permute-start.30 = (bf16[64,2048]{1,0:T(8,128)(2,1)S(1)}, bf16[64,2048]{1,0:T(8,128)(2,1)S(1)}, u32[]{:S(2)}, u32[]{:S(2)}) collective-permute-start(bf16[64,2048]{1,0:T(8,128)(2,1)S(1)} %get-tuple-element.111.refs_0_), channel_id=1, source_target_pairs={{0,12},{4,0},{8,4},{12,8},{1,13},{5,1},{9,5},{13,9},{2,14},{6,2},{... | collective-permute-start | bytes 786440 | tf_op jit(solution)/shard_map/ppermute | solution.py:205
  152.7 8.4 %collective-permute-start.33 = (f32[65,64]{1,0:T(8,128)S(1)}, f32[65,64]{1,0:T(8,128)S(1)}, u32[]{:S(2)}, u32[]{:S(2)}) collective-permute-start(f32[65,64]{1,0:T(8,128)S(1)} %add.321), channel_id=1, source_target_pairs={{0,8},{4,12},{8,0},{12,4},{1,9},{5,13},{9,1},{13,5},{2,10},{6,14},... | collective-permute-start | bytes 49928 | tf_op jit(solution)/shard_map/ppermute | solution.py:205
  163.0 12.6 %collective-permute-start.34 = (bf16[64,2048]{1,0:T(8,128)(2,1)S(1)}, bf16[64,2048]{1,0:T(8,128)(2,1)S(1)}, u32[]{:S(2)}, u32[]{:S(2)}) collective-permute-start(bf16[64,2048]{1,0:T(8,128)(2,1)S(1)} %get-tuple-element.111.refs_0_), channel_id=1, source_target_pairs={{0,4},{4,8},{8,12},{12,0},{1,5},{5,9},{9,13},{13,1},{2,6},{6,10},{... | collective-permute-start | bytes 786440 | tf_op jit(solution)/shard_map/ppermute | solution.py:205
  163.1 19.4 %collective-permute-start.38 = (bf16[64,2048]{1,0:T(8,128)(2,1)S(1)}, bf16[64,2048]{1,0:T(8,128)(2,1)S(1)}, u32[]{:S(2)}, u32[]{:S(2)}) collective-permute-start(bf16[64,2048]{1,0:T(8,128)(2,1)S(1)} %get-tuple-element.111.refs_0_), channel_id=1, source_target_pairs={{0,8},{4,12},{8,0},{12,4},{1,9},{5,13},{9,1},{13,5},{2,10},{6,14},... | collective-permute-start | bytes 786440 | tf_op jit(solution)/shard_map/ppermute | solution.py:205
  175.6 8.8 %collective-permute-start.35 = (f32[1,4096]{1,0:T(1,128)S(1)}, f32[1,4096]{1,0:T(1,128)S(1)}, u32[]{:S(2)}, u32[]{:S(2)}) collective-permute-start(f32[1,4096]{1,0:T(1,128)S(1)} %solve.1), channel_id=1, source_target_pairs={{0,12},{4,0},{8,4},{12,8},{1,13},{5,1},{9,5},{13,9},{2,14},{6,2},{... | collective-permute-start | bytes 49160 | tf_op jit(solution)/shard_map/ppermute | solution.py:205
  176.6 7.7 %collective-permute-start.36 = (f32[1,4096]{1,0:T(1,128)S(1)}, f32[1,4096]{1,0:T(1,128)S(1)}, u32[]{:S(2)}, u32[]{:S(2)}) collective-permute-start(f32[1,4096]{1,0:T(1,128)S(1)} %solve.1), channel_id=1, source_target_pairs={{0,8},{4,12},{8,0},{12,4},{1,9},{5,13},{9,1},{13,5},{2,10},{6,14},... | collective-permute-start | bytes 49160 | tf_op jit(solution)/shard_map/ppermute | solution.py:205
  (17 other events, 199.9 us)
